TPU v7x, 32 devices: a whole 2x2x4 slice. The times are simulated.
32 devices in a mesh: ty: 4 (over y, x), tx: 8 (over z, core).
Axes of the slice: x: 2, y: 2, z: 4, core: 2. Of those that a mesh axis runs over, the one named last changes fastest.
Arguments:
- transmission: float32 [2, 2, 256, 512], P(None, None, 'ty', 'tx'), may hold values from -4 to 4
- probe_field: float32 [2, 128, 128], replicated, may hold values from -4 to 4
- propagator_phase: float32 [128, 128], replicated, may hold values from -3.140625 to 3.140625
- scan_offsets: int32 [4, 8, 6, 2], P('ty', 'tx'), may hold values from 0 to 64, as said below
- position_counts: int32 [4, 8], P('ty', 'tx'), may hold values from 1 to 6, as said below
- intensities: float32 [4, 8, 6, 128, 128], P('ty', 'tx'), may hold values from 0 to 2
Outputs:
- updated_object: float32 [2, 2, 256, 512], P(None, None, 'ty', 'tx')
Inputs may be any that keep to these rules, and one draw needn't show every extreme that they name: `scan_offsets`: each pair is a row and a column offset within the extended region of 192 pixels; offsets 0 and 64 both occur. `position_counts`: positions k of a tile with k >= its count are ignored; some tile has 6 and some tile has 1.
All inputs are finite; a program needn't handle non-finite values.
Results may differ from a plain program's by a relative error of at most 0.0003.
Values sent between devices are 32-bit elements; how exact they have to be, the bound alone decides.
No kernel may reach another device: no remote copies, remote signals or barrier semaphores. Data moves between devices by JAX's collectives and lax.ppermute only.
A program may use at most 64 MiB of HBM per device.

v0:
```python
import math

import jax
import jax.numpy as jnp
import numpy as np
from jax import lax
from jax.experimental import pallas as pl
from jax.experimental.pallas import tpu as pltpu
from jax.sharding import PartitionSpec as P

ITERS = 2
STEP = 0.003
GROUP = 2


def dft_blocks(length):
    index = np.arange(length)
    angle = 2.0 * math.pi / length * (index[:, None] * index[None, :] % length)
    re, im = np.cos(angle) / math.sqrt(length), -np.sin(angle) / math.sqrt(length)
    full = np.block([[re, -im], [im, re]])
    high = full.astype(jnp.bfloat16)
    low = (full - high.astype(np.float64)).astype(jnp.bfloat16)
    return np.stack([high, low, high.T, low.T])


def halves(x):
    high = x.astype(jnp.bfloat16)
    return high, (x - high.astype(jnp.float32)).astype(jnp.bfloat16)


def mm(a, b):
    return jnp.dot(a, b, preferred_element_type=jnp.float32)


def gradient_kernel(
    offsets, count, place, far_ref, mid_ref, near_ref, probe_ref, prop_ref, data_ref, table_ref,
    gfar_ref, gmid_ref, gnear_ref, ext, acc,
):
    layers, rows, lanes = mid_ref.shape
    length = probe_ref.shape[1]
    core = lanes // 2
    lane = lax.broadcasted_iota(jnp.int32, (rows, lanes), 1)
    low_half = lane < core
    is_first, has_far = place[0] == 1, place[1] == 1
    for s in range(layers):
        outer = jnp.where(has_far, far_ref[s], 0.0)
        left = jnp.where(is_first, outer, near_ref[s])
        right = jnp.where(is_first, near_ref[s], outer)
        mid = mid_ref[s]
        ext[s, 0, 0] = jnp.where(low_half, left, pltpu.roll(mid, core, 1))
        ext[s, 1, 0] = jnp.where(low_half, pltpu.roll(left, core, 1), mid)
        ext[s, 0, 1] = right
        ext[s, 1, 1] = pltpu.roll(right, core, 1)
    acc[...] = jnp.zeros_like(acc)

    def right_mul(blocks, table):
        x = jnp.concatenate([jnp.concatenate([r, i], axis=1) for r, i in blocks], axis=0)
        xh, xl = halves(x)
        th, tl = table_ref[2 * table], table_ref[2 * table + 1]
        y = mm(xh, th) + (mm(xl, th) + mm(xh, tl))
        return [
            (y[q * length : (q + 1) * length, :length], y[q * length : (q + 1) * length, length:])
            for q in range(len(blocks))
        ]

    def left_mul(blocks, table):
        x = jnp.concatenate(
            [
                jnp.concatenate([r for r, _ in blocks], axis=1),
                jnp.concatenate([i for _, i in blocks], axis=1),
            ],
            axis=0,
        )
        xh, xl = halves(x)
        th, tl = table_ref[2 * table], table_ref[2 * table + 1]
        y = mm(th, xh) + (mm(th, xl) + mm(tl, xh))
        return [
            (y[:length, q * length : (q + 1) * length], y[length:, q * length : (q + 1) * length])
            for q in range(len(blocks))
        ]

    def fourier(blocks):
        return left_mul(right_mul(blocks, 1), 0)

    def inverse(blocks):
        return left_mul(right_mul(blocks, 0), 1)

    def times(a, b):
        return a[0] * b[0] - a[1] * b[1], a[0] * b[1] + a[1] * b[0]

    def conj_times(a, b):
        return a[0] * b[0] + a[1] * b[1], a[0] * b[1] - a[1] * b[0]

    wide = lax.broadcasted_iota(jnp.int32, (length, lanes), 1)

    @pl.loop(0, pl.cdiv(count[0], GROUP))
    def _(trip):
        slots = [jnp.minimum(trip * GROUP + q, offsets.shape[0] // 2 - 1) for q in range(GROUP)]
        weight = [
            jnp.where(trip * GROUP + q < count[0], 4.0, 0.0).astype(jnp.float32)
            for q in range(GROUP)
        ]
        row = [offsets[2 * k] for k in slots]
        col = [offsets[2 * k + 1] for k in slots]

        def window(q, s):
            back = jnp.where(col[q] == 0, 0, lanes - col[q])
            parts = []
            for part in range(2):
                near = pltpu.roll(ext[s, part, 0, pl.ds(row[q], length), :], back, 1)
                far = pltpu.roll(ext[s, part, 1, pl.ds(row[q], length), :], back, 1)
                parts.append(jnp.where(wide < lanes - col[q], near, far))
            return tuple(parts)

        prop = (prop_ref[0], prop_ref[1])
        probe = (probe_ref[0], probe_ref[1])
        fields = [[probe] * GROUP]
        for s in range(layers):
            exits = [times(fields[s][q], window(q, s)) for q in range(GROUP)]
            if s < layers - 1:
                spectrum = [times(b, prop) for b in fourier(exits)]
                fields.append(inverse(spectrum))
        far = fourier(exits)
        back = []
        for q in range(GROUP):
            re, im = far[q]
            factor = weight[q] * (re * re + im * im - data_ref[slots[q]])
            back.append((factor * re, factor * im))
        grad = inverse(back)
        for s in reversed(range(layers)):
            for q in range(GROUP):
                own = conj_times(fields[s][q], grad[q])
                for part in range(2):
                    turned = pltpu.roll(own[part], col[q], 1)
                    rows_of = pl.ds(row[q], length)
                    acc[s, part, 0, rows_of, :] += jnp.where(wide >= col[q], turned, 0.0)
                    acc[s, part, 1, rows_of, :] += jnp.where(wide < col[q], turned, 0.0)
            if s > 0:
                spectrum = fourier([conj_times(window(q, s), grad[q]) for q in range(GROUP)])
                grad = inverse([conj_times(prop, b) for b in spectrum])

    for s in range(layers):
        re0, re1, im0, im1 = acc[s, 0, 0], acc[s, 0, 1], acc[s, 1, 0], acc[s, 1, 1]
        left = jnp.where(low_half, re0, pltpu.roll(im0, core, 1))
        right = jnp.where(low_half, re1, pltpu.roll(im1, core, 1))
        gmid_ref[s] = jnp.where(low_half, pltpu.roll(re0, core, 1), im0)
        gfar_ref[s] = jnp.where(is_first, left, right)
        gnear_ref[s] = jnp.where(is_first, right, left)


def tile_gradient(offsets, count, place, far, mid, near, probe, prop, data, table):
    layers, rows, lanes = mid.shape
    vmem = pl.BlockSpec(memory_space=pltpu.VMEM)
    smem = pl.BlockSpec(memory_space=pltpu.SMEM)
    strip = jax.ShapeDtypeStruct(mid.shape, jnp.float32)
    return pl.pallas_call(
        gradient_kernel,
        out_shape=(strip, strip, strip),
        in_specs=[smem] * 3 + [vmem] * 7,
        out_specs=(vmem, vmem, vmem),
        scratch_shapes=[pltpu.VMEM((layers, 2, 2, rows, lanes), jnp.float32)] * 2,
        compiler_params=pltpu.CompilerParams(vmem_limit_bytes=32 * 1024 * 1024),
        name="tile_gradient",
    )(offsets, count, place, far, mid, near, probe, prop, data, table)


def around(shard, axis, by):
    count = lax.axis_size(axis)
    return lax.ppermute(shard, axis, [(i, (i + by) % count) for i in range(count)])


def partners(far, near, axis):
    count = lax.axis_size(axis)
    ends = count - 1
    outer = [(i, min(max(i + 1 if i % 2 else i - 1, 0), ends)) for i in range(count)]
    inner = [(i, i ^ 1) for i in range(count)]
    return lax.ppermute(far, axis, outer), lax.ppermute(near, axis, inner)


def on_device(
    transmission, probe_field, propagator_phase, scan_offsets, position_counts, intensities
):
    core = transmission.shape[2]
    tall, broad = lax.axis_size("ty"), lax.axis_size("tx")
    row, col = lax.axis_index("ty"), lax.axis_index("tx")
    table = jnp.asarray(dft_blocks(probe_field.shape[1]))
    prop = jnp.stack([jnp.cos(propagator_phase), jnp.sin(propagator_phase)])
    is_first = col % 2 == 0
    has_far = jnp.where(is_first, col > 0, col < broad - 1)
    place = jnp.stack([is_first, has_far]).astype(jnp.int32)
    has_above, has_below = row > 0, row < tall - 1

    def gradient(strip, far, near):
        gfar, gmid, gnear = tile_gradient(
            scan_offsets.reshape(-1), position_counts.reshape(-1), place, far, strip, near,
            probe_field, prop, intensities[0, 0], table,
        )
        far, near = partners(gfar, gnear, "tx")
        return gmid + near + jnp.where(has_far, far, 0.0)

    own = jnp.concatenate([transmission[0], transmission[1]], axis=-1)
    above = jnp.where(has_above, around(own, "ty", 1), 0.0)
    below = jnp.where(has_below, around(own, "ty", -1), 0.0)
    strip = jnp.concatenate([above, own, below], axis=1)
    for sweep in range(ITERS):
        total = gradient(strip, *partners(strip, strip, "tx"))
        top, mid, bottom = total[:, :core], total[:, core : 2 * core], total[:, 2 * core :]
        if sweep < ITERS - 1:
            down = jnp.where(has_above, around(total[:, core:], "ty", 1), 0.0)
            up = jnp.where(has_below, around(total[:, : 2 * core], "ty", -1), 0.0)
            if tall == 4:
                mixed = around(jnp.where(row < 2, bottom, top), "ty", 2)
                down2, up2 = jnp.where(row < 2, 0.0, mixed), jnp.where(row < 2, mixed, 0.0)
            else:
                down2 = jnp.where(row > 1, around(bottom, "ty", 2), 0.0)
                up2 = jnp.where(row < tall - 2, around(top, "ty", -2), 0.0)
            above = jnp.where(has_above, top + down[:, :core] + down2, 0.0)
            inside = mid + down[:, core:] + up[:, :core]
            below = jnp.where(has_below, bottom + up[:, core:] + up2, 0.0)
            strip = strip - STEP * jnp.concatenate([above, inside, below], axis=1)
        else:
            down = jnp.where(has_above, around(bottom, "ty", 1), 0.0)
            up = jnp.where(has_below, around(top, "ty", -1), 0.0)
            own = strip[:, core : 2 * core] - STEP * (mid + down + up)
    return jnp.stack([own[..., :core], own[..., core:]])


def solution(mesh):
    in_specs = (
        P(None, None, "ty", "tx"),
        P(),
        P(),
        P("ty", "tx", None, None),
        P("ty", "tx"),
        P("ty", "tx", None, None, None),
    )
    return jax.shard_map(
        on_device, mesh=mesh, in_specs=in_specs, out_specs=P(None, None, "ty", "tx"), check_vma=False
    )
```

profile of v0, /device:TPU:8, one launch (start us, length us, event | category | flops | bytes accessed | tf_op | source)
XLA Modules:
  0.0 80.6 jit_solution(10183270559972057415)
XLA Ops:
  0.0 0.9 %slice_bitcast_fusion.3 = (f32[2,64,64]{2,1,0:T(8,128)S(1)}, f32[2,64,64]{2,1,0:T(8,128)S(1)}) fusion(f32[2,2,64,64]{3,2,1,0:T(8,128)} %param.7), kind=kLoop, calls=%fused_computation.27 | loop fusion | bytes 131072 | tf_op jit(solution)/shard_map/squeeze | solution.py:201
  0.9 0.1 pad_maximum_fusion.3
  1.0 2.5 %collective-permute-start.1 = (f32[2,64,128]{2,1,0:T(8,128)S(1)}, f32[2,64,128]{2,1,0:T(8,128)S(1)}, u32[]{:S(2)}, u32[]{:S(2)}) collective-permute-start(f32[2,64,128]{2,1,0:T(8,128)S(1)} %pad_maximum_fusion.3), channel_id=1, source_target_pairs={{0,24},{8,0},{16,8},{24,16},{1,25},{9,1},{17,9},{25,17},{2,26},{10... | collective-permute-start | bytes 196616 | tf_op jit(solution)/shard_map/ppermute | solution.py:169
  3.5 0.2 cosine_bitcast_fusion
  4.5 0.1 copy.9
  4.6 0.1 reshape.8.offsets
  4.7 0.9 %collective-permute-done.1 = f32[2,64,128]{2,1,0:T(8,128)S(1)} collective-permute-done((f32[2,64,128]{2,1,0:T(8,128)S(1)}, f32[2,64,128]{2,1,0:T(8,128)S(1)}, u32[]{:S(2)}, u32[]{:S(2)}) %collective-permute-start.1) | collective-permute-done | bytes 65568 | tf_op jit(solution)/shard_map/ppermute | solution.py:169
  5.5 3.1 %collective-permute-done = f32[2,64,128]{2,1,0:T(8,128)S(1)} collective-permute-done((f32[2,64,128]{2,1,0:T(8,128)S(1)}, f32[2,64,128]{2,1,0:T(8,128)S(1)}, u32[]{:S(2)}, u32[]{:S(2)}) %collective-permute-start) | collective-permute-done | bytes 65568 | tf_op jit(solution)/shard_map/ppermute | solution.py:169
  8.7 0.1 pad_maximum_fusion.mid_ref
  8.8 0.1 collective-permute-start.3
  8.8 2.4 %collective-permute-start.2 = (f32[2,192,128]{2,1,0:T(8,128)S(1)}, f32[2,192,128]{2,1,0:T(8,128)S(1)}, u32[]{:S(2)}, u32[]{:S(2)}) collective-permute-start(f32[2,192,128]{2,1,0:T(8,128)S(1)} %pad_maximum_fusion.mid_ref), channel_id=1, source_target_pairs={{0,0},{1,2},{2,1},{3,4},{4,3},{5,6},{6,5},{7,7},{8,8},{9,10},{10,9... | collective-permute-start | bytes 589832 | tf_op jit(solution)/shard_map/ppermute | solution.py:177
  11.3 0.1 add_convert_fusion.place
  11.4 4.4 %collective-permute-done.2.far_ref = f32[2,192,128]{2,1,0:T(8,128)S(1)} collective-permute-done((f32[2,192,128]{2,1,0:T(8,128)S(1)}, f32[2,192,128]{2,1,0:T(8,128)S(1)}, u32[]{:S(2)}, u32[]{:S(2)}) %collective-permute-start.2) | collective-permute-done | bytes 196640 | tf_op jit(solution)/shard_map/ppermute | solution.py:177
  15.8 13.4 %tile_gradient.2 = (f32[2,192,128]{2,1,0:T(8,128)S(1)}, f32[2,192,128]{2,1,0:T(8,128)S(1)}, f32[2,192,128]{2,1,0:T(8,128)S(1)}) custom-call(s32[12]{0:T(128)S(1)} %reshape.8.offsets, s32[1]{0:T(128)} %bitcast.16.count, s32[2]{0:T(128)S(1)} %add_convert_fusion.place, f32[2,192,128]{2,1,0:T(8,128)S(1)} %collective-permute-done.2.far_ref, ...), custom_call_target="tpu_custom_call" | custom-call | tf_op jit(solution)/shard_map/tile_gradient/pallas_call | solution.py:156
  29.2 0.1 collective-permute-start.4
  29.3 2.5 %collective-permute-start.5 = (f32[2,192,128]{2,1,0:T(8,128)S(1)}, f32[2,192,128]{2,1,0:T(8,128)S(1)}, u32[]{:S(2)}, u32[]{:S(2)}) collective-permute-start(f32[2,192,128]{2,1,0:T(8,128)S(1)} %get-tuple-element.13), channel_id=1, source_target_pairs={{0,0},{1,2},{2,1},{3,4},{4,3},{5,6},{6,5},{7,7},{8,8},{9,10},{10,9... | collective-permute-start | bytes 589832 | tf_op jit(solution)/shard_map/ppermute | solution.py:177
  31.8 4.5 %collective-permute-done.5 = f32[2,192,128]{2,1,0:T(8,128)S(1)} collective-permute-done((f32[2,192,128]{2,1,0:T(8,128)S(1)}, f32[2,192,128]{2,1,0:T(8,128)S(1)}, u32[]{:S(2)}, u32[]{:S(2)}) %collective-permute-start.5) | collective-permute-done | bytes 196640 | tf_op jit(solution)/shard_map/ppermute | solution.py:177
  36.5 1.0 %collective-permute-start.7 = (f32[2,64,128]{2,1,0:T(8,128)S(1)}, f32[2,64,128]{2,1,0:T(8,128)S(1)}, u32[]{:S(2)}, u32[]{:S(2)}) collective-permute-start(f32[2,64,128]{2,1,0:T(8,128)S(1)} %slice_select_fusion), channel_id=1, source_target_pairs={{0,16},{8,24},{16,0},{24,8},{1,17},{9,25},{17,1},{25,9},{2,18},{10... | collective-permute-start | bytes 196616 | tf_op jit(solution)/shard_map/ppermute | solution.py:169
  37.5 2.9 %collective-permute-start.8 = (f32[2,128,128]{2,1,0:T(8,128)S(1)}, f32[2,128,128]{2,1,0:T(8,128)S(1)}, u32[]{:S(2)}, u32[]{:S(2)}) collective-permute-start(f32[2,128,128]{2,1,0:T(8,128)S(1)} %get-tuple-element.23), channel_id=1, source_target_pairs={{0,24},{8,0},{16,8},{24,16},{1,25},{9,1},{17,9},{25,17},{2,26},{10... | collective-permute-start | bytes 393224 | tf_op jit(solution)/shard_map/ppermute | solution.py:169
  40.4 3.3 %collective-permute-done.6 = f32[2,128,128]{2,1,0:T(8,128)S(1)} collective-permute-done((f32[2,128,128]{2,1,0:T(8,128)S(1)}, f32[2,128,128]{2,1,0:T(8,128)S(1)}, u32[]{:S(2)}, u32[]{:S(2)}) %collective-permute-start.6) | collective-permute-done | bytes 131104 | tf_op jit(solution)/shard_map/ppermute | solution.py:169
  43.8 1.4 %collective-permute-done.8 = f32[2,128,128]{2,1,0:T(8,128)S(1)} collective-permute-done((f32[2,128,128]{2,1,0:T(8,128)S(1)}, f32[2,128,128]{2,1,0:T(8,128)S(1)}, u32[]{:S(2)}, u32[]{:S(2)}) %collective-permute-start.8) | collective-permute-done | bytes 131104 | tf_op jit(solution)/shard_map/ppermute | solution.py:169
  45.3 0.1 fusion.mid_ref
  45.4 1.9 %collective-permute-start.9 = (f32[2,192,128]{2,1,0:T(8,128)S(1)}, f32[2,192,128]{2,1,0:T(8,128)S(1)}, u32[]{:S(2)}, u32[]{:S(2)}) collective-permute-start(f32[2,192,128]{2,1,0:T(8,128)S(1)} %fusion.mid_ref), channel_id=1, source_target_pairs={{0,0},{1,2},{2,1},{3,4},{4,3},{5,6},{6,5},{7,7},{8,8},{9,10},{10,9... | collective-permute-start | bytes 589832 | tf_op jit(solution)/shard_map/ppermute | solution.py:177
  47.4 5.0 %collective-permute-done.9.far_ref = f32[2,192,128]{2,1,0:T(8,128)S(1)} collective-permute-done((f32[2,192,128]{2,1,0:T(8,128)S(1)}, f32[2,192,128]{2,1,0:T(8,128)S(1)}, u32[]{:S(2)}, u32[]{:S(2)}) %collective-permute-start.9) | collective-permute-done | bytes 196640 | tf_op jit(solution)/shard_map/ppermute | solution.py:177
  52.4 13.4 %tile_gradient.3 = (f32[2,192,128]{2,1,0:T(8,128)S(1)}, f32[2,192,128]{2,1,0:T(8,128)S(1)}, f32[2,192,128]{2,1,0:T(8,128)S(1)}) custom-call(s32[12]{0:T(128)S(1)} %reshape.8.offsets, s32[1]{0:T(128)} %bitcast.17.count, s32[2]{0:T(128)S(1)} %add_convert_fusion.place, f32[2,192,128]{2,1,0:T(8,128)S(1)} %collective-permute-done.9.far_ref, ...), custom_call_target="tpu_custom_call" | custom-call | tf_op jit(solution)/shard_map/tile_gradient/pallas_call | solution.py:156
  65.9 1.9 %collective-permute-start.12 = (f32[2,192,128]{2,1,0:T(8,128)S(1)}, f32[2,192,128]{2,1,0:T(8,128)S(1)}, u32[]{:S(2)}, u32[]{:S(2)}) collective-permute-start(f32[2,192,128]{2,1,0:T(8,128)S(1)} %get-tuple-element.16), channel_id=1, source_target_pairs={{0,0},{1,2},{2,1},{3,4},{4,3},{5,6},{6,5},{7,7},{8,8},{9,10},{10,9... | collective-permute-start | bytes 589832 | tf_op jit(solution)/shard_map/ppermute | solution.py:177
  67.9 5.0 %collective-permute-done.12 = f32[2,192,128]{2,1,0:T(8,128)S(1)} collective-permute-done((f32[2,192,128]{2,1,0:T(8,128)S(1)}, f32[2,192,128]{2,1,0:T(8,128)S(1)}, u32[]{:S(2)}, u32[]{:S(2)}) %collective-permute-start.12) | collective-permute-done | bytes 196640 | tf_op jit(solution)/shard_map/ppermute | solution.py:177
  73.0 2.9 %collective-permute-start.14 = (f32[2,64,128]{2,1,0:T(8,128)S(1)}, f32[2,64,128]{2,1,0:T(8,128)S(1)}, u32[]{:S(2)}, u32[]{:S(2)}) collective-permute-start(f32[2,64,128]{2,1,0:T(8,128)S(1)} %get-tuple-element.21), channel_id=1, source_target_pairs={{0,24},{8,0},{16,8},{24,16},{1,25},{9,1},{17,9},{25,17},{2,26},{10... | collective-permute-start | bytes 196616 | tf_op jit(solution)/shard_map/ppermute | solution.py:169
  75.9 2.9 %collective-permute-done.13 = f32[2,64,128]{2,1,0:T(8,128)S(1)} collective-permute-done((f32[2,64,128]{2,1,0:T(8,128)S(1)}, f32[2,64,128]{2,1,0:T(8,128)S(1)}, u32[]{:S(2)}, u32[]{:S(2)}) %collective-permute-start.13) | collective-permute-done | bytes 65568 | tf_op jit(solution)/shard_map/ppermute | solution.py:169
  78.9 1.0 %collective-permute-done.14 = f32[2,64,128]{2,1,0:T(8,128)S(1)} collective-permute-done((f32[2,64,128]{2,1,0:T(8,128)S(1)}, f32[2,64,128]{2,1,0:T(8,128)S(1)}, u32[]{:S(2)}, u32[]{:S(2)}) %collective-permute-start.14) | collective-permute-done | bytes 65568 | tf_op jit(solution)/shard_map/ppermute | solution.py:169
  79.9 0.1 slice_bitcast_fusion.1
  80.0 0.7 pad_maximum_fusion.2
  (32 shorter events, 0.5 us)
Async XLA Ops:
  0.9 2.6 %copy-start.3 = (f32[128,128]{1,0:T(8,128)S(1)}, f32[128,128]{1,0:T(8,128)}, u32[]{:S(2)}) copy-start(f32[128,128]{1,0:T(8,128)} %param.9) | copy-start | bytes 196612
  1.0 4.6 %collective-permute-start.1 = (f32[2,64,128]{2,1,0:T(8,128)S(1)}, f32[2,64,128]{2,1,0:T(8,128)S(1)}, u32[]{:S(2)}, u32[]{:S(2)}) collective-permute-start(f32[2,64,128]{2,1,0:T(8,128)S(1)} %pad_maximum_fusion.3), channel_id=1, source_target_pairs={{0,24},{8,0},{16,8},{24,16},{1,25},{9,1},{17,9},{25,17},{2,26},{10... | collective-permute-start | bytes 196616 | tf_op jit(solution)/shard_map/ppermute | solution.py:169
  3.5 5.2 %collective-permute-start = (f32[2,64,128]{2,1,0:T(8,128)S(1)}, f32[2,64,128]{2,1,0:T(8,128)S(1)}, u32[]{:S(2)}, u32[]{:S(2)}) collective-permute-start(f32[2,64,128]{2,1,0:T(8,128)S(1)} %pad_maximum_fusion.3), channel_id=1, source_target_pairs={{0,8},{8,16},{16,24},{24,0},{1,9},{9,17},{17,25},{25,1},{2,10},{10... | collective-permute-start | bytes 196616 | tf_op jit(solution)/shard_map/ppermute | solution.py:169
  3.5 1.0 %copy-start.4 = (s32[1,1,6,2]{2,3,1,0:T(2,128)S(1)}, s32[1,1,6,2]{2,3,1,0:T(2,128)}, u32[]{:S(2)}) copy-start(s32[1,1,6,2]{2,3,1,0:T(2,128)} %param.10) | copy-start | bytes 148
  3.7 12.1 %copy-start.2 = (f32[2,128,128]{2,1,0:T(8,128)S(1)}, f32[2,128,128]{2,1,0:T(8,128)}, u32[]{:S(2)}) copy-start(f32[2,128,128]{2,1,0:T(8,128)} %probe_ref.3) | copy-start | bytes 393220
  3.8 12.1 %copy-start = (bf16[4,256,256]{2,1,0:T(8,128)(2,1)S(1)}, bf16[4,256,256]{2,1,0:T(8,128)(2,1)}, u32[]{:S(2)}) copy-start(bf16[4,256,256]{2,1,0:T(8,128)(2,1)} %constant.33.clone.table_ref) | copy-start | bytes 1572868
  8.7 7.2 %copy-start.1 = (f32[1,1,6,128,128]{4,3,2,1,0:T(8,128)S(1)}, f32[1,1,6,128,128]{4,3,2,1,0:T(8,128)}, u32[]{:S(2)}) copy-start(f32[1,1,6,128,128]{4,3,2,1,0:T(8,128)} %param.12) | copy-start | bytes 1179652
  8.8 2.6 %collective-permute-start.3 = (f32[2,192,128]{2,1,0:T(8,128)S(1)}, f32[2,192,128]{2,1,0:T(8,128)S(1)}, u32[]{:S(2)}, u32[]{:S(2)}) collective-permute-start(f32[2,192,128]{2,1,0:T(8,128)S(1)} %pad_maximum_fusion.mid_ref), channel_id=1, source_target_pairs={{0,1},{1,0},{2,3},{3,2},{4,5},{5,4},{6,7},{7,6},{8,9},{9,8},{10,11... | collective-permute-start | bytes 589832 | tf_op jit(solution)/shard_map/ppermute | solution.py:177
  8.8 7.0 %collective-permute-start.2 = (f32[2,192,128]{2,1,0:T(8,128)S(1)}, f32[2,192,128]{2,1,0:T(8,128)S(1)}, u32[]{:S(2)}, u32[]{:S(2)}) collective-permute-start(f32[2,192,128]{2,1,0:T(8,128)S(1)} %pad_maximum_fusion.mid_ref), channel_id=1, source_target_pairs={{0,0},{1,2},{2,1},{3,4},{4,3},{5,6},{6,5},{7,7},{8,8},{9,10},{10,9... | collective-permute-start | bytes 589832 | tf_op jit(solution)/shard_map/ppermute | solution.py:177
  29.2 2.6 %collective-permute-start.4 = (f32[2,192,128]{2,1,0:T(8,128)S(1)}, f32[2,192,128]{2,1,0:T(8,128)S(1)}, u32[]{:S(2)}, u32[]{:S(2)}) collective-permute-start(f32[2,192,128]{2,1,0:T(8,128)S(1)} %get-tuple-element.12), channel_id=1, source_target_pairs={{0,1},{1,0},{2,3},{3,2},{4,5},{5,4},{6,7},{7,6},{8,9},{9,8},{10,11... | collective-permute-start | bytes 589832 | tf_op jit(solution)/shard_map/ppermute | solution.py:177
  29.3 7.0 %collective-permute-start.5 = (f32[2,192,128]{2,1,0:T(8,128)S(1)}, f32[2,192,128]{2,1,0:T(8,128)S(1)}, u32[]{:S(2)}, u32[]{:S(2)}) collective-permute-start(f32[2,192,128]{2,1,0:T(8,128)S(1)} %get-tuple-element.13), channel_id=1, source_target_pairs={{0,0},{1,2},{2,1},{3,4},{4,3},{5,6},{6,5},{7,7},{8,8},{9,10},{10,9... | collective-permute-start | bytes 589832 | tf_op jit(solution)/shard_map/ppermute | solution.py:177
  36.4 7.4 %collective-permute-start.6 = (f32[2,128,128]{2,1,0:T(8,128)S(1)}, f32[2,128,128]{2,1,0:T(8,128)S(1)}, u32[]{:S(2)}, u32[]{:S(2)}) collective-permute-start(f32[2,128,128]{2,1,0:T(8,128)S(1)} %get-tuple-element.22), channel_id=1, source_target_pairs={{0,8},{8,16},{16,24},{24,0},{1,9},{9,17},{17,25},{25,1},{2,10},{10... | collective-permute-start | bytes 393224 | tf_op jit(solution)/shard_map/ppermute | solution.py:169
  36.5 8.8 %collective-permute-start.7 = (f32[2,64,128]{2,1,0:T(8,128)S(1)}, f32[2,64,128]{2,1,0:T(8,128)S(1)}, u32[]{:S(2)}, u32[]{:S(2)}) collective-permute-start(f32[2,64,128]{2,1,0:T(8,128)S(1)} %slice_select_fusion), channel_id=1, source_target_pairs={{0,16},{8,24},{16,0},{24,8},{1,17},{9,25},{17,1},{25,9},{2,18},{10... | collective-permute-start | bytes 196616 | tf_op jit(solution)/shard_map/ppermute | solution.py:169
  37.5 7.7 %collective-permute-start.8 = (f32[2,128,128]{2,1,0:T(8,128)S(1)}, f32[2,128,128]{2,1,0:T(8,128)S(1)}, u32[]{:S(2)}, u32[]{:S(2)}) collective-permute-start(f32[2,128,128]{2,1,0:T(8,128)S(1)} %get-tuple-element.23), channel_id=1, source_target_pairs={{0,24},{8,0},{16,8},{24,16},{1,25},{9,1},{17,9},{25,17},{2,26},{10... | collective-permute-start | bytes 393224 | tf_op jit(solution)/shard_map/ppermute | solution.py:169
  45.4 2.0 %collective-permute-start.10 = (f32[2,192,128]{2,1,0:T(8,128)S(1)}, f32[2,192,128]{2,1,0:T(8,128)S(1)}, u32[]{:S(2)}, u32[]{:S(2)}) collective-permute-start(f32[2,192,128]{2,1,0:T(8,128)S(1)} %fusion.mid_ref), channel_id=1, source_target_pairs={{0,1},{1,0},{2,3},{3,2},{4,5},{5,4},{6,7},{7,6},{8,9},{9,8},{10,11... | collective-permute-start | bytes 589832 | tf_op jit(solution)/shard_map/ppermute | solution.py:177
  45.4 7.0 %collective-permute-start.9 = (f32[2,192,128]{2,1,0:T(8,128)S(1)}, f32[2,192,128]{2,1,0:T(8,128)S(1)}, u32[]{:S(2)}, u32[]{:S(2)}) collective-permute-start(f32[2,192,128]{2,1,0:T(8,128)S(1)} %fusion.mid_ref), channel_id=1, source_target_pairs={{0,0},{1,2},{2,1},{3,4},{4,3},{5,6},{6,5},{7,7},{8,8},{9,10},{10,9... | collective-permute-start | bytes 589832 | tf_op jit(solution)/shard_map/ppermute | solution.py:177
  65.8 2.0 %collective-permute-start.11 = (f32[2,192,128]{2,1,0:T(8,128)S(1)}, f32[2,192,128]{2,1,0:T(8,128)S(1)}, u32[]{:S(2)}, u32[]{:S(2)}) collective-permute-start(f32[2,192,128]{2,1,0:T(8,128)S(1)} %get-tuple-element.15), channel_id=1, source_target_pairs={{0,1},{1,0},{2,3},{3,2},{4,5},{5,4},{6,7},{7,6},{8,9},{9,8},{10,11... | collective-permute-start | bytes 589832 | tf_op jit(solution)/shard_map/ppermute | solution.py:177
  65.9 7.0 %collective-permute-start.12 = (f32[2,192,128]{2,1,0:T(8,128)S(1)}, f32[2,192,128]{2,1,0:T(8,128)S(1)}, u32[]{:S(2)}, u32[]{:S(2)}) collective-permute-start(f32[2,192,128]{2,1,0:T(8,128)S(1)} %get-tuple-element.16), channel_id=1, source_target_pairs={{0,0},{1,2},{2,1},{3,4},{4,3},{5,6},{6,5},{7,7},{8,8},{9,10},{10,9... | collective-permute-start | bytes 589832 | tf_op jit(solution)/shard_map/ppermute | solution.py:177
  72.9 5.9 %collective-permute-start.13 = (f32[2,64,128]{2,1,0:T(8,128)S(1)}, f32[2,64,128]{2,1,0:T(8,128)S(1)}, u32[]{:S(2)}, u32[]{:S(2)}) collective-permute-start(f32[2,64,128]{2,1,0:T(8,128)S(1)} %get-tuple-element.20), channel_id=1, source_target_pairs={{0,8},{8,16},{16,24},{24,0},{1,9},{9,17},{17,25},{25,1},{2,10},{10... | collective-permute-start | bytes 196616 | tf_op jit(solution)/shard_map/ppermute | solution.py:169
  73.0 6.8 %collective-permute-start.14 = (f32[2,64,128]{2,1,0:T(8,128)S(1)}, f32[2,64,128]{2,1,0:T(8,128)S(1)}, u32[]{:S(2)}, u32[]{:S(2)}) collective-permute-start(f32[2,64,128]{2,1,0:T(8,128)S(1)} %get-tuple-element.21), channel_id=1, source_target_pairs={{0,24},{8,0},{16,8},{24,16},{1,25},{9,1},{17,9},{25,17},{2,26},{10... | collective-permute-start | bytes 196616 | tf_op jit(solution)/shard_map/ppermute | solution.py:169
where the time goes:
time: 81.1 us; the launch traced here: 80.6 us
  waiting for transfers between devices  31.7 us (39%)
  Pallas kernels  26.8 us (33%)
  starting transfers between devices  18.5 us (23%)
  local copies, waits for them, and re-layouts  1.43 us (2%)
  other arithmetic  1.22 us (2%)
  between operations  0.98 us (1%)
    pallas_call x2, Pallas kernels, tile_gradient(): pl.pallas_call(gradient_kernel, out_shape=(strip, strip, strip), in_specs...  26.8 us
    ppermute x8, waiting for transfers between devices, partners(): return (lax.ppermute(far, axis, outer), lax.ppermute(near, axis, inner))  19 us
    ppermute x7, waiting for transfers between devices, around(): lax.ppermute(shard, axis, [(i, (i + by) % count) for i in range(count)])  12.7 us
    ppermute x7, starting transfers between devices, around(): lax.ppermute(shard, axis, [(i, (i + by) % count) for i in range(count)])  9.46 us
    ppermute x8, starting transfers between devices, partners(): return (lax.ppermute(far, axis, outer), lax.ppermute(near, axis, inner))  9.06 us
  transfers between devices with their start and end apart: 15, of which 10 were waited for; matrix products, arithmetic and copies ran while one was open for 1% of the time, Pallas kernels for 0%

commit v1 on v0

--- a/solution.py
+++ b/solution.py
@@ -10,7 +10,7 @@
 
 ITERS = 2
 STEP = 0.003
-GROUP = 2
+GROUP = 6
 
 
 def dft_blocks(length):
@@ -39,6 +39,8 @@
     layers, rows, lanes = mid_ref.shape
     length = probe_ref.shape[1]
     core = lanes // 2
+    positions = offsets.shape[0] // 2
+    group = min(GROUP, positions)
     lane = lax.broadcasted_iota(jnp.int32, (rows, lanes), 1)
     low_half = lane < core
     is_first, has_far = place[0] == 1, place[1] == 1
@@ -93,12 +95,12 @@
 
     wide = lax.broadcasted_iota(jnp.int32, (length, lanes), 1)
 
-    @pl.loop(0, pl.cdiv(count[0], GROUP))
+    @pl.loop(0, pl.cdiv(count[0], group))
     def _(trip):
-        slots = [jnp.minimum(trip * GROUP + q, offsets.shape[0] // 2 - 1) for q in range(GROUP)]
+        slots = [jnp.minimum(trip * group + q, positions - 1) for q in range(group)]
         weight = [
-            jnp.where(trip * GROUP + q < count[0], 4.0, 0.0).astype(jnp.float32)
-            for q in range(GROUP)
+            jnp.where(trip * group + q < count[0], 4.0, 0.0).astype(jnp.float32)
+            for q in range(group)
         ]
         row = [offsets[2 * k] for k in slots]
         col = [offsets[2 * k + 1] for k in slots]
@@ -107,28 +109,29 @@
             back = jnp.where(col[q] == 0, 0, lanes - col[q])
             parts = []
             for part in range(2):
-                near = pltpu.roll(ext[s, part, 0, pl.ds(row[q], length), :], back, 1)
-                far = pltpu.roll(ext[s, part, 1, pl.ds(row[q], length), :], back, 1)
-                parts.append(jnp.where(wide < lanes - col[q], near, far))
+                rows_of = pl.ds(row[q], length)
+                both = jnp.where(wide >= col[q], ext[s, part, 0, rows_of, :], ext[s, part, 1, rows_of, :])
+                parts.append(pltpu.roll(both, back, 1))
             return tuple(parts)
 
         prop = (prop_ref[0], prop_ref[1])
         probe = (probe_ref[0], probe_ref[1])
-        fields = [[probe] * GROUP]
+        windows = [[window(q, s) for q in range(group)] for s in range(layers)]
+        fields = [[probe] * group]
         for s in range(layers):
-            exits = [times(fields[s][q], window(q, s)) for q in range(GROUP)]
+            exits = [times(fields[s][q], windows[s][q]) for q in range(group)]
             if s < layers - 1:
                 spectrum = [times(b, prop) for b in fourier(exits)]
                 fields.append(inverse(spectrum))
         far = fourier(exits)
         back = []
-        for q in range(GROUP):
+        for q in range(group):
             re, im = far[q]
             factor = weight[q] * (re * re + im * im - data_ref[slots[q]])
             back.append((factor * re, factor * im))
         grad = inverse(back)
         for s in reversed(range(layers)):
-            for q in range(GROUP):
+            for q in range(group):
                 own = conj_times(fields[s][q], grad[q])
                 for part in range(2):
                     turned = pltpu.roll(own[part], col[q], 1)
@@ -136,7 +139,7 @@
                     acc[s, part, 0, rows_of, :] += jnp.where(wide >= col[q], turned, 0.0)
                     acc[s, part, 1, rows_of, :] += jnp.where(wide < col[q], turned, 0.0)
             if s > 0:
-                spectrum = fourier([conj_times(window(q, s), grad[q]) for q in range(GROUP)])
+                spectrum = fourier([conj_times(windows[s][q], grad[q]) for q in range(group)])
                 grad = inverse([conj_times(prop, b) for b in spectrum])
 
     for s in range(layers):

time: 81.1 us -> 71.8 us (0.89)
  Pallas kernels: 26.8 us -> 17.4 us
    pallas_call x2, Pallas kernels: 26.8 us -> 17.4 us  [tile_gradient(): pl.pallas_call(gradient_kernel, out_shape=(strip, strip, strip), in_specs...]
where the time goes in v1:
time: 71.8 us; the launch traced here: 71.4 us
  waiting for transfers between devices  31.8 us (44%)
  starting transfers between devices  18.5 us (26%)
  Pallas kernels  17.4 us (24%)
  local copies, waits for them, and re-layouts  1.43 us (2%)
  other arithmetic  1.22 us (2%)
  between operations  0.95 us (1%)
    ppermute x8, waiting for transfers between devices, partners(): return (lax.ppermute(far, axis, outer), lax.ppermute(near, axis, inner))  19.5 us
    pallas_call x2, Pallas kernels, tile_gradient(): pl.pallas_call(gradient_kernel, out_shape=(strip, strip, strip), in_specs...  17.4 us
    ppermute x7, waiting for transfers between devices, around(): lax.ppermute(shard, axis, [(i, (i + by) % count) for i in range(count)])  12.3 us
    ppermute x8, starting transfers between devices, partners(): return (lax.ppermute(far, axis, outer), lax.ppermute(near, axis, inner))  9.52 us
    ppermute x7, starting transfers between devices, around(): lax.ppermute(shard, axis, [(i, (i + by) % count) for i in range(count)])  9.02 us
  transfers between devices with their start and end apart: 15, of which 10 were waited for; matrix products, arithmetic and copies ran while one was open for 1% of the time, Pallas kernels for 0%

profile of v1, /device:TPU:8, one launch (start us, length us, event | category | flops | bytes accessed | tf_op | source)
XLA Modules:
  0.0 71.4 jit_solution(13680562602064945295)
XLA Ops:
  0.0 0.9 %slice_bitcast_fusion.3 = (f32[2,64,64]{2,1,0:T(8,128)S(1)}, f32[2,64,64]{2,1,0:T(8,128)S(1)}) fusion(f32[2,2,64,64]{3,2,1,0:T(8,128)} %param.7), kind=kLoop, calls=%fused_computation.27 | loop fusion | bytes 131072 | tf_op jit(solution)/shard_map/squeeze | solution.py:204
  0.9 0.1 pad_maximum_fusion.3
  1.0 2.5 %collective-permute-start.1 = (f32[2,64,128]{2,1,0:T(8,128)S(1)}, f32[2,64,128]{2,1,0:T(8,128)S(1)}, u32[]{:S(2)}, u32[]{:S(2)}) collective-permute-start(f32[2,64,128]{2,1,0:T(8,128)S(1)} %pad_maximum_fusion.3), channel_id=1, source_target_pairs={{0,24},{8,0},{16,8},{24,16},{1,25},{9,1},{17,9},{25,17},{2,26},{10... | collective-permute-start | bytes 196616 | tf_op jit(solution)/shard_map/ppermute | solution.py:172
  3.5 0.2 cosine_bitcast_fusion
  4.5 0.1 copy.9
  4.6 0.1 reshape.8.offsets
  4.7 0.9 %collective-permute-done.1 = f32[2,64,128]{2,1,0:T(8,128)S(1)} collective-permute-done((f32[2,64,128]{2,1,0:T(8,128)S(1)}, f32[2,64,128]{2,1,0:T(8,128)S(1)}, u32[]{:S(2)}, u32[]{:S(2)}) %collective-permute-start.1) | collective-permute-done | bytes 65568 | tf_op jit(solution)/shard_map/ppermute | solution.py:172
  5.5 3.1 %collective-permute-done = f32[2,64,128]{2,1,0:T(8,128)S(1)} collective-permute-done((f32[2,64,128]{2,1,0:T(8,128)S(1)}, f32[2,64,128]{2,1,0:T(8,128)S(1)}, u32[]{:S(2)}, u32[]{:S(2)}) %collective-permute-start) | collective-permute-done | bytes 65568 | tf_op jit(solution)/shard_map/ppermute | solution.py:172
  8.7 0.1 pad_maximum_fusion.mid_ref
  8.8 2.4 %collective-permute-start.2 = (f32[2,192,128]{2,1,0:T(8,128)S(1)}, f32[2,192,128]{2,1,0:T(8,128)S(1)}, u32[]{:S(2)}, u32[]{:S(2)}) collective-permute-start(f32[2,192,128]{2,1,0:T(8,128)S(1)} %pad_maximum_fusion.mid_ref), channel_id=1, source_target_pairs={{0,0},{1,2},{2,1},{3,4},{4,3},{5,6},{6,5},{7,7},{8,8},{9,10},{10,9... | collective-permute-start | bytes 589832 | tf_op jit(solution)/shard_map/ppermute | solution.py:180
  11.4 4.4 %collective-permute-done.2.far_ref = f32[2,192,128]{2,1,0:T(8,128)S(1)} collective-permute-done((f32[2,192,128]{2,1,0:T(8,128)S(1)}, f32[2,192,128]{2,1,0:T(8,128)S(1)}, u32[]{:S(2)}, u32[]{:S(2)}) %collective-permute-start.2) | collective-permute-done | bytes 196640 | tf_op jit(solution)/shard_map/ppermute | solution.py:180
  15.8 8.6 %tile_gradient.2 = (f32[2,192,128]{2,1,0:T(8,128)S(1)}, f32[2,192,128]{2,1,0:T(8,128)S(1)}, f32[2,192,128]{2,1,0:T(8,128)S(1)}) custom-call(s32[12]{0:T(128)S(1)} %reshape.8.offsets, s32[1]{0:T(128)} %bitcast.16.count, s32[2]{0:T(128)S(1)} %add_convert_fusion.place, f32[2,192,128]{2,1,0:T(8,128)S(1)} %collective-permute-done.2.far_ref, ...), custom_call_target="tpu_custom_call" | custom-call | tf_op jit(solution)/shard_map/tile_gradient/pallas_call | solution.py:159
  24.5 0.6 collective-permute-start.4
  25.0 2.0 %collective-permute-start.5 = (f32[2,192,128]{2,1,0:T(8,128)S(1)}, f32[2,192,128]{2,1,0:T(8,128)S(1)}, u32[]{:S(2)}, u32[]{:S(2)}) collective-permute-start(f32[2,192,128]{2,1,0:T(8,128)S(1)} %get-tuple-element.13), channel_id=1, source_target_pairs={{0,0},{1,2},{2,1},{3,4},{4,3},{5,6},{6,5},{7,7},{8,8},{9,10},{10,9... | collective-permute-start | bytes 589832 | tf_op jit(solution)/shard_map/ppermute | solution.py:180
  27.0 5.0 %collective-permute-done.5 = f32[2,192,128]{2,1,0:T(8,128)S(1)} collective-permute-done((f32[2,192,128]{2,1,0:T(8,128)S(1)}, f32[2,192,128]{2,1,0:T(8,128)S(1)}, u32[]{:S(2)}, u32[]{:S(2)}) %collective-permute-start.5) | collective-permute-done | bytes 196640 | tf_op jit(solution)/shard_map/ppermute | solution.py:180
  32.1 0.1 collective-permute-start.6
  32.2 0.8 %collective-permute-start.7 = (f32[2,64,128]{2,1,0:T(8,128)S(1)}, f32[2,64,128]{2,1,0:T(8,128)S(1)}, u32[]{:S(2)}, u32[]{:S(2)}) collective-permute-start(f32[2,64,128]{2,1,0:T(8,128)S(1)} %slice_select_fusion), channel_id=1, source_target_pairs={{0,16},{8,24},{16,0},{24,8},{1,17},{9,25},{17,1},{25,9},{2,18},{10... | collective-permute-start | bytes 196616 | tf_op jit(solution)/shard_map/ppermute | solution.py:172
  33.1 2.6 %collective-permute-start.8 = (f32[2,128,128]{2,1,0:T(8,128)S(1)}, f32[2,128,128]{2,1,0:T(8,128)S(1)}, u32[]{:S(2)}, u32[]{:S(2)}) collective-permute-start(f32[2,128,128]{2,1,0:T(8,128)S(1)} %get-tuple-element.23), channel_id=1, source_target_pairs={{0,24},{8,0},{16,8},{24,16},{1,25},{9,1},{17,9},{25,17},{2,26},{10... | collective-permute-start | bytes 393224 | tf_op jit(solution)/shard_map/ppermute | solution.py:172
  35.6 3.8 %collective-permute-done.6 = f32[2,128,128]{2,1,0:T(8,128)S(1)} collective-permute-done((f32[2,128,128]{2,1,0:T(8,128)S(1)}, f32[2,128,128]{2,1,0:T(8,128)S(1)}, u32[]{:S(2)}, u32[]{:S(2)}) %collective-permute-start.6) | collective-permute-done | bytes 131104 | tf_op jit(solution)/shard_map/ppermute | solution.py:172
  39.4 0.9 %collective-permute-done.8 = f32[2,128,128]{2,1,0:T(8,128)S(1)} collective-permute-done((f32[2,128,128]{2,1,0:T(8,128)S(1)}, f32[2,128,128]{2,1,0:T(8,128)S(1)}, u32[]{:S(2)}, u32[]{:S(2)}) %collective-permute-start.8) | collective-permute-done | bytes 131104 | tf_op jit(solution)/shard_map/ppermute | solution.py:172
  40.5 0.1 fusion.mid_ref
  40.6 1.9 %collective-permute-start.9 = (f32[2,192,128]{2,1,0:T(8,128)S(1)}, f32[2,192,128]{2,1,0:T(8,128)S(1)}, u32[]{:S(2)}, u32[]{:S(2)}) collective-permute-start(f32[2,192,128]{2,1,0:T(8,128)S(1)} %fusion.mid_ref), channel_id=1, source_target_pairs={{0,0},{1,2},{2,1},{3,4},{4,3},{5,6},{6,5},{7,7},{8,8},{9,10},{10,9... | collective-permute-start | bytes 589832 | tf_op jit(solution)/shard_map/ppermute | solution.py:180
  42.6 5.0 %collective-permute-done.9.far_ref = f32[2,192,128]{2,1,0:T(8,128)S(1)} collective-permute-done((f32[2,192,128]{2,1,0:T(8,128)S(1)}, f32[2,192,128]{2,1,0:T(8,128)S(1)}, u32[]{:S(2)}, u32[]{:S(2)}) %collective-permute-start.9) | collective-permute-done | bytes 196640 | tf_op jit(solution)/shard_map/ppermute | solution.py:180
  47.6 8.8 %tile_gradient.3 = (f32[2,192,128]{2,1,0:T(8,128)S(1)}, f32[2,192,128]{2,1,0:T(8,128)S(1)}, f32[2,192,128]{2,1,0:T(8,128)S(1)}) custom-call(s32[12]{0:T(128)S(1)} %reshape.8.offsets, s32[1]{0:T(128)} %bitcast.17.count, s32[2]{0:T(128)S(1)} %add_convert_fusion.place, f32[2,192,128]{2,1,0:T(8,128)S(1)} %collective-permute-done.9.far_ref, ...), custom_call_target="tpu_custom_call" | custom-call | tf_op jit(solution)/shard_map/tile_gradient/pallas_call | solution.py:159
  56.4 0.6 collective-permute-start.11
  57.0 1.9 %collective-permute-start.12 = (f32[2,192,128]{2,1,0:T(8,128)S(1)}, f32[2,192,128]{2,1,0:T(8,128)S(1)}, u32[]{:S(2)}, u32[]{:S(2)}) collective-permute-start(f32[2,192,128]{2,1,0:T(8,128)S(1)} %get-tuple-element.16), channel_id=1, source_target_pairs={{0,0},{1,2},{2,1},{3,4},{4,3},{5,6},{6,5},{7,7},{8,8},{9,10},{10,9... | collective-permute-start | bytes 589832 | tf_op jit(solution)/shard_map/ppermute | solution.py:180
  58.9 5.0 %collective-permute-done.12 = f32[2,192,128]{2,1,0:T(8,128)S(1)} collective-permute-done((f32[2,192,128]{2,1,0:T(8,128)S(1)}, f32[2,192,128]{2,1,0:T(8,128)S(1)}, u32[]{:S(2)}, u32[]{:S(2)}) %collective-permute-start.12) | collective-permute-done | bytes 196640 | tf_op jit(solution)/shard_map/ppermute | solution.py:180
  64.0 1.2 %collective-permute-start.13 = (f32[2,64,128]{2,1,0:T(8,128)S(1)}, f32[2,64,128]{2,1,0:T(8,128)S(1)}, u32[]{:S(2)}, u32[]{:S(2)}) collective-permute-start(f32[2,64,128]{2,1,0:T(8,128)S(1)} %get-tuple-element.20), channel_id=1, source_target_pairs={{0,8},{8,16},{16,24},{24,0},{1,9},{9,17},{17,25},{25,1},{2,10},{10... | collective-permute-start | bytes 196616 | tf_op jit(solution)/shard_map/ppermute | solution.py:172
  65.3 1.7 %collective-permute-start.14 = (f32[2,64,128]{2,1,0:T(8,128)S(1)}, f32[2,64,128]{2,1,0:T(8,128)S(1)}, u32[]{:S(2)}, u32[]{:S(2)}) collective-permute-start(f32[2,64,128]{2,1,0:T(8,128)S(1)} %get-tuple-element.21), channel_id=1, source_target_pairs={{0,24},{8,0},{16,8},{24,16},{1,25},{9,1},{17,9},{25,17},{2,26},{10... | collective-permute-start | bytes 196616 | tf_op jit(solution)/shard_map/ppermute | solution.py:172
  67.0 2.8 %collective-permute-done.13 = f32[2,64,128]{2,1,0:T(8,128)S(1)} collective-permute-done((f32[2,64,128]{2,1,0:T(8,128)S(1)}, f32[2,64,128]{2,1,0:T(8,128)S(1)}, u32[]{:S(2)}, u32[]{:S(2)}) %collective-permute-start.13) | collective-permute-done | bytes 65568 | tf_op jit(solution)/shard_map/ppermute | solution.py:172
  69.8 0.8 %collective-permute-done.14 = f32[2,64,128]{2,1,0:T(8,128)S(1)} collective-permute-done((f32[2,64,128]{2,1,0:T(8,128)S(1)}, f32[2,64,128]{2,1,0:T(8,128)S(1)}, u32[]{:S(2)}, u32[]{:S(2)}) %collective-permute-start.14) | collective-permute-done | bytes 65568 | tf_op jit(solution)/shard_map/ppermute | solution.py:172
  70.7 0.7 pad_maximum_fusion.2
  (32 shorter events, 0.6 us)
Async XLA Ops:
  0.9 2.6 %copy-start.3 = (f32[128,128]{1,0:T(8,128)S(1)}, f32[128,128]{1,0:T(8,128)}, u32[]{:S(2)}) copy-start(f32[128,128]{1,0:T(8,128)} %param.9) | copy-start | bytes 196612
  1.0 4.6 %collective-permute-start.1 = (f32[2,64,128]{2,1,0:T(8,128)S(1)}, f32[2,64,128]{2,1,0:T(8,128)S(1)}, u32[]{:S(2)}, u32[]{:S(2)}) collective-permute-start(f32[2,64,128]{2,1,0:T(8,128)S(1)} %pad_maximum_fusion.3), channel_id=1, source_target_pairs={{0,24},{8,0},{16,8},{24,16},{1,25},{9,1},{17,9},{25,17},{2,26},{10... | collective-permute-start | bytes 196616 | tf_op jit(solution)/shard_map/ppermute | solution.py:172
  3.5 5.2 %collective-permute-start = (f32[2,64,128]{2,1,0:T(8,128)S(1)}, f32[2,64,128]{2,1,0:T(8,128)S(1)}, u32[]{:S(2)}, u32[]{:S(2)}) collective-permute-start(f32[2,64,128]{2,1,0:T(8,128)S(1)} %pad_maximum_fusion.3), channel_id=1, source_target_pairs={{0,8},{8,16},{16,24},{24,0},{1,9},{9,17},{17,25},{25,1},{2,10},{10... | collective-permute-start | bytes 196616 | tf_op jit(solution)/shard_map/ppermute | solution.py:172
  3.5 1.0 %copy-start.4 = (s32[1,1,6,2]{2,3,1,0:T(2,128)S(1)}, s32[1,1,6,2]{2,3,1,0:T(2,128)}, u32[]{:S(2)}) copy-start(s32[1,1,6,2]{2,3,1,0:T(2,128)} %param.10) | copy-start | bytes 148
  3.7 12.1 %copy-start.2 = (f32[2,128,128]{2,1,0:T(8,128)S(1)}, f32[2,128,128]{2,1,0:T(8,128)}, u32[]{:S(2)}) copy-start(f32[2,128,128]{2,1,0:T(8,128)} %probe_ref.3) | copy-start | bytes 393220
  3.8 12.1 %copy-start = (bf16[4,256,256]{2,1,0:T(8,128)(2,1)S(1)}, bf16[4,256,256]{2,1,0:T(8,128)(2,1)}, u32[]{:S(2)}) copy-start(bf16[4,256,256]{2,1,0:T(8,128)(2,1)} %constant.33.clone.table_ref) | copy-start | bytes 1572868
  8.7 7.2 %copy-start.1 = (f32[1,1,6,128,128]{4,3,2,1,0:T(8,128)S(1)}, f32[1,1,6,128,128]{4,3,2,1,0:T(8,128)}, u32[]{:S(2)}) copy-start(f32[1,1,6,128,128]{4,3,2,1,0:T(8,128)} %param.12) | copy-start | bytes 1179652
  8.8 2.6 %collective-permute-start.3 = (f32[2,192,128]{2,1,0:T(8,128)S(1)}, f32[2,192,128]{2,1,0:T(8,128)S(1)}, u32[]{:S(2)}, u32[]{:S(2)}) collective-permute-start(f32[2,192,128]{2,1,0:T(8,128)S(1)} %pad_maximum_fusion.mid_ref), channel_id=1, source_target_pairs={{0,1},{1,0},{2,3},{3,2},{4,5},{5,4},{6,7},{7,6},{8,9},{9,8},{10,11... | collective-permute-start | bytes 589832 | tf_op jit(solution)/shard_map/ppermute | solution.py:180
  8.8 7.0 %collective-permute-start.2 = (f32[2,192,128]{2,1,0:T(8,128)S(1)}, f32[2,192,128]{2,1,0:T(8,128)S(1)}, u32[]{:S(2)}, u32[]{:S(2)}) collective-permute-start(f32[2,192,128]{2,1,0:T(8,128)S(1)} %pad_maximum_fusion.mid_ref), channel_id=1, source_target_pairs={{0,0},{1,2},{2,1},{3,4},{4,3},{5,6},{6,5},{7,7},{8,8},{9,10},{10,9... | collective-permute-start | bytes 589832 | tf_op jit(solution)/shard_map/ppermute | solution.py:180
  24.5 2.6 %collective-permute-start.4 = (f32[2,192,128]{2,1,0:T(8,128)S(1)}, f32[2,192,128]{2,1,0:T(8,128)S(1)}, u32[]{:S(2)}, u32[]{:S(2)}) collective-permute-start(f32[2,192,128]{2,1,0:T(8,128)S(1)} %get-tuple-element.12), channel_id=1, source_target_pairs={{0,1},{1,0},{2,3},{3,2},{4,5},{5,4},{6,7},{7,6},{8,9},{9,8},{10,11... | collective-permute-start | bytes 589832 | tf_op jit(solution)/shard_map/ppermute | solution.py:180
  25.0 7.0 %collective-permute-start.5 = (f32[2,192,128]{2,1,0:T(8,128)S(1)}, f32[2,192,128]{2,1,0:T(8,128)S(1)}, u32[]{:S(2)}, u32[]{:S(2)}) collective-permute-start(f32[2,192,128]{2,1,0:T(8,128)S(1)} %get-tuple-element.13), channel_id=1, source_target_pairs={{0,0},{1,2},{2,1},{3,4},{4,3},{5,6},{6,5},{7,7},{8,8},{9,10},{10,9... | collective-permute-start | bytes 589832 | tf_op jit(solution)/shard_map/ppermute | solution.py:180
  32.1 7.4 %collective-permute-start.6 = (f32[2,128,128]{2,1,0:T(8,128)S(1)}, f32[2,128,128]{2,1,0:T(8,128)S(1)}, u32[]{:S(2)}, u32[]{:S(2)}) collective-permute-start(f32[2,128,128]{2,1,0:T(8,128)S(1)} %get-tuple-element.22), channel_id=1, source_target_pairs={{0,8},{8,16},{16,24},{24,0},{1,9},{9,17},{17,25},{25,1},{2,10},{10... | collective-permute-start | bytes 393224 | tf_op jit(solution)/shard_map/ppermute | solution.py:172
  32.2 8.2 %collective-permute-start.7 = (f32[2,64,128]{2,1,0:T(8,128)S(1)}, f32[2,64,128]{2,1,0:T(8,128)S(1)}, u32[]{:S(2)}, u32[]{:S(2)}) collective-permute-start(f32[2,64,128]{2,1,0:T(8,128)S(1)} %slice_select_fusion), channel_id=1, source_target_pairs={{0,16},{8,24},{16,0},{24,8},{1,17},{9,25},{17,1},{25,9},{2,18},{10... | collective-permute-start | bytes 196616 | tf_op jit(solution)/shard_map/ppermute | solution.py:172
  33.1 7.3 %collective-permute-start.8 = (f32[2,128,128]{2,1,0:T(8,128)S(1)}, f32[2,128,128]{2,1,0:T(8,128)S(1)}, u32[]{:S(2)}, u32[]{:S(2)}) collective-permute-start(f32[2,128,128]{2,1,0:T(8,128)S(1)} %get-tuple-element.23), channel_id=1, source_target_pairs={{0,24},{8,0},{16,8},{24,16},{1,25},{9,1},{17,9},{25,17},{2,26},{10... | collective-permute-start | bytes 393224 | tf_op jit(solution)/shard_map/ppermute | solution.py:172
  40.6 2.0 %collective-permute-start.10 = (f32[2,192,128]{2,1,0:T(8,128)S(1)}, f32[2,192,128]{2,1,0:T(8,128)S(1)}, u32[]{:S(2)}, u32[]{:S(2)}) collective-permute-start(f32[2,192,128]{2,1,0:T(8,128)S(1)} %fusion.mid_ref), channel_id=1, source_target_pairs={{0,1},{1,0},{2,3},{3,2},{4,5},{5,4},{6,7},{7,6},{8,9},{9,8},{10,11... | collective-permute-start | bytes 589832 | tf_op jit(solution)/shard_map/ppermute | solution.py:180
  40.6 7.0 %collective-permute-start.9 = (f32[2,192,128]{2,1,0:T(8,128)S(1)}, f32[2,192,128]{2,1,0:T(8,128)S(1)}, u32[]{:S(2)}, u32[]{:S(2)}) collective-permute-start(f32[2,192,128]{2,1,0:T(8,128)S(1)} %fusion.mid_ref), channel_id=1, source_target_pairs={{0,0},{1,2},{2,1},{3,4},{4,3},{5,6},{6,5},{7,7},{8,8},{9,10},{10,9... | collective-permute-start | bytes 589832 | tf_op jit(solution)/shard_map/ppermute | solution.py:180
  56.4 2.5 %collective-permute-start.11 = (f32[2,192,128]{2,1,0:T(8,128)S(1)}, f32[2,192,128]{2,1,0:T(8,128)S(1)}, u32[]{:S(2)}, u32[]{:S(2)}) collective-permute-start(f32[2,192,128]{2,1,0:T(8,128)S(1)} %get-tuple-element.15), channel_id=1, source_target_pairs={{0,1},{1,0},{2,3},{3,2},{4,5},{5,4},{6,7},{7,6},{8,9},{9,8},{10,11... | collective-permute-start | bytes 589832 | tf_op jit(solution)/shard_map/ppermute | solution.py:180
  57.0 7.0 %collective-permute-start.12 = (f32[2,192,128]{2,1,0:T(8,128)S(1)}, f32[2,192,128]{2,1,0:T(8,128)S(1)}, u32[]{:S(2)}, u32[]{:S(2)}) collective-permute-start(f32[2,192,128]{2,1,0:T(8,128)S(1)} %get-tuple-element.16), channel_id=1, source_target_pairs={{0,0},{1,2},{2,1},{3,4},{4,3},{5,6},{6,5},{7,7},{8,8},{9,10},{10,9... | collective-permute-start | bytes 589832 | tf_op jit(solution)/shard_map/ppermute | solution.py:180
  64.0 5.8 %collective-permute-start.13 = (f32[2,64,128]{2,1,0:T(8,128)S(1)}, f32[2,64,128]{2,1,0:T(8,128)S(1)}, u32[]{:S(2)}, u32[]{:S(2)}) collective-permute-start(f32[2,64,128]{2,1,0:T(8,128)S(1)} %get-tuple-element.20), channel_id=1, source_target_pairs={{0,8},{8,16},{16,24},{24,0},{1,9},{9,17},{17,25},{25,1},{2,10},{10... | collective-permute-start | bytes 196616 | tf_op jit(solution)/shard_map/ppermute | solution.py:172
  65.3 5.3 %collective-permute-start.14 = (f32[2,64,128]{2,1,0:T(8,128)S(1)}, f32[2,64,128]{2,1,0:T(8,128)S(1)}, u32[]{:S(2)}, u32[]{:S(2)}) collective-permute-start(f32[2,64,128]{2,1,0:T(8,128)S(1)} %get-tuple-element.21), channel_id=1, source_target_pairs={{0,24},{8,0},{16,8},{24,16},{1,25},{9,1},{17,9},{25,17},{2,26},{10... | collective-permute-start | bytes 196616 | tf_op jit(solution)/shard_map/ppermute | solution.py:172

commit v2 on v1

--- a/solution.py
+++ b/solution.py
@@ -13,14 +13,22 @@
 GROUP = 6
 
 
-def dft_blocks(length):
-    index = np.arange(length)
-    angle = 2.0 * math.pi / length * (index[:, None] * index[None, :] % length)
-    re, im = np.cos(angle) / math.sqrt(length), -np.sin(angle) / math.sqrt(length)
-    full = np.block([[re, -im], [im, re]])
-    high = full.astype(jnp.bfloat16)
-    low = (full - high.astype(np.float64)).astype(jnp.bfloat16)
-    return np.stack([high, low, high.T, low.T])
+def dft_tables(length):
+    half = length // 2
+    inner = np.arange(half)
+
+    def block(odd):
+        order = 2 * inner + odd
+        angle = 2.0 * math.pi / length * (inner[:, None] * order[None, :] % length)
+        re, im = np.cos(angle) / math.sqrt(length), -np.sin(angle) / math.sqrt(length)
+        return np.block([[im, re], [-re, im]]) if odd else np.block([[re, im], [-im, re]])
+
+    tables = []
+    for whole in (block(0), block(1), block(0).T, block(1).T):
+        high = whole.astype(jnp.bfloat16)
+        low = (whole - high.astype(np.float64)).astype(jnp.bfloat16)
+        tables.append(np.block([[high, low], [high, np.zeros_like(low)]]))
+    return np.stack(tables + [t.T for t in tables])
 
 
 def halves(x):
@@ -55,37 +63,87 @@
         ext[s, 1, 1] = pltpu.roll(right, core, 1)
     acc[...] = jnp.zeros_like(acc)
 
-    def right_mul(blocks, table):
-        x = jnp.concatenate([jnp.concatenate([r, i], axis=1) for r, i in blocks], axis=0)
-        xh, xl = halves(x)
-        th, tl = table_ref[2 * table], table_ref[2 * table + 1]
-        y = mm(xh, th) + (mm(xl, th) + mm(xh, tl))
+    half = length // 2
+    low_lanes = lax.broadcasted_iota(jnp.int32, (length, length), 1) < half
+
+    def swap(x):
+        return pltpu.roll(x, half, 1)
+
+    def row_products(rows, table):
+        high, low = halves(jnp.concatenate(rows, axis=0))
+        y = mm(jnp.concatenate([high, low], axis=1), table_ref[table])
+        y = y[:, :length] + y[:, length:]
+        return [y[q * length : (q + 1) * length] for q in range(len(rows))]
+
+    def column_products(columns, table):
+        high, low = halves(jnp.concatenate(columns, axis=1))
+        x = jnp.concatenate([high, low], axis=0)
+        y = mm(table_ref[table, :length], x) + mm(table_ref[table, length:], x)
+        return [y[:, q * length : (q + 1) * length] for q in range(len(columns))]
+
+    def rows_forward(blocks):
+        evens, odds = [], []
+        for re, im in blocks:
+            x, y = jnp.where(low_lanes, re, im), swap(jnp.where(low_lanes, im, re))
+            evens.append(x + y)
+            odds.append(x - y)
+        evens, odds = row_products(evens, 0), row_products(odds, 1)
         return [
-            (y[q * length : (q + 1) * length, :length], y[q * length : (q + 1) * length, length:])
-            for q in range(len(blocks))
+            (jnp.where(low_lanes, e, o), swap(jnp.where(low_lanes, o, e)))
+            for e, o in zip(evens, odds)
         ]
 
-    def left_mul(blocks, table):
-        x = jnp.concatenate(
-            [
-                jnp.concatenate([r for r, _ in blocks], axis=1),
-                jnp.concatenate([i for _, i in blocks], axis=1),
-            ],
-            axis=0,
-        )
-        xh, xl = halves(x)
-        th, tl = table_ref[2 * table], table_ref[2 * table + 1]
-        y = mm(th, xh) + (mm(th, xl) + mm(tl, xh))
+    def rows_inverse(blocks):
+        evens, odds = [], []
+        for re, im in blocks:
+            turned = swap(im)
+            evens.append(jnp.where(low_lanes, re, turned))
+            odds.append(jnp.where(low_lanes, turned, re))
+        evens, odds = row_products(evens, 2), row_products(odds, 3)
+        out = []
+        for e, o in zip(evens, odds):
+            x, y = e + o, swap(e - o)
+            out.append((jnp.where(low_lanes, x, y), jnp.where(low_lanes, y, x)))
+        return out
+
+    def columns_forward(blocks):
+        evens, odds = [], []
+        for re, im in blocks:
+            evens.append(jnp.concatenate([re[:half] + re[half:], im[:half] + im[half:]], axis=0))
+            odds.append(jnp.concatenate([re[:half] - re[half:], im[half:] - im[:half]], axis=0))
+        evens, odds = column_products(evens, 4), column_products(odds, 5)
         return [
-            (y[:length, q * length : (q + 1) * length], y[length:, q * length : (q + 1) * length])
-            for q in range(len(blocks))
+            (
+                jnp.concatenate([e[:half], o[half:]], axis=0),
+                jnp.concatenate([e[half:], o[:half]], axis=0),
+            )
+            for e, o in zip(evens, odds)
         ]
 
+    def columns_inverse(blocks):
+        evens = [jnp.concatenate([re[:half], im[:half]], axis=0) for re, im in blocks]
+        odds = [jnp.concatenate([im[half:], re[half:]], axis=0) for re, im in blocks]
+        evens, odds = column_products(evens, 6), column_products(odds, 7)
+        return [
+            (
+                jnp.concatenate([e[:half] + o[:half], e[:half] - o[:half]], axis=0),
+                jnp.concatenate([e[half:] - o[half:], e[half:] + o[half:]], axis=0),
+            )
+            for e, o in zip(evens, odds)
+        ]
+
     def fourier(blocks):
-        return left_mul(right_mul(blocks, 1), 0)
+        return columns_forward(rows_forward(blocks))
 
     def inverse(blocks):
-        return left_mul(right_mul(blocks, 0), 1)
+        return rows_inverse(columns_inverse(blocks))
+
+    lanes_of = lax.broadcasted_iota(jnp.int32, (length, length), 1)
+    order = jnp.where(low_lanes, 2 * lanes_of, 2 * lanes_of - (length - 1))
+
+    def even_odd(ref, k):
+        rows_split = [ref[k, pl.ds(odd, half, stride=2), :] for odd in range(2)]
+        return jnp.take_along_axis(jnp.concatenate(rows_split, axis=0), order, axis=1)
 
     def times(a, b):
         return a[0] * b[0] - a[1] * b[1], a[0] * b[1] + a[1] * b[0]
@@ -114,7 +172,7 @@
                 parts.append(pltpu.roll(both, back, 1))
             return tuple(parts)
 
-        prop = (prop_ref[0], prop_ref[1])
+        prop = (even_odd(prop_ref, 0), even_odd(prop_ref, 1))
         probe = (probe_ref[0], probe_ref[1])
         windows = [[window(q, s) for q in range(group)] for s in range(layers)]
         fields = [[probe] * group]
@@ -127,7 +185,7 @@
         back = []
         for q in range(group):
             re, im = far[q]
-            factor = weight[q] * (re * re + im * im - data_ref[slots[q]])
+            factor = weight[q] * (re * re + im * im - even_odd(data_ref, slots[q]))
             back.append((factor * re, factor * im))
         grad = inverse(back)
         for s in reversed(range(layers)):
@@ -186,7 +244,7 @@
     core = transmission.shape[2]
     tall, broad = lax.axis_size("ty"), lax.axis_size("tx")
     row, col = lax.axis_index("ty"), lax.axis_index("tx")
-    table = jnp.asarray(dft_blocks(probe_field.shape[1]))
+    table = jnp.asarray(dft_tables(probe_field.shape[1]))
     prop = jnp.stack([jnp.cos(propagator_phase), jnp.sin(propagator_phase)])
     is_first = col % 2 == 0
     has_far = jnp.where(is_first, col > 0, col < broad - 1)

time: 71.8 us -> 66.7 us (0.929)
  Pallas kernels: 17.4 us -> 12.2 us
  local copies, waits for them, and re-layouts: 1.43 us -> 3.02 us
  waiting for transfers between devices: 31.8 us -> 30.4 us
    pallas_call x2, Pallas kernels: 17.4 us -> 12.2 us  [tile_gradient(): pl.pallas_call(gradient_kernel, out_shape=(strip, strip, strip), in_specs...]
    ppermute x7, waiting for transfers between devices: 12.3 us -> 10.9 us  [around(): lax.ppermute(shard, axis, [(i, (i + by) % count) for i in range(count)])]
    another operation x1, local copies, waits for them, and re-layouts: 0.24 us -> 1.08 us  [on_device(): prop = jnp.stack([jnp.cos(propagator_phase), jnp.sin(propagator_phase)])]
  transfers between devices with their start and end apart: 15 -> 15, of which waited for: 10 -> 9; matrix products, arithmetic and copies ran while one was open for 1% -> 3% of each run, Pallas kernels for 0% -> 0%
where the time goes in v2:
time: 66.7 us; the launch traced here: 66.2 us
  waiting for transfers between devices  30.4 us (46%)
  starting transfers between devices  18.6 us (28%)
  Pallas kernels  12.2 us (18%)
  local copies, waits for them, and re-layouts  3.02 us (5%)
  other arithmetic  1.22 us (2%)
  between operations  0.86 us (1%)
    ppermute x8, waiting for transfers between devices, partners(): return (lax.ppermute(far, axis, outer), lax.ppermute(near, axis, inner))  19.5 us
    pallas_call x2, Pallas kernels, tile_gradient(): pl.pallas_call(gradient_kernel, out_shape=(strip, strip, strip), in_specs...  12.2 us
    ppermute x7, waiting for transfers between devices, around(): lax.ppermute(shard, axis, [(i, (i + by) % count) for i in range(count)])  10.9 us
    ppermute x8, starting transfers between devices, partners(): return (lax.ppermute(far, axis, outer), lax.ppermute(near, axis, inner))  9.56 us
    ppermute x7, starting transfers between devices, around(): lax.ppermute(shard, axis, [(i, (i + by) % count) for i in range(count)])  9.01 us
  transfers between devices with their start and end apart: 15, of which 9 were waited for; matrix products, arithmetic and copies ran while one was open for 3% of the time, Pallas kernels for 0%

profile of v2, /device:TPU:8, one launch (start us, length us, event | category | flops | bytes accessed | tf_op | source)
XLA Modules:
  0.0 66.2 jit_solution(14436081535041014252)
XLA Ops:
  0.0 1.0 %slice_bitcast_fusion.3 = (f32[2,64,64]{2,1,0:T(8,128)S(1)}, f32[2,64,64]{2,1,0:T(8,128)S(1)}) fusion(f32[2,2,64,64]{3,2,1,0:T(8,128)} %param.7), kind=kLoop, calls=%fused_computation.27 | loop fusion | bytes 131072 | tf_op jit(solution)/shard_map/squeeze | solution.py:262
  1.0 0.1 pad_maximum_fusion.3
  1.1 2.5 %collective-permute-start.1 = (f32[2,64,128]{2,1,0:T(8,128)S(1)}, f32[2,64,128]{2,1,0:T(8,128)S(1)}, u32[]{:S(2)}, u32[]{:S(2)}) collective-permute-start(f32[2,64,128]{2,1,0:T(8,128)S(1)} %pad_maximum_fusion.3), channel_id=1, source_target_pairs={{0,24},{8,0},{16,8},{24,16},{1,25},{9,1},{17,9},{25,17},{2,26},{10... | collective-permute-start | bytes 196616 | tf_op jit(solution)/shard_map/ppermute | solution.py:230
  3.6 1.1 %cosine_bitcast_fusion = (f32[1,128,128]{2,1,0:T(8,128)S(1)}, f32[1,128,128]{2,1,0:T(8,128)S(1)}) fusion(f32[128,128]{1,0:T(8,128)} %param.9), kind=kLoop, calls=%fused_computation.25 | loop fusion | bytes 196608 | tf_op jit(solution)/shard_map/stack | solution.py:248
  5.3 0.8 %copy.9 = s32[1,1,6,2]{3,2,1,0:T(8,128)S(1)} copy(s32[1,1,6,2]{2,3,1,0:T(2,128)} %param.10) | data formatting | bytes 96 | tf_op args[3]
  6.1 0.1 reshape.8.offsets
  6.2 2.5 %collective-permute-done = f32[2,64,128]{2,1,0:T(8,128)S(1)} collective-permute-done((f32[2,64,128]{2,1,0:T(8,128)S(1)}, f32[2,64,128]{2,1,0:T(8,128)S(1)}, u32[]{:S(2)}, u32[]{:S(2)}) %collective-permute-start) | collective-permute-done | bytes 65568 | tf_op jit(solution)/shard_map/ppermute | solution.py:230
  8.8 0.1 pad_maximum_fusion.mid_ref
  8.9 2.4 %collective-permute-start.2 = (f32[2,192,128]{2,1,0:T(8,128)S(1)}, f32[2,192,128]{2,1,0:T(8,128)S(1)}, u32[]{:S(2)}, u32[]{:S(2)}) collective-permute-start(f32[2,192,128]{2,1,0:T(8,128)S(1)} %pad_maximum_fusion.mid_ref), channel_id=1, source_target_pairs={{0,0},{1,2},{2,1},{3,4},{4,3},{5,6},{6,5},{7,7},{8,8},{9,10},{10,9... | collective-permute-start | bytes 589832 | tf_op jit(solution)/shard_map/ppermute | solution.py:238
  11.5 4.4 %collective-permute-done.2.far_ref = f32[2,192,128]{2,1,0:T(8,128)S(1)} collective-permute-done((f32[2,192,128]{2,1,0:T(8,128)S(1)}, f32[2,192,128]{2,1,0:T(8,128)S(1)}, u32[]{:S(2)}, u32[]{:S(2)}) %collective-permute-start.2) | collective-permute-done | bytes 196640 | tf_op jit(solution)/shard_map/ppermute | solution.py:238
  15.9 6.1 %tile_gradient.2 = (f32[2,192,128]{2,1,0:T(8,128)S(1)}, f32[2,192,128]{2,1,0:T(8,128)S(1)}, f32[2,192,128]{2,1,0:T(8,128)S(1)}) custom-call(s32[12]{0:T(128)S(1)} %reshape.8.offsets, s32[1]{0:T(128)} %bitcast.16.count, s32[2]{0:T(128)S(1)} %add_convert_fusion.place, f32[2,192,128]{2,1,0:T(8,128)S(1)} %collective-permute-done.2.far_ref, ...), custom_call_target="tpu_custom_call" | custom-call | tf_op jit(solution)/shard_map/tile_gradient/pallas_call | solution.py:217
  22.0 0.6 collective-permute-start.4
  22.6 2.0 %collective-permute-start.5 = (f32[2,192,128]{2,1,0:T(8,128)S(1)}, f32[2,192,128]{2,1,0:T(8,128)S(1)}, u32[]{:S(2)}, u32[]{:S(2)}) collective-permute-start(f32[2,192,128]{2,1,0:T(8,128)S(1)} %get-tuple-element.13), channel_id=1, source_target_pairs={{0,0},{1,2},{2,1},{3,4},{4,3},{5,6},{6,5},{7,7},{8,8},{9,10},{10,9... | collective-permute-start | bytes 589832 | tf_op jit(solution)/shard_map/ppermute | solution.py:238
  24.6 5.0 %collective-permute-done.5 = f32[2,192,128]{2,1,0:T(8,128)S(1)} collective-permute-done((f32[2,192,128]{2,1,0:T(8,128)S(1)}, f32[2,192,128]{2,1,0:T(8,128)S(1)}, u32[]{:S(2)}, u32[]{:S(2)}) %collective-permute-start.5) | collective-permute-done | bytes 196640 | tf_op jit(solution)/shard_map/ppermute | solution.py:238
  29.6 0.1 collective-permute-start.6
  29.8 0.9 %collective-permute-start.7 = (f32[2,64,128]{2,1,0:T(8,128)S(1)}, f32[2,64,128]{2,1,0:T(8,128)S(1)}, u32[]{:S(2)}, u32[]{:S(2)}) collective-permute-start(f32[2,64,128]{2,1,0:T(8,128)S(1)} %slice_select_fusion), channel_id=1, source_target_pairs={{0,16},{8,24},{16,0},{24,8},{1,17},{9,25},{17,1},{25,9},{2,18},{10... | collective-permute-start | bytes 196616 | tf_op jit(solution)/shard_map/ppermute | solution.py:230
  30.7 2.4 %collective-permute-start.8 = (f32[2,128,128]{2,1,0:T(8,128)S(1)}, f32[2,128,128]{2,1,0:T(8,128)S(1)}, u32[]{:S(2)}, u32[]{:S(2)}) collective-permute-start(f32[2,128,128]{2,1,0:T(8,128)S(1)} %get-tuple-element.23), channel_id=1, source_target_pairs={{0,24},{8,0},{16,8},{24,16},{1,25},{9,1},{17,9},{25,17},{2,26},{10... | collective-permute-start | bytes 393224 | tf_op jit(solution)/shard_map/ppermute | solution.py:230
  33.2 3.8 %collective-permute-done.6 = f32[2,128,128]{2,1,0:T(8,128)S(1)} collective-permute-done((f32[2,128,128]{2,1,0:T(8,128)S(1)}, f32[2,128,128]{2,1,0:T(8,128)S(1)}, u32[]{:S(2)}, u32[]{:S(2)}) %collective-permute-start.6) | collective-permute-done | bytes 131104 | tf_op jit(solution)/shard_map/ppermute | solution.py:230
  37.0 1.0 %collective-permute-done.8 = f32[2,128,128]{2,1,0:T(8,128)S(1)} collective-permute-done((f32[2,128,128]{2,1,0:T(8,128)S(1)}, f32[2,128,128]{2,1,0:T(8,128)S(1)}, u32[]{:S(2)}, u32[]{:S(2)}) %collective-permute-start.8) | collective-permute-done | bytes 131104 | tf_op jit(solution)/shard_map/ppermute | solution.py:230
  38.1 0.1 fusion.mid_ref
  38.2 1.9 %collective-permute-start.9 = (f32[2,192,128]{2,1,0:T(8,128)S(1)}, f32[2,192,128]{2,1,0:T(8,128)S(1)}, u32[]{:S(2)}, u32[]{:S(2)}) collective-permute-start(f32[2,192,128]{2,1,0:T(8,128)S(1)} %fusion.mid_ref), channel_id=1, source_target_pairs={{0,0},{1,2},{2,1},{3,4},{4,3},{5,6},{6,5},{7,7},{8,8},{9,10},{10,9... | collective-permute-start | bytes 589832 | tf_op jit(solution)/shard_map/ppermute | solution.py:238
  40.2 5.0 %collective-permute-done.9.far_ref = f32[2,192,128]{2,1,0:T(8,128)S(1)} collective-permute-done((f32[2,192,128]{2,1,0:T(8,128)S(1)}, f32[2,192,128]{2,1,0:T(8,128)S(1)}, u32[]{:S(2)}, u32[]{:S(2)}) %collective-permute-start.9) | collective-permute-done | bytes 196640 | tf_op jit(solution)/shard_map/ppermute | solution.py:238
  45.2 6.1 %tile_gradient.3 = (f32[2,192,128]{2,1,0:T(8,128)S(1)}, f32[2,192,128]{2,1,0:T(8,128)S(1)}, f32[2,192,128]{2,1,0:T(8,128)S(1)}) custom-call(s32[12]{0:T(128)S(1)} %reshape.8.offsets, s32[1]{0:T(128)} %bitcast.17.count, s32[2]{0:T(128)S(1)} %add_convert_fusion.place, f32[2,192,128]{2,1,0:T(8,128)S(1)} %collective-permute-done.9.far_ref, ...), custom_call_target="tpu_custom_call" | custom-call | tf_op jit(solution)/shard_map/tile_gradient/pallas_call | solution.py:217
  51.3 0.6 collective-permute-start.11
  51.9 1.9 %collective-permute-start.12 = (f32[2,192,128]{2,1,0:T(8,128)S(1)}, f32[2,192,128]{2,1,0:T(8,128)S(1)}, u32[]{:S(2)}, u32[]{:S(2)}) collective-permute-start(f32[2,192,128]{2,1,0:T(8,128)S(1)} %get-tuple-element.16), channel_id=1, source_target_pairs={{0,0},{1,2},{2,1},{3,4},{4,3},{5,6},{6,5},{7,7},{8,8},{9,10},{10,9... | collective-permute-start | bytes 589832 | tf_op jit(solution)/shard_map/ppermute | solution.py:238
  53.8 5.0 %collective-permute-done.12 = f32[2,192,128]{2,1,0:T(8,128)S(1)} collective-permute-done((f32[2,192,128]{2,1,0:T(8,128)S(1)}, f32[2,192,128]{2,1,0:T(8,128)S(1)}, u32[]{:S(2)}, u32[]{:S(2)}) %collective-permute-start.12) | collective-permute-done | bytes 196640 | tf_op jit(solution)/shard_map/ppermute | solution.py:238
  58.9 1.2 %collective-permute-start.13 = (f32[2,64,128]{2,1,0:T(8,128)S(1)}, f32[2,64,128]{2,1,0:T(8,128)S(1)}, u32[]{:S(2)}, u32[]{:S(2)}) collective-permute-start(f32[2,64,128]{2,1,0:T(8,128)S(1)} %get-tuple-element.20), channel_id=1, source_target_pairs={{0,8},{8,16},{16,24},{24,0},{1,9},{9,17},{17,25},{25,1},{2,10},{10... | collective-permute-start | bytes 196616 | tf_op jit(solution)/shard_map/ppermute | solution.py:230
  60.1 1.8 %collective-permute-start.14 = (f32[2,64,128]{2,1,0:T(8,128)S(1)}, f32[2,64,128]{2,1,0:T(8,128)S(1)}, u32[]{:S(2)}, u32[]{:S(2)}) collective-permute-start(f32[2,64,128]{2,1,0:T(8,128)S(1)} %get-tuple-element.21), channel_id=1, source_target_pairs={{0,24},{8,0},{16,8},{24,16},{1,25},{9,1},{17,9},{25,17},{2,26},{10... | collective-permute-start | bytes 196616 | tf_op jit(solution)/shard_map/ppermute | solution.py:230
  61.9 2.8 %collective-permute-done.13 = f32[2,64,128]{2,1,0:T(8,128)S(1)} collective-permute-done((f32[2,64,128]{2,1,0:T(8,128)S(1)}, f32[2,64,128]{2,1,0:T(8,128)S(1)}, u32[]{:S(2)}, u32[]{:S(2)}) %collective-permute-start.13) | collective-permute-done | bytes 65568 | tf_op jit(solution)/shard_map/ppermute | solution.py:230
  64.7 0.7 %collective-permute-done.14 = f32[2,64,128]{2,1,0:T(8,128)S(1)} collective-permute-done((f32[2,64,128]{2,1,0:T(8,128)S(1)}, f32[2,64,128]{2,1,0:T(8,128)S(1)}, u32[]{:S(2)}, u32[]{:S(2)}) %collective-permute-start.14) | collective-permute-done | bytes 65568 | tf_op jit(solution)/shard_map/ppermute | solution.py:230
  65.4 0.1 slice_bitcast_fusion.1
  65.5 0.7 %pad_maximum_fusion.2 = f32[2,2,64,64]{3,2,1,0:T(8,128)} fusion(f32[1,2,64,64]{3,2,1,0:T(8,128)S(1)} %get-tuple-element.27, f32[1,2,64,64]{3,2,1,0:T(8,128)S(1)} %get-tuple-element.26), kind=kLoop, calls=%fused_computation.6 | loop fusion | flops 16384 | bytes 131072 | tf_op jit(solution)/shard_map/stack | solution.py:286
  (28 shorter events, 0.5 us)
Async XLA Ops:
  0.0 15.9 %copy-start = (bf16[8,256,256]{2,1,0:T(8,128)(2,1)S(1)}, bf16[8,256,256]{2,1,0:T(8,128)(2,1)}, u32[]{:S(2)}) copy-start(bf16[8,256,256]{2,1,0:T(8,128)(2,1)} %constant.33.clone.table_ref) | copy-start | bytes 3145732
  1.1 5.1 %collective-permute-start.1 = (f32[2,64,128]{2,1,0:T(8,128)S(1)}, f32[2,64,128]{2,1,0:T(8,128)S(1)}, u32[]{:S(2)}, u32[]{:S(2)}) collective-permute-start(f32[2,64,128]{2,1,0:T(8,128)S(1)} %pad_maximum_fusion.3), channel_id=1, source_target_pairs={{0,24},{8,0},{16,8},{24,16},{1,25},{9,1},{17,9},{25,17},{2,26},{10... | collective-permute-start | bytes 196616 | tf_op jit(solution)/shard_map/ppermute | solution.py:230
  3.6 5.2 %collective-permute-start = (f32[2,64,128]{2,1,0:T(8,128)S(1)}, f32[2,64,128]{2,1,0:T(8,128)S(1)}, u32[]{:S(2)}, u32[]{:S(2)}) collective-permute-start(f32[2,64,128]{2,1,0:T(8,128)S(1)} %pad_maximum_fusion.3), channel_id=1, source_target_pairs={{0,8},{8,16},{16,24},{24,0},{1,9},{9,17},{17,25},{25,1},{2,10},{10... | collective-permute-start | bytes 196616 | tf_op jit(solution)/shard_map/ppermute | solution.py:230
  8.7 7.2 %copy-start.1 = (f32[1,1,6,128,128]{4,3,2,1,0:T(8,128)S(1)}, f32[1,1,6,128,128]{4,3,2,1,0:T(8,128)}, u32[]{:S(2)}) copy-start(f32[1,1,6,128,128]{4,3,2,1,0:T(8,128)} %param.12) | copy-start | bytes 1179652
  8.8 2.6 %collective-permute-start.3 = (f32[2,192,128]{2,1,0:T(8,128)S(1)}, f32[2,192,128]{2,1,0:T(8,128)S(1)}, u32[]{:S(2)}, u32[]{:S(2)}) collective-permute-start(f32[2,192,128]{2,1,0:T(8,128)S(1)} %pad_maximum_fusion.mid_ref), channel_id=1, source_target_pairs={{0,1},{1,0},{2,3},{3,2},{4,5},{5,4},{6,7},{7,6},{8,9},{9,8},{10,11... | collective-permute-start | bytes 589832 | tf_op jit(solution)/shard_map/ppermute | solution.py:238
  8.9 7.0 %collective-permute-start.2 = (f32[2,192,128]{2,1,0:T(8,128)S(1)}, f32[2,192,128]{2,1,0:T(8,128)S(1)}, u32[]{:S(2)}, u32[]{:S(2)}) collective-permute-start(f32[2,192,128]{2,1,0:T(8,128)S(1)} %pad_maximum_fusion.mid_ref), channel_id=1, source_target_pairs={{0,0},{1,2},{2,1},{3,4},{4,3},{5,6},{6,5},{7,7},{8,8},{9,10},{10,9... | collective-permute-start | bytes 589832 | tf_op jit(solution)/shard_map/ppermute | solution.py:238
  11.5 4.5 %copy-start.2 = (f32[2,128,128]{2,1,0:T(8,128)S(1)}, f32[2,128,128]{2,1,0:T(8,128)}, u32[]{:S(2)}) copy-start(f32[2,128,128]{2,1,0:T(8,128)} %probe_ref.3) | copy-start | bytes 393220
  22.0 2.6 %collective-permute-start.4 = (f32[2,192,128]{2,1,0:T(8,128)S(1)}, f32[2,192,128]{2,1,0:T(8,128)S(1)}, u32[]{:S(2)}, u32[]{:S(2)}) collective-permute-start(f32[2,192,128]{2,1,0:T(8,128)S(1)} %get-tuple-element.12), channel_id=1, source_target_pairs={{0,1},{1,0},{2,3},{3,2},{4,5},{5,4},{6,7},{7,6},{8,9},{9,8},{10,11... | collective-permute-start | bytes 589832 | tf_op jit(solution)/shard_map/ppermute | solution.py:238
  22.6 7.0 %collective-permute-start.5 = (f32[2,192,128]{2,1,0:T(8,128)S(1)}, f32[2,192,128]{2,1,0:T(8,128)S(1)}, u32[]{:S(2)}, u32[]{:S(2)}) collective-permute-start(f32[2,192,128]{2,1,0:T(8,128)S(1)} %get-tuple-element.13), channel_id=1, source_target_pairs={{0,0},{1,2},{2,1},{3,4},{4,3},{5,6},{6,5},{7,7},{8,8},{9,10},{10,9... | collective-permute-start | bytes 589832 | tf_op jit(solution)/shard_map/ppermute | solution.py:238
  29.6 7.4 %collective-permute-start.6 = (f32[2,128,128]{2,1,0:T(8,128)S(1)}, f32[2,128,128]{2,1,0:T(8,128)S(1)}, u32[]{:S(2)}, u32[]{:S(2)}) collective-permute-start(f32[2,128,128]{2,1,0:T(8,128)S(1)} %get-tuple-element.22), channel_id=1, source_target_pairs={{0,8},{8,16},{16,24},{24,0},{1,9},{9,17},{17,25},{25,1},{2,10},{10... | collective-permute-start | bytes 393224 | tf_op jit(solution)/shard_map/ppermute | solution.py:230
  29.8 8.2 %collective-permute-start.7 = (f32[2,64,128]{2,1,0:T(8,128)S(1)}, f32[2,64,128]{2,1,0:T(8,128)S(1)}, u32[]{:S(2)}, u32[]{:S(2)}) collective-permute-start(f32[2,64,128]{2,1,0:T(8,128)S(1)} %slice_select_fusion), channel_id=1, source_target_pairs={{0,16},{8,24},{16,0},{24,8},{1,17},{9,25},{17,1},{25,9},{2,18},{10... | collective-permute-start | bytes 196616 | tf_op jit(solution)/shard_map/ppermute | solution.py:230
  30.7 7.2 %collective-permute-start.8 = (f32[2,128,128]{2,1,0:T(8,128)S(1)}, f32[2,128,128]{2,1,0:T(8,128)S(1)}, u32[]{:S(2)}, u32[]{:S(2)}) collective-permute-start(f32[2,128,128]{2,1,0:T(8,128)S(1)} %get-tuple-element.23), channel_id=1, source_target_pairs={{0,24},{8,0},{16,8},{24,16},{1,25},{9,1},{17,9},{25,17},{2,26},{10... | collective-permute-start | bytes 393224 | tf_op jit(solution)/shard_map/ppermute | solution.py:230
  38.2 2.0 %collective-permute-start.10 = (f32[2,192,128]{2,1,0:T(8,128)S(1)}, f32[2,192,128]{2,1,0:T(8,128)S(1)}, u32[]{:S(2)}, u32[]{:S(2)}) collective-permute-start(f32[2,192,128]{2,1,0:T(8,128)S(1)} %fusion.mid_ref), channel_id=1, source_target_pairs={{0,1},{1,0},{2,3},{3,2},{4,5},{5,4},{6,7},{7,6},{8,9},{9,8},{10,11... | collective-permute-start | bytes 589832 | tf_op jit(solution)/shard_map/ppermute | solution.py:238
  38.2 7.0 %collective-permute-start.9 = (f32[2,192,128]{2,1,0:T(8,128)S(1)}, f32[2,192,128]{2,1,0:T(8,128)S(1)}, u32[]{:S(2)}, u32[]{:S(2)}) collective-permute-start(f32[2,192,128]{2,1,0:T(8,128)S(1)} %fusion.mid_ref), channel_id=1, source_target_pairs={{0,0},{1,2},{2,1},{3,4},{4,3},{5,6},{6,5},{7,7},{8,8},{9,10},{10,9... | collective-permute-start | bytes 589832 | tf_op jit(solution)/shard_map/ppermute | solution.py:238
  51.3 2.5 %collective-permute-start.11 = (f32[2,192,128]{2,1,0:T(8,128)S(1)}, f32[2,192,128]{2,1,0:T(8,128)S(1)}, u32[]{:S(2)}, u32[]{:S(2)}) collective-permute-start(f32[2,192,128]{2,1,0:T(8,128)S(1)} %get-tuple-element.15), channel_id=1, source_target_pairs={{0,1},{1,0},{2,3},{3,2},{4,5},{5,4},{6,7},{7,6},{8,9},{9,8},{10,11... | collective-permute-start | bytes 589832 | tf_op jit(solution)/shard_map/ppermute | solution.py:238
  51.9 7.0 %collective-permute-start.12 = (f32[2,192,128]{2,1,0:T(8,128)S(1)}, f32[2,192,128]{2,1,0:T(8,128)S(1)}, u32[]{:S(2)}, u32[]{:S(2)}) collective-permute-start(f32[2,192,128]{2,1,0:T(8,128)S(1)} %get-tuple-element.16), channel_id=1, source_target_pairs={{0,0},{1,2},{2,1},{3,4},{4,3},{5,6},{6,5},{7,7},{8,8},{9,10},{10,9... | collective-permute-start | bytes 589832 | tf_op jit(solution)/shard_map/ppermute | solution.py:238
  58.9 5.8 %collective-permute-start.13 = (f32[2,64,128]{2,1,0:T(8,128)S(1)}, f32[2,64,128]{2,1,0:T(8,128)S(1)}, u32[]{:S(2)}, u32[]{:S(2)}) collective-permute-start(f32[2,64,128]{2,1,0:T(8,128)S(1)} %get-tuple-element.20), channel_id=1, source_target_pairs={{0,8},{8,16},{16,24},{24,0},{1,9},{9,17},{17,25},{25,1},{2,10},{10... | collective-permute-start | bytes 196616 | tf_op jit(solution)/shard_map/ppermute | solution.py:230
  60.1 5.3 %collective-permute-start.14 = (f32[2,64,128]{2,1,0:T(8,128)S(1)}, f32[2,64,128]{2,1,0:T(8,128)S(1)}, u32[]{:S(2)}, u32[]{:S(2)}) collective-permute-start(f32[2,64,128]{2,1,0:T(8,128)S(1)} %get-tuple-element.21), channel_id=1, source_target_pairs={{0,24},{8,0},{16,8},{24,16},{1,25},{9,1},{17,9},{25,17},{2,26},{10... | collective-permute-start | bytes 196616 | tf_op jit(solution)/shard_map/ppermute | solution.py:230

commit v3 on v2

--- a/solution.py
+++ b/solution.py
@@ -78,7 +78,8 @@
     def column_products(columns, table):
         high, low = halves(jnp.concatenate(columns, axis=1))
         x = jnp.concatenate([high, low], axis=0)
-        y = mm(table_ref[table, :length], x) + mm(table_ref[table, length:], x)
+        y = mm(table_ref[table], x)
+        y = y[:length] + y[length:]
         return [y[:, q * length : (q + 1) * length] for q in range(len(columns))]
 
     def rows_forward(blocks):
@@ -225,17 +226,54 @@
     )(offsets, count, place, far, mid, near, probe, prop, data, table)
 
 
-def around(shard, axis, by):
-    count = lax.axis_size(axis)
-    return lax.ppermute(shard, axis, [(i, (i + by) % count) for i in range(count)])
-
-
-def partners(far, near, axis):
-    count = lax.axis_size(axis)
-    ends = count - 1
-    outer = [(i, min(max(i + 1 if i % 2 else i - 1, 0), ends)) for i in range(count)]
-    inner = [(i, i ^ 1) for i in range(count)]
-    return lax.ppermute(far, axis, outer), lax.ppermute(near, axis, inner)
+def exchange(shard, partner):
+    tall, broad = lax.axis_size("ty"), lax.axis_size("tx")
+    pairs = []
+    for row in range(tall):
+        for col in range(broad):
+            to_row, to_col = partner(row, col)
+            pairs.append((row * broad + col, to_row % tall * broad + to_col % broad))
+    return lax.ppermute(shard, ("ty", "tx"), pairs)
+
+
+def same_chip(row, col):
+    return row, col ^ 1
+
+
+def other_chip(rows):
+    def partner(row, col):
+        broad = lax.axis_size("tx")
+        to_col = col + 1 if col % 2 else col - 1
+        inside = 0 <= to_col < broad
+        if inside:
+            return rows(row), to_col
+        return (row ^ 1 if rows is same_row else rows(row)), col
+
+    return partner
+
+
+def same_row(row):
+    return row
+
+
+def row_pair(row):
+    return row ^ 1
+
+
+def row_cross(row):
+    return row + 1 if row % 2 else row - 1
+
+
+def two_pair(row):
+    return row ^ 2
+
+
+def two_cross(row):
+    return row - 2 if row % 4 < 2 else row + 2
+
+
+def within_column(rows):
+    return lambda row, col: (rows(row), col)
 
 
 def on_device(
@@ -243,6 +281,8 @@
 ):
     core = transmission.shape[2]
     tall, broad = lax.axis_size("ty"), lax.axis_size("tx")
+    if tall % 2 or broad % 2 or (tall > 2 and tall % 4):
+        raise ValueError("unsupported mesh")
     row, col = lax.axis_index("ty"), lax.axis_index("tx")
     table = jnp.asarray(dft_tables(probe_field.shape[1]))
     prop = jnp.stack([jnp.cos(propagator_phase), jnp.sin(propagator_phase)])
@@ -250,39 +290,72 @@
     has_far = jnp.where(is_first, col > 0, col < broad - 1)
     place = jnp.stack([is_first, has_far]).astype(jnp.int32)
     has_above, has_below = row > 0, row < tall - 1
+    odd = row % 2 == 1
+
+    def masked(keep, x):
+        return jnp.where(keep, x, 0.0)
+
+    def sorted_rows(pair, cross):
+        above = masked(has_above, jnp.where(odd, pair, cross))
+        below = masked(has_below, jnp.where(odd, cross, pair))
+        return above, below
 
     def gradient(strip, far, near):
-        gfar, gmid, gnear = tile_gradient(
+        return tile_gradient(
             scan_offsets.reshape(-1), position_counts.reshape(-1), place, far, strip, near,
             probe_field, prop, intensities[0, 0], table,
         )
-        far, near = partners(gfar, gnear, "tx")
-        return gmid + near + jnp.where(has_far, far, 0.0)
+
+    def column_exchange(far, near):
+        return exchange(far, other_chip(same_row)), exchange(near, same_chip)
 
     own = jnp.concatenate([transmission[0], transmission[1]], axis=-1)
-    above = jnp.where(has_above, around(own, "ty", 1), 0.0)
-    below = jnp.where(has_below, around(own, "ty", -1), 0.0)
+    above, below = sorted_rows(
+        exchange(own, within_column(row_pair)), exchange(own, within_column(row_cross))
+    )
     strip = jnp.concatenate([above, own, below], axis=1)
+    near = exchange(strip, same_chip)
+    far_above, far_below = sorted_rows(
+        exchange(own, other_chip(row_pair)), exchange(own, other_chip(row_cross))
+    )
+    far = jnp.concatenate([far_above, exchange(own, other_chip(same_row)), far_below], axis=1)
+
     for sweep in range(ITERS):
-        total = gradient(strip, *partners(strip, strip, "tx"))
-        top, mid, bottom = total[:, :core], total[:, core : 2 * core], total[:, 2 * core :]
+        gfar, gmid, gnear = gradient(strip, far, near)
         if sweep < ITERS - 1:
-            down = jnp.where(has_above, around(total[:, core:], "ty", 1), 0.0)
-            up = jnp.where(has_below, around(total[:, : 2 * core], "ty", -1), 0.0)
-            if tall == 4:
-                mixed = around(jnp.where(row < 2, bottom, top), "ty", 2)
-                down2, up2 = jnp.where(row < 2, 0.0, mixed), jnp.where(row < 2, mixed, 0.0)
-            else:
-                down2 = jnp.where(row > 1, around(bottom, "ty", 2), 0.0)
-                up2 = jnp.where(row < tall - 2, around(top, "ty", -2), 0.0)
-            above = jnp.where(has_above, top + down[:, :core] + down2, 0.0)
-            inside = mid + down[:, core:] + up[:, :core]
-            below = jnp.where(has_below, bottom + up[:, core:] + up2, 0.0)
-            strip = strip - STEP * jnp.concatenate([above, inside, below], axis=1)
+            far, near = column_exchange(gfar, gnear)
+            total = gmid + near + masked(has_far, far)
+            top, mid, bottom = total[:, :core], total[:, core : 2 * core], total[:, 2 * core :]
+            upper, lower = total[:, : 2 * core], total[:, core:]
+            pair = exchange(jnp.where(odd, upper, lower), within_column(row_pair))
+            cross = exchange(jnp.where(odd, lower, upper), within_column(row_cross))
+            down, up = sorted_rows(pair, cross)
+            above, inside, below = top + down[:, :core], mid + down[:, core:] + up[:, :core], bottom + up[:, core:]
+            if tall > 2:
+                early = row % 4 < 2
+                got = exchange(jnp.where(early, bottom, top), within_column(two_pair))
+                above, below = above + masked(~early, got), below + masked(early, got)
+            if tall > 4:
+                got = exchange(jnp.where(early, top, bottom), within_column(two_cross))
+                above = above + masked(early & (row > 1), got)
+                below = below + masked(~early & (row < tall - 2), got)
+            step = [masked(has_above, above), inside, masked(has_below, below)]
+            strip = strip - STEP * jnp.concatenate(step, axis=1)
+            far, near = column_exchange(strip, strip)
         else:
-            down = jnp.where(has_above, around(bottom, "ty", 1), 0.0)
-            up = jnp.where(has_below, around(top, "ty", -1), 0.0)
-            own = strip[:, core : 2 * core] - STEP * (mid + down + up)
+            total = gmid + exchange(gnear, same_chip)
+            grad = total[:, core : 2 * core]
+            grad += masked(has_far, exchange(gfar[:, core : 2 * core], other_chip(same_row)))
+            for part, keep, reach in (
+                (gfar, has_far, other_chip),
+                (total, True, within_column),
+            ):
+                top, bottom = part[:, :core], part[:, 2 * core :]
+                pair = exchange(jnp.where(odd, top, bottom), reach(row_pair))
+                cross = exchange(jnp.where(odd, bottom, top), reach(row_cross))
+                down, up = sorted_rows(pair, cross)
+                grad += masked(keep, down + up)
+            own = strip[:, core : 2 * core] - STEP * grad
     return jnp.stack([own[..., :core], own[..., core:]])
 
 

time: 66.7 us -> 60.1 us (0.901)
  the two profiles are of different devices: /device:TPU:8 before, /device:TPU:0 now
where the time goes in v3:
time: 60.1 us; the launch traced here: 60 us
  waiting for transfers between devices  24.7 us (41%)
  starting transfers between devices  20.1 us (33%)
  Pallas kernels  11.6 us (19%)
  local copies, waits for them, and re-layouts  1.41 us (2%)
  other arithmetic  1.29 us (2%)
  between operations  0.83 us (1%)
    ppermute x19, waiting for transfers between devices, exchange(): return lax.ppermute(shard, ('ty', 'tx'), pairs)  24.7 us
    ppermute x19, starting transfers between devices, exchange(): return lax.ppermute(shard, ('ty', 'tx'), pairs)  20.1 us
    pallas_call x2, Pallas kernels, tile_gradient(): pl.pallas_call(gradient_kernel, out_shape=(strip, strip, strip), in_specs...  11.6 us
  transfers between devices with their start and end apart: 19, of which 13 were waited for; matrix products, arithmetic and copies ran while one was open for 1% of the time, Pallas kernels for 0%

profile of v3, /device:TPU:0, one launch (start us, length us, event | category | flops | bytes accessed | tf_op | source)
XLA Modules:
  0.0 60.0 jit_solution(10056040545833425315)
XLA Ops:
  0.0 0.9 %slice_bitcast_fusion.3 = (f32[2,64,64]{2,1,0:T(8,128)S(1)}, f32[2,64,64]{2,1,0:T(8,128)S(1)}) fusion(f32[2,2,64,64]{3,2,1,0:T(8,128)} %param.7), kind=kLoop, calls=%fused_computation.34 | loop fusion | bytes 131072 | tf_op jit(solution)/shard_map/squeeze | solution.py:312
  1.0 4.0 %collective-permute-start.3 = (f32[2,64,128]{2,1,0:T(8,128)S(1)}, f32[2,64,128]{2,1,0:T(8,128)S(1)}, u32[]{:S(2)}, u32[]{:S(2)}) collective-permute-start(f32[2,64,128]{2,1,0:T(8,128)S(1)} %pad_maximum_fusion.4), channel_id=1, source_target_pairs={{0,24},{1,26},{2,25},{3,28},{4,27},{5,30},{6,29},{7,31},{8,16},{9,... | collective-permute-start | bytes 196616 | tf_op jit(solution)/shard_map/ppermute | solution.py:236
  5.0 0.5 collective-permute-start.2
  5.5 1.5 %collective-permute-start.4 = (f32[2,64,128]{2,1,0:T(8,128)S(1)}, f32[2,64,128]{2,1,0:T(8,128)S(1)}, u32[]{:S(2)}, u32[]{:S(2)}) collective-permute-start(f32[2,64,128]{2,1,0:T(8,128)S(1)} %pad_maximum_fusion.4), channel_id=1, source_target_pairs={{0,8},{1,2},{2,1},{3,4},{4,3},{5,6},{6,5},{7,15},{8,0},{9,10},{10,... | collective-permute-start | bytes 196616 | tf_op jit(solution)/shard_map/ppermute | solution.py:236
  7.1 1.9 %collective-permute-start = (f32[2,64,128]{2,1,0:T(8,128)S(1)}, f32[2,64,128]{2,1,0:T(8,128)S(1)}, u32[]{:S(2)}, u32[]{:S(2)}) collective-permute-start(f32[2,64,128]{2,1,0:T(8,128)S(1)} %pad_maximum_fusion.4), channel_id=1, source_target_pairs={{0,8},{1,9},{2,10},{3,11},{4,12},{5,13},{6,14},{7,15},{8,0},{9,1},... | collective-permute-start | bytes 196616 | tf_op jit(solution)/shard_map/ppermute | solution.py:236
  9.8 0.2 cosine_bitcast_fusion
  10.2 2.7 %collective-permute-done.1 = f32[2,64,128]{2,1,0:T(8,128)S(1)} collective-permute-done((f32[2,64,128]{2,1,0:T(8,128)S(1)}, f32[2,64,128]{2,1,0:T(8,128)S(1)}, u32[]{:S(2)}, u32[]{:S(2)}) %collective-permute-start.1) | collective-permute-done | bytes 65568 | tf_op jit(solution)/shard_map/ppermute | solution.py:236
  12.9 0.8 %collective-permute-done = f32[2,64,128]{2,1,0:T(8,128)S(1)} collective-permute-done((f32[2,64,128]{2,1,0:T(8,128)S(1)}, f32[2,64,128]{2,1,0:T(8,128)S(1)}, u32[]{:S(2)}, u32[]{:S(2)}) %collective-permute-start) | collective-permute-done | bytes 65568 | tf_op jit(solution)/shard_map/ppermute | solution.py:236
  14.1 1.3 %collective-permute-done.5.near_ref = f32[2,192,128]{2,1,0:T(8,128)S(1)} collective-permute-done((f32[2,192,128]{2,1,0:T(8,128)S(1)}, f32[2,192,128]{2,1,0:T(8,128)S(1)}, u32[]{:S(2)}, u32[]{:S(2)}) %collective-permute-start.5) | collective-permute-done | bytes 196640 | tf_op jit(solution)/shard_map/ppermute | solution.py:236
  15.3 5.8 %tile_gradient.2 = (f32[2,192,128]{2,1,0:T(8,128)S(1)}, f32[2,192,128]{2,1,0:T(8,128)S(1)}, f32[2,192,128]{2,1,0:T(8,128)S(1)}) custom-call(s32[12]{0:T(128)S(1)} %reshape.8.offsets, s32[1]{0:T(128)} %bitcast.16.count, s32[2]{0:T(128)S(1)} %add_convert_fusion.place, f32[2,192,128]{2,1,0:T(8,128)S(1)} %pad_maximum_fusion.1.far_ref, ...), custom_call_target="tpu_custom_call" | custom-call | tf_op jit(solution)/shard_map/tile_gradient/pallas_call | solution.py:218
  21.2 0.2 collective-permute-start.6
  21.4 1.2 %collective-permute-start.7 = (f32[2,192,128]{2,1,0:T(8,128)S(1)}, f32[2,192,128]{2,1,0:T(8,128)S(1)}, u32[]{:S(2)}, u32[]{:S(2)}) collective-permute-start(f32[2,192,128]{2,1,0:T(8,128)S(1)} %get-tuple-element.13), channel_id=1, source_target_pairs={{0,8},{1,2},{2,1},{3,4},{4,3},{5,6},{6,5},{7,15},{8,0},{9,10},{10,... | collective-permute-start | bytes 589832 | tf_op jit(solution)/shard_map/ppermute | solution.py:236
  22.7 4.4 %collective-permute-done.7 = f32[2,192,128]{2,1,0:T(8,128)S(1)} collective-permute-done((f32[2,192,128]{2,1,0:T(8,128)S(1)}, f32[2,192,128]{2,1,0:T(8,128)S(1)}, u32[]{:S(2)}, u32[]{:S(2)}) %collective-permute-start.7) | collective-permute-done | bytes 196640 | tf_op jit(solution)/shard_map/ppermute | solution.py:236
  27.1 1.2 %collective-permute-start.8 = (f32[2,128,128]{2,1,0:T(8,128)S(1)}, f32[2,128,128]{2,1,0:T(8,128)S(1)}, u32[]{:S(2)}, u32[]{:S(2)}) collective-permute-start(f32[2,128,128]{2,1,0:T(8,128)S(1)} %get-tuple-element.27), channel_id=1, source_target_pairs={{0,8},{1,9},{2,10},{3,11},{4,12},{5,13},{6,14},{7,15},{8,0},{9,1},... | collective-permute-start | bytes 393224 | tf_op jit(solution)/shard_map/ppermute | solution.py:236
  28.4 1.3 %collective-permute-start.9 = (f32[2,128,128]{2,1,0:T(8,128)S(1)}, f32[2,128,128]{2,1,0:T(8,128)S(1)}, u32[]{:S(2)}, u32[]{:S(2)}) collective-permute-start(f32[2,128,128]{2,1,0:T(8,128)S(1)} %get-tuple-element.28), channel_id=1, source_target_pairs={{0,24},{1,25},{2,26},{3,27},{4,28},{5,29},{6,30},{7,31},{8,16},{9,... | collective-permute-start | bytes 393224 | tf_op jit(solution)/shard_map/ppermute | solution.py:236
  29.7 1.1 %collective-permute-start.10 = (f32[2,64,128]{2,1,0:T(8,128)S(1)}, f32[2,64,128]{2,1,0:T(8,128)S(1)}, u32[]{:S(2)}, u32[]{:S(2)}) collective-permute-start(f32[2,64,128]{2,1,0:T(8,128)S(1)} %slice_select_fusion.4), channel_id=1, source_target_pairs={{0,16},{1,17},{2,18},{3,19},{4,20},{5,21},{6,22},{7,23},{8,24},{9,... | collective-permute-start | bytes 196616 | tf_op jit(solution)/shard_map/ppermute | solution.py:236
  30.8 2.8 %collective-permute-done.8 = f32[2,128,128]{2,1,0:T(8,128)S(1)} collective-permute-done((f32[2,128,128]{2,1,0:T(8,128)S(1)}, f32[2,128,128]{2,1,0:T(8,128)S(1)}, u32[]{:S(2)}, u32[]{:S(2)}) %collective-permute-start.8) | collective-permute-done | bytes 131104 | tf_op jit(solution)/shard_map/ppermute | solution.py:236
  33.6 2.5 %collective-permute-done.9 = f32[2,128,128]{2,1,0:T(8,128)S(1)} collective-permute-done((f32[2,128,128]{2,1,0:T(8,128)S(1)}, f32[2,128,128]{2,1,0:T(8,128)S(1)}, u32[]{:S(2)}, u32[]{:S(2)}) %collective-permute-start.9) | collective-permute-done | bytes 131104 | tf_op jit(solution)/shard_map/ppermute | solution.py:236
  36.1 0.2 collective-permute-done.10
  36.5 0.8 %collective-permute-start.11 = (f32[2,192,128]{2,1,0:T(8,128)S(1)}, f32[2,192,128]{2,1,0:T(8,128)S(1)}, u32[]{:S(2)}, u32[]{:S(2)}) collective-permute-start(f32[2,192,128]{2,1,0:T(8,128)S(1)} %fusion.mid_ref), channel_id=1, source_target_pairs={{0,8},{1,2},{2,1},{3,4},{4,3},{5,6},{6,5},{7,15},{8,0},{9,10},{10,... | collective-permute-start | bytes 589832 | tf_op jit(solution)/shard_map/ppermute | solution.py:236
  37.3 0.6 %collective-permute-done.12.near_ref = f32[2,192,128]{2,1,0:T(8,128)S(1)} collective-permute-done((f32[2,192,128]{2,1,0:T(8,128)S(1)}, f32[2,192,128]{2,1,0:T(8,128)S(1)}, u32[]{:S(2)}, u32[]{:S(2)}) %collective-permute-start.12) | collective-permute-done | bytes 196640 | tf_op jit(solution)/shard_map/ppermute | solution.py:236
  37.9 4.3 %collective-permute-done.11.far_ref = f32[2,192,128]{2,1,0:T(8,128)S(1)} collective-permute-done((f32[2,192,128]{2,1,0:T(8,128)S(1)}, f32[2,192,128]{2,1,0:T(8,128)S(1)}, u32[]{:S(2)}, u32[]{:S(2)}) %collective-permute-start.11) | collective-permute-done | bytes 196640 | tf_op jit(solution)/shard_map/ppermute | solution.py:236
  42.2 5.8 %tile_gradient.3 = (f32[2,192,128]{2,1,0:T(8,128)S(1)}, f32[2,192,128]{2,1,0:T(8,128)S(1)}, f32[2,192,128]{2,1,0:T(8,128)S(1)}) custom-call(s32[12]{0:T(128)S(1)} %reshape.8.offsets, s32[1]{0:T(128)} %bitcast.17.count, s32[2]{0:T(128)S(1)} %add_convert_fusion.place, f32[2,192,128]{2,1,0:T(8,128)S(1)} %collective-permute-done.11.far_ref, ...), custom_call_target="tpu_custom_call" | custom-call | tf_op jit(solution)/shard_map/tile_gradient/pallas_call | solution.py:218
  48.2 0.8 %collective-permute-start.14 = (f32[2,64,128]{2,1,0:T(8,128)S(1)}, f32[2,64,128]{2,1,0:T(8,128)S(1)}, u32[]{:S(2)}, u32[]{:S(2)}) collective-permute-start(f32[2,64,128]{2,1,0:T(8,128)S(1)} %get-tuple-element.22), channel_id=1, source_target_pairs={{0,8},{1,2},{2,1},{3,4},{4,3},{5,6},{6,5},{7,15},{8,0},{9,10},{10,... | collective-permute-start | bytes 196616 | tf_op jit(solution)/shard_map/ppermute | solution.py:236
  49.1 1.3 %collective-permute-start.15 = (f32[2,64,128]{2,1,0:T(8,128)S(1)}, f32[2,64,128]{2,1,0:T(8,128)S(1)}, u32[]{:S(2)}, u32[]{:S(2)}) collective-permute-start(f32[2,64,128]{2,1,0:T(8,128)S(1)} %get-tuple-element.23), channel_id=1, source_target_pairs={{0,8},{1,10},{2,9},{3,12},{4,11},{5,14},{6,13},{7,15},{8,0},{9,2},... | collective-permute-start | bytes 196616 | tf_op jit(solution)/shard_map/ppermute | solution.py:236
  50.3 1.7 %collective-permute-start.16 = (f32[2,64,128]{2,1,0:T(8,128)S(1)}, f32[2,64,128]{2,1,0:T(8,128)S(1)}, u32[]{:S(2)}, u32[]{:S(2)}) collective-permute-start(f32[2,64,128]{2,1,0:T(8,128)S(1)} %get-tuple-element.24), channel_id=1, source_target_pairs={{0,24},{1,26},{2,25},{3,28},{4,27},{5,30},{6,29},{7,31},{8,16},{9,... | collective-permute-start | bytes 196616 | tf_op jit(solution)/shard_map/ppermute | solution.py:236
  52.1 0.9 %collective-permute-start.17 = (f32[2,64,128]{2,1,0:T(8,128)S(1)}, f32[2,64,128]{2,1,0:T(8,128)S(1)}, u32[]{:S(2)}, u32[]{:S(2)}) collective-permute-start(f32[2,64,128]{2,1,0:T(8,128)S(1)} %get-tuple-element.25), channel_id=1, source_target_pairs={{0,8},{1,9},{2,10},{3,11},{4,12},{5,13},{6,14},{7,15},{8,0},{9,1},... | collective-permute-start | bytes 196616 | tf_op jit(solution)/shard_map/ppermute | solution.py:236
  52.9 1.2 %collective-permute-start.18 = (f32[2,64,128]{2,1,0:T(8,128)S(1)}, f32[2,64,128]{2,1,0:T(8,128)S(1)}, u32[]{:S(2)}, u32[]{:S(2)}) collective-permute-start(f32[2,64,128]{2,1,0:T(8,128)S(1)} %get-tuple-element.26), channel_id=1, source_target_pairs={{0,24},{1,25},{2,26},{3,27},{4,28},{5,29},{6,30},{7,31},{8,16},{9,... | collective-permute-start | bytes 196616 | tf_op jit(solution)/shard_map/ppermute | solution.py:236
  54.2 2.8 %collective-permute-done.16 = f32[2,64,128]{2,1,0:T(8,128)S(1)} collective-permute-done((f32[2,64,128]{2,1,0:T(8,128)S(1)}, f32[2,64,128]{2,1,0:T(8,128)S(1)}, u32[]{:S(2)}, u32[]{:S(2)}) %collective-permute-start.16) | collective-permute-done | bytes 65568 | tf_op jit(solution)/shard_map/ppermute | solution.py:236
  57.0 0.8 %collective-permute-done.17 = f32[2,64,128]{2,1,0:T(8,128)S(1)} collective-permute-done((f32[2,64,128]{2,1,0:T(8,128)S(1)}, f32[2,64,128]{2,1,0:T(8,128)S(1)}, u32[]{:S(2)}, u32[]{:S(2)}) %collective-permute-start.17) | collective-permute-done | bytes 65568 | tf_op jit(solution)/shard_map/ppermute | solution.py:236
  57.8 1.4 %collective-permute-done.18 = f32[2,64,128]{2,1,0:T(8,128)S(1)} collective-permute-done((f32[2,64,128]{2,1,0:T(8,128)S(1)}, f32[2,64,128]{2,1,0:T(8,128)S(1)}, u32[]{:S(2)}, u32[]{:S(2)}) %collective-permute-start.18) | collective-permute-done | bytes 65568 | tf_op jit(solution)/shard_map/ppermute | solution.py:236
  59.3 0.7 %pad_maximum_fusion.3 = f32[2,2,64,64]{3,2,1,0:T(8,128)} fusion(f32[1,2,64,64]{3,2,1,0:T(8,128)S(1)} %get-tuple-element.36, f32[1,2,64,64]{3,2,1,0:T(8,128)S(1)} %get-tuple-element.35), kind=kLoop, calls=%fused_computation.6 | loop fusion | flops 16384 | bytes 131072 | tf_op jit(solution)/shard_map/stack | solution.py:359
  (41 shorter events, 1.5 us)
Async XLA Ops:
  0.0 9.7 %copy-start.4 = (s32[1,1,6,2]{2,3,1,0:T(2,128)S(1)}, s32[1,1,6,2]{2,3,1,0:T(2,128)}, u32[]{:S(2)}) copy-start(s32[1,1,6,2]{2,3,1,0:T(2,128)} %param.10) | copy-start | bytes 148
  0.9 8.9 %copy-start.3 = (f32[128,128]{1,0:T(8,128)S(1)}, f32[128,128]{1,0:T(8,128)}, u32[]{:S(2)}) copy-start(f32[128,128]{1,0:T(8,128)} %param.9) | copy-start | bytes 196612
  0.9 14.4 %copy-start = (bf16[8,256,256]{2,1,0:T(8,128)(2,1)S(1)}, bf16[8,256,256]{2,1,0:T(8,128)(2,1)}, u32[]{:S(2)}) copy-start(bf16[8,256,256]{2,1,0:T(8,128)(2,1)} %constant.48.clone.table_ref) | copy-start | bytes 3145732
  1.0 13.0 %collective-permute-start.3 = (f32[2,64,128]{2,1,0:T(8,128)S(1)}, f32[2,64,128]{2,1,0:T(8,128)S(1)}, u32[]{:S(2)}, u32[]{:S(2)}) collective-permute-start(f32[2,64,128]{2,1,0:T(8,128)S(1)} %pad_maximum_fusion.4), channel_id=1, source_target_pairs={{0,24},{1,26},{2,25},{3,28},{4,27},{5,30},{6,29},{7,31},{8,16},{9,... | collective-permute-start | bytes 196616 | tf_op jit(solution)/shard_map/ppermute | solution.py:236
  5.0 9.0 %collective-permute-start.2 = (f32[2,64,128]{2,1,0:T(8,128)S(1)}, f32[2,64,128]{2,1,0:T(8,128)S(1)}, u32[]{:S(2)}, u32[]{:S(2)}) collective-permute-start(f32[2,64,128]{2,1,0:T(8,128)S(1)} %pad_maximum_fusion.4), channel_id=1, source_target_pairs={{0,8},{1,10},{2,9},{3,12},{4,11},{5,14},{6,13},{7,15},{8,0},{9,2},... | collective-permute-start | bytes 196616 | tf_op jit(solution)/shard_map/ppermute | solution.py:236
  5.5 8.5 %collective-permute-start.4 = (f32[2,64,128]{2,1,0:T(8,128)S(1)}, f32[2,64,128]{2,1,0:T(8,128)S(1)}, u32[]{:S(2)}, u32[]{:S(2)}) collective-permute-start(f32[2,64,128]{2,1,0:T(8,128)S(1)} %pad_maximum_fusion.4), channel_id=1, source_target_pairs={{0,8},{1,2},{2,1},{3,4},{4,3},{5,6},{6,5},{7,15},{8,0},{9,10},{10,... | collective-permute-start | bytes 196616 | tf_op jit(solution)/shard_map/ppermute | solution.py:236
  7.0 5.9 %collective-permute-start.1 = (f32[2,64,128]{2,1,0:T(8,128)S(1)}, f32[2,64,128]{2,1,0:T(8,128)S(1)}, u32[]{:S(2)}, u32[]{:S(2)}) collective-permute-start(f32[2,64,128]{2,1,0:T(8,128)S(1)} %pad_maximum_fusion.4), channel_id=1, source_target_pairs={{0,24},{1,25},{2,26},{3,27},{4,28},{5,29},{6,30},{7,31},{8,16},{9,... | collective-permute-start | bytes 196616 | tf_op jit(solution)/shard_map/ppermute | solution.py:236
  7.1 6.6 %collective-permute-start = (f32[2,64,128]{2,1,0:T(8,128)S(1)}, f32[2,64,128]{2,1,0:T(8,128)S(1)}, u32[]{:S(2)}, u32[]{:S(2)}) collective-permute-start(f32[2,64,128]{2,1,0:T(8,128)S(1)} %pad_maximum_fusion.4), channel_id=1, source_target_pairs={{0,8},{1,9},{2,10},{3,11},{4,12},{5,13},{6,14},{7,15},{8,0},{9,1},... | collective-permute-start | bytes 196616 | tf_op jit(solution)/shard_map/ppermute | solution.py:236
  13.8 1.5 %copy-start.1 = (f32[1,1,6,128,128]{4,3,2,1,0:T(8,128)S(1)}, f32[1,1,6,128,128]{4,3,2,1,0:T(8,128)}, u32[]{:S(2)}) copy-start(f32[1,1,6,128,128]{4,3,2,1,0:T(8,128)} %param.12) | copy-start | bytes 1179652
  13.8 1.5 %collective-permute-start.5 = (f32[2,192,128]{2,1,0:T(8,128)S(1)}, f32[2,192,128]{2,1,0:T(8,128)S(1)}, u32[]{:S(2)}, u32[]{:S(2)}) collective-permute-start(f32[2,192,128]{2,1,0:T(8,128)S(1)} %pad_maximum_fusion.mid_ref), channel_id=1, source_target_pairs={{0,1},{1,0},{2,3},{3,2},{4,5},{5,4},{6,7},{7,6},{8,9},{9,8},{10,11... | collective-permute-start | bytes 589832 | tf_op jit(solution)/shard_map/ppermute | solution.py:236
  14.0 1.3 %copy-start.2 = (f32[2,128,128]{2,1,0:T(8,128)S(1)}, f32[2,128,128]{2,1,0:T(8,128)}, u32[]{:S(2)}) copy-start(f32[2,128,128]{2,1,0:T(8,128)} %probe_ref.3) | copy-start | bytes 393220
  21.2 1.5 %collective-permute-start.6 = (f32[2,192,128]{2,1,0:T(8,128)S(1)}, f32[2,192,128]{2,1,0:T(8,128)S(1)}, u32[]{:S(2)}, u32[]{:S(2)}) collective-permute-start(f32[2,192,128]{2,1,0:T(8,128)S(1)} %get-tuple-element.12), channel_id=1, source_target_pairs={{0,1},{1,0},{2,3},{3,2},{4,5},{5,4},{6,7},{7,6},{8,9},{9,8},{10,11... | collective-permute-start | bytes 589832 | tf_op jit(solution)/shard_map/ppermute | solution.py:236
  21.4 5.7 %collective-permute-start.7 = (f32[2,192,128]{2,1,0:T(8,128)S(1)}, f32[2,192,128]{2,1,0:T(8,128)S(1)}, u32[]{:S(2)}, u32[]{:S(2)}) collective-permute-start(f32[2,192,128]{2,1,0:T(8,128)S(1)} %get-tuple-element.13), channel_id=1, source_target_pairs={{0,8},{1,2},{2,1},{3,4},{4,3},{5,6},{6,5},{7,15},{8,0},{9,10},{10,... | collective-permute-start | bytes 589832 | tf_op jit(solution)/shard_map/ppermute | solution.py:236
  27.1 6.4 %collective-permute-start.8 = (f32[2,128,128]{2,1,0:T(8,128)S(1)}, f32[2,128,128]{2,1,0:T(8,128)S(1)}, u32[]{:S(2)}, u32[]{:S(2)}) collective-permute-start(f32[2,128,128]{2,1,0:T(8,128)S(1)} %get-tuple-element.27), channel_id=1, source_target_pairs={{0,8},{1,9},{2,10},{3,11},{4,12},{5,13},{6,14},{7,15},{8,0},{9,1},... | collective-permute-start | bytes 393224 | tf_op jit(solution)/shard_map/ppermute | solution.py:236
  28.4 7.7 %collective-permute-start.9 = (f32[2,128,128]{2,1,0:T(8,128)S(1)}, f32[2,128,128]{2,1,0:T(8,128)S(1)}, u32[]{:S(2)}, u32[]{:S(2)}) collective-permute-start(f32[2,128,128]{2,1,0:T(8,128)S(1)} %get-tuple-element.28), channel_id=1, source_target_pairs={{0,24},{1,25},{2,26},{3,27},{4,28},{5,29},{6,30},{7,31},{8,16},{9,... | collective-permute-start | bytes 393224 | tf_op jit(solution)/shard_map/ppermute | solution.py:236
  29.7 6.6 %collective-permute-start.10 = (f32[2,64,128]{2,1,0:T(8,128)S(1)}, f32[2,64,128]{2,1,0:T(8,128)S(1)}, u32[]{:S(2)}, u32[]{:S(2)}) collective-permute-start(f32[2,64,128]{2,1,0:T(8,128)S(1)} %slice_select_fusion.4), channel_id=1, source_target_pairs={{0,16},{1,17},{2,18},{3,19},{4,20},{5,21},{6,22},{7,23},{8,24},{9,... | collective-permute-start | bytes 196616 | tf_op jit(solution)/shard_map/ppermute | solution.py:236
  36.4 1.5 %collective-permute-start.12 = (f32[2,192,128]{2,1,0:T(8,128)S(1)}, f32[2,192,128]{2,1,0:T(8,128)S(1)}, u32[]{:S(2)}, u32[]{:S(2)}) collective-permute-start(f32[2,192,128]{2,1,0:T(8,128)S(1)} %fusion.mid_ref), channel_id=1, source_target_pairs={{0,1},{1,0},{2,3},{3,2},{4,5},{5,4},{6,7},{7,6},{8,9},{9,8},{10,11... | collective-permute-start | bytes 589832 | tf_op jit(solution)/shard_map/ppermute | solution.py:236
  36.5 5.7 %collective-permute-start.11 = (f32[2,192,128]{2,1,0:T(8,128)S(1)}, f32[2,192,128]{2,1,0:T(8,128)S(1)}, u32[]{:S(2)}, u32[]{:S(2)}) collective-permute-start(f32[2,192,128]{2,1,0:T(8,128)S(1)} %fusion.mid_ref), channel_id=1, source_target_pairs={{0,8},{1,2},{2,1},{3,4},{4,3},{5,6},{6,5},{7,15},{8,0},{9,10},{10,... | collective-permute-start | bytes 589832 | tf_op jit(solution)/shard_map/ppermute | solution.py:236
  48.0 4.0 %collective-permute-start.13 = (f32[2,192,128]{2,1,0:T(8,128)S(1)}, f32[2,192,128]{2,1,0:T(8,128)S(1)}, u32[]{:S(2)}, u32[]{:S(2)}) collective-permute-start(f32[2,192,128]{2,1,0:T(8,128)S(1)} %get-tuple-element.15), channel_id=1, source_target_pairs={{0,1},{1,0},{2,3},{3,2},{4,5},{5,4},{6,7},{7,6},{8,9},{9,8},{10,11... | collective-permute-start | bytes 589832 | tf_op jit(solution)/shard_map/ppermute | solution.py:236
  48.2 5.9 %collective-permute-start.14 = (f32[2,64,128]{2,1,0:T(8,128)S(1)}, f32[2,64,128]{2,1,0:T(8,128)S(1)}, u32[]{:S(2)}, u32[]{:S(2)}) collective-permute-start(f32[2,64,128]{2,1,0:T(8,128)S(1)} %get-tuple-element.22), channel_id=1, source_target_pairs={{0,8},{1,2},{2,1},{3,4},{4,3},{5,6},{6,5},{7,15},{8,0},{9,10},{10,... | collective-permute-start | bytes 196616 | tf_op jit(solution)/shard_map/ppermute | solution.py:236
  49.1 5.1 %collective-permute-start.15 = (f32[2,64,128]{2,1,0:T(8,128)S(1)}, f32[2,64,128]{2,1,0:T(8,128)S(1)}, u32[]{:S(2)}, u32[]{:S(2)}) collective-permute-start(f32[2,64,128]{2,1,0:T(8,128)S(1)} %get-tuple-element.23), channel_id=1, source_target_pairs={{0,8},{1,10},{2,9},{3,12},{4,11},{5,14},{6,13},{7,15},{8,0},{9,2},... | collective-permute-start | bytes 196616 | tf_op jit(solution)/shard_map/ppermute | solution.py:236
  50.3 6.6 %collective-permute-start.16 = (f32[2,64,128]{2,1,0:T(8,128)S(1)}, f32[2,64,128]{2,1,0:T(8,128)S(1)}, u32[]{:S(2)}, u32[]{:S(2)}) collective-permute-start(f32[2,64,128]{2,1,0:T(8,128)S(1)} %get-tuple-element.24), channel_id=1, source_target_pairs={{0,24},{1,26},{2,25},{3,28},{4,27},{5,30},{6,29},{7,31},{8,16},{9,... | collective-permute-start | bytes 196616 | tf_op jit(solution)/shard_map/ppermute | solution.py:236
  52.1 5.7 %collective-permute-start.17 = (f32[2,64,128]{2,1,0:T(8,128)S(1)}, f32[2,64,128]{2,1,0:T(8,128)S(1)}, u32[]{:S(2)}, u32[]{:S(2)}) collective-permute-start(f32[2,64,128]{2,1,0:T(8,128)S(1)} %get-tuple-element.25), channel_id=1, source_target_pairs={{0,8},{1,9},{2,10},{3,11},{4,12},{5,13},{6,14},{7,15},{8,0},{9,1},... | collective-permute-start | bytes 196616 | tf_op jit(solution)/shard_map/ppermute | solution.py:236
  52.9 6.3 %collective-permute-start.18 = (f32[2,64,128]{2,1,0:T(8,128)S(1)}, f32[2,64,128]{2,1,0:T(8,128)S(1)}, u32[]{:S(2)}, u32[]{:S(2)}) collective-permute-start(f32[2,64,128]{2,1,0:T(8,128)S(1)} %get-tuple-element.26), channel_id=1, source_target_pairs={{0,24},{1,25},{2,26},{3,27},{4,28},{5,29},{6,30},{7,31},{8,16},{9,... | collective-permute-start | bytes 196616 | tf_op jit(solution)/shard_map/ppermute | solution.py:236

commit v4 on v3

--- a/solution.py
+++ b/solution.py
@@ -40,18 +40,67 @@
     return jnp.dot(a, b, preferred_element_type=jnp.float32)
 
 
+def column_place():
+    col, broad = lax.axis_index("tx"), lax.axis_size("tx")
+    is_first = lax.rem(col, 2) == 0
+    return is_first, jnp.where(is_first, col, broad - 1 - col) > 0
+
+
+def prepare_kernel(offsets, count, phase_ref, probe_ref, data_ref, field_ref, ordered_ref, plan_ref):
+    length = phase_ref.shape[0]
+    half = length // 2
+    lane = lax.broadcasted_iota(jnp.int32, (length, length), 1)
+    order = jnp.where(lane < half, 2 * lane, 2 * lane - (length - 1))
+
+    def even_odd(ref):
+        rows = [ref[pl.ds(odd, half, stride=2), :] for odd in range(2)]
+        return jnp.take_along_axis(jnp.concatenate(rows, axis=0), order, axis=1)
+
+    phase = even_odd(phase_ref)
+    field_ref[0] = probe_ref[0]
+    field_ref[1] = probe_ref[1]
+    field_ref[2] = jnp.cos(phase)
+    field_ref[3] = jnp.sin(phase)
+    for k in range(data_ref.shape[0]):
+        ordered_ref[k] = even_odd(data_ref.at[k])
+    line = lax.broadcasted_iota(jnp.int32, plan_ref.shape, 0)
+    slot = lax.broadcasted_iota(jnp.int32, plan_ref.shape, 1)
+    plan = jnp.where(line == 2, count[0, 0], 0)
+    for k in range(data_ref.shape[0]):
+        pair = jnp.where(line == 0, offsets[0, k], offsets[1, k])
+        plan = jnp.where((slot == k) & (line < 2), pair, plan)
+    plan_ref[...] = plan
+
+
+def prepared(offsets, count, phase, probe, data):
+    vmem = pl.BlockSpec(memory_space=pltpu.VMEM)
+    smem = pl.BlockSpec(memory_space=pltpu.SMEM)
+    return pl.pallas_call(
+        prepare_kernel,
+        out_shape=(
+            jax.ShapeDtypeStruct((4, *phase.shape), jnp.float32),
+            jax.ShapeDtypeStruct(data.shape, jnp.float32),
+            jax.ShapeDtypeStruct((8, 128), jnp.int32),
+        ),
+        in_specs=[smem] * 2 + [vmem] * 3,
+        out_specs=(vmem, vmem, vmem),
+        compiler_params=pltpu.CompilerParams(vmem_limit_bytes=16 * 1024 * 1024),
+        name="prepare",
+    )(offsets, count, phase, probe, data)
+
+
 def gradient_kernel(
-    offsets, count, place, far_ref, mid_ref, near_ref, probe_ref, prop_ref, data_ref, table_ref,
+    plan, far_ref, mid_ref, near_ref, field_ref, data_ref, table_ref,
     gfar_ref, gmid_ref, gnear_ref, ext, acc,
 ):
     layers, rows, lanes = mid_ref.shape
-    length = probe_ref.shape[1]
+    length = field_ref.shape[1]
     core = lanes // 2
-    positions = offsets.shape[0] // 2
+    positions = data_ref.shape[0]
     group = min(GROUP, positions)
     lane = lax.broadcasted_iota(jnp.int32, (rows, lanes), 1)
     low_half = lane < core
-    is_first, has_far = place[0] == 1, place[1] == 1
+    is_first, has_far = column_place()
     for s in range(layers):
         outer = jnp.where(has_far, far_ref[s], 0.0)
         left = jnp.where(is_first, outer, near_ref[s])
@@ -139,13 +188,6 @@
     def inverse(blocks):
         return rows_inverse(columns_inverse(blocks))
 
-    lanes_of = lax.broadcasted_iota(jnp.int32, (length, length), 1)
-    order = jnp.where(low_lanes, 2 * lanes_of, 2 * lanes_of - (length - 1))
-
-    def even_odd(ref, k):
-        rows_split = [ref[k, pl.ds(odd, half, stride=2), :] for odd in range(2)]
-        return jnp.take_along_axis(jnp.concatenate(rows_split, axis=0), order, axis=1)
-
     def times(a, b):
         return a[0] * b[0] - a[1] * b[1], a[0] * b[1] + a[1] * b[0]
 
@@ -154,15 +196,15 @@
 
     wide = lax.broadcasted_iota(jnp.int32, (length, lanes), 1)
 
-    @pl.loop(0, pl.cdiv(count[0], group))
+    @pl.loop(0, pl.cdiv(plan[2, 0], group))
     def _(trip):
         slots = [jnp.minimum(trip * group + q, positions - 1) for q in range(group)]
         weight = [
-            jnp.where(trip * group + q < count[0], 4.0, 0.0).astype(jnp.float32)
+            jnp.where(trip * group + q < plan[2, 0], 4.0, 0.0).astype(jnp.float32)
             for q in range(group)
         ]
-        row = [offsets[2 * k] for k in slots]
-        col = [offsets[2 * k + 1] for k in slots]
+        row = [plan[0, k] for k in slots]
+        col = [plan[1, k] for k in slots]
 
         def window(q, s):
             back = jnp.where(col[q] == 0, 0, lanes - col[q])
@@ -173,8 +215,8 @@
                 parts.append(pltpu.roll(both, back, 1))
             return tuple(parts)
 
-        prop = (even_odd(prop_ref, 0), even_odd(prop_ref, 1))
-        probe = (probe_ref[0], probe_ref[1])
+        prop = (field_ref[2], field_ref[3])
+        probe = (field_ref[0], field_ref[1])
         windows = [[window(q, s) for q in range(group)] for s in range(layers)]
         fields = [[probe] * group]
         for s in range(layers):
@@ -186,7 +228,7 @@
         back = []
         for q in range(group):
             re, im = far[q]
-            factor = weight[q] * (re * re + im * im - even_odd(data_ref, slots[q]))
+            factor = weight[q] * (re * re + im * im - data_ref[slots[q]])
             back.append((factor * re, factor * im))
         grad = inverse(back)
         for s in reversed(range(layers)):
@@ -210,7 +252,7 @@
         gnear_ref[s] = jnp.where(is_first, right, left)
 
 
-def tile_gradient(offsets, count, place, far, mid, near, probe, prop, data, table):
+def tile_gradient(plan, far, mid, near, field, data, table):
     layers, rows, lanes = mid.shape
     vmem = pl.BlockSpec(memory_space=pltpu.VMEM)
     smem = pl.BlockSpec(memory_space=pltpu.SMEM)
@@ -218,12 +260,12 @@
     return pl.pallas_call(
         gradient_kernel,
         out_shape=(strip, strip, strip),
-        in_specs=[smem] * 3 + [vmem] * 7,
+        in_specs=[smem] + [vmem] * 6,
         out_specs=(vmem, vmem, vmem),
         scratch_shapes=[pltpu.VMEM((layers, 2, 2, rows, lanes), jnp.float32)] * 2,
         compiler_params=pltpu.CompilerParams(vmem_limit_bytes=32 * 1024 * 1024),
         name="tile_gradient",
-    )(offsets, count, place, far, mid, near, probe, prop, data, table)
+    )(plan, far, mid, near, field, data, table)
 
 
 def exchange(shard, partner):
@@ -283,12 +325,12 @@
     tall, broad = lax.axis_size("ty"), lax.axis_size("tx")
     if tall % 2 or broad % 2 or (tall > 2 and tall % 4):
         raise ValueError("unsupported mesh")
-    row, col = lax.axis_index("ty"), lax.axis_index("tx")
+    row = lax.axis_index("ty")
     table = jnp.asarray(dft_tables(probe_field.shape[1]))
-    prop = jnp.stack([jnp.cos(propagator_phase), jnp.sin(propagator_phase)])
-    is_first = col % 2 == 0
-    has_far = jnp.where(is_first, col > 0, col < broad - 1)
-    place = jnp.stack([is_first, has_far]).astype(jnp.int32)
+    field, ordered, plan = prepared(
+        scan_offsets[0, 0].T, position_counts, propagator_phase, probe_field, intensities[0, 0]
+    )
+    _, has_far = column_place()
     has_above, has_below = row > 0, row < tall - 1
     odd = row % 2 == 1
 
@@ -301,23 +343,16 @@
         return above, below
 
     def gradient(strip, far, near):
-        return tile_gradient(
-            scan_offsets.reshape(-1), position_counts.reshape(-1), place, far, strip, near,
-            probe_field, prop, intensities[0, 0], table,
-        )
+        return tile_gradient(plan, far, strip, near, field, ordered, table)
 
     def column_exchange(far, near):
-        return exchange(far, other_chip(same_row)), exchange(near, same_chip)
+        return (exchange(far, other_chip(same_row)), exchange(near, same_chip))
 
     own = jnp.concatenate([transmission[0], transmission[1]], axis=-1)
-    above, below = sorted_rows(
-        exchange(own, within_column(row_pair)), exchange(own, within_column(row_cross))
-    )
+    above, below = sorted_rows(exchange(own, within_column(row_pair)), exchange(own, within_column(row_cross)))
     strip = jnp.concatenate([above, own, below], axis=1)
     near = exchange(strip, same_chip)
-    far_above, far_below = sorted_rows(
-        exchange(own, other_chip(row_pair)), exchange(own, other_chip(row_cross))
-    )
+    far_above, far_below = sorted_rows(exchange(own, other_chip(row_pair)), exchange(own, other_chip(row_cross)))
     far = jnp.concatenate([far_above, exchange(own, other_chip(same_row)), far_below], axis=1)
 
     for sweep in range(ITERS):
@@ -346,10 +381,7 @@
             total = gmid + exchange(gnear, same_chip)
             grad = total[:, core : 2 * core]
             grad += masked(has_far, exchange(gfar[:, core : 2 * core], other_chip(same_row)))
-            for part, keep, reach in (
-                (gfar, has_far, other_chip),
-                (total, True, within_column),
-            ):
+            for part, keep, reach in ((gfar, has_far, other_chip), (total, True, within_column)):
                 top, bottom = part[:, :core], part[:, 2 * core :]
                 pair = exchange(jnp.where(odd, top, bottom), reach(row_pair))
                 cross = exchange(jnp.where(odd, bottom, top), reach(row_cross))

time: 60.1 us -> 59 us (0.982)
  waiting for transfers between devices: 24.7 us -> 19.5 us
  starting transfers between devices: 20.1 us -> 22.8 us
  Pallas kernels: 11.6 us -> 12.6 us
    ppermute x19, waiting for transfers between devices: 24.7 us -> 19.5 us  [exchange(): return lax.ppermute(shard, ('ty', 'tx'), pairs)]
    ppermute x19, starting transfers between devices: 20.1 us -> 22.8 us  [exchange(): return lax.ppermute(shard, ('ty', 'tx'), pairs)]
    pallas_call x0 -> x1, Pallas kernels: none -> 0.86 us  [prepared(): pl.pallas_call(prepare_kernel, out_shape=(jax.ShapeDtypeStruct((4, *phase...]
    unnamed x11 -> x10, local copies, waits for them, and re-layouts: 0.12 us -> 0.92 us
  transfers between devices with their start and end apart: 19 -> 19, of which waited for: 13 -> 9; matrix products, arithmetic and copies ran while one was open for 1% -> 0% of each run, Pallas kernels for 0% -> 1%
where the time goes in v4:
time: 59 us; the launch traced here: 58.9 us
  starting transfers between devices  22.8 us (39%)
  waiting for transfers between devices  19.5 us (33%)
  Pallas kernels  12.6 us (21%)
  local copies, waits for them, and re-layouts  1.93 us (3%)
  other arithmetic  1.21 us (2%)
  between operations  0.84 us (1%)
    ppermute x19, starting transfers between devices, exchange(): return lax.ppermute(shard, ('ty', 'tx'), pairs)  22.8 us
    ppermute x19, waiting for transfers between devices, exchange(): return lax.ppermute(shard, ('ty', 'tx'), pairs)  19.5 us
    pallas_call x2, Pallas kernels, tile_gradient(): pl.pallas_call(gradient_kernel, out_shape=(strip, strip, strip), in_specs...  11.7 us
  transfers between devices with their start and end apart: 19, of which 9 were waited for; matrix products, arithmetic and copies ran while one was open for 0% of the time, Pallas kernels for 1%

profile of v4, /device:TPU:0, one launch (start us, length us, event | category | flops | bytes accessed | tf_op | source)
XLA Modules:
  0.0 58.9 jit_solution(16738511945202121437)
XLA Ops:
  0.0 0.9 %slice_bitcast_fusion.3 = (f32[2,64,64]{2,1,0:T(8,128)S(1)}, f32[2,64,64]{2,1,0:T(8,128)S(1)}) fusion(f32[2,2,64,64]{3,2,1,0:T(8,128)} %param.7), kind=kLoop, calls=%fused_computation.31 | loop fusion | bytes 131072 | tf_op jit(solution)/shard_map/squeeze | solution.py:351
  1.1 4.0 %collective-permute-start.1 = (f32[2,64,128]{2,1,0:T(8,128)S(1)}, f32[2,64,128]{2,1,0:T(8,128)S(1)}, u32[]{:S(2)}, u32[]{:S(2)}) collective-permute-start(f32[2,64,128]{2,1,0:T(8,128)S(1)} %pad_maximum_fusion.3), channel_id=1, source_target_pairs={{0,24},{1,25},{2,26},{3,27},{4,28},{5,29},{6,30},{7,31},{8,16},{9,... | collective-permute-start | bytes 196616 | tf_op jit(solution)/shard_map/ppermute | solution.py:278
  5.1 0.5 collective-permute-start
  5.6 1.4 %collective-permute-start.3 = (f32[2,64,128]{2,1,0:T(8,128)S(1)}, f32[2,64,128]{2,1,0:T(8,128)S(1)}, u32[]{:S(2)}, u32[]{:S(2)}) collective-permute-start(f32[2,64,128]{2,1,0:T(8,128)S(1)} %pad_maximum_fusion.3), channel_id=1, source_target_pairs={{0,24},{1,26},{2,25},{3,28},{4,27},{5,30},{6,29},{7,31},{8,16},{9,... | collective-permute-start | bytes 196616 | tf_op jit(solution)/shard_map/ppermute | solution.py:278
  7.2 1.9 %collective-permute-start.4 = (f32[2,64,128]{2,1,0:T(8,128)S(1)}, f32[2,64,128]{2,1,0:T(8,128)S(1)}, u32[]{:S(2)}, u32[]{:S(2)}) collective-permute-start(f32[2,64,128]{2,1,0:T(8,128)S(1)} %pad_maximum_fusion.3), channel_id=1, source_target_pairs={{0,8},{1,2},{2,1},{3,4},{4,3},{5,6},{6,5},{7,15},{8,0},{9,10},{10,... | collective-permute-start | bytes 196616 | tf_op jit(solution)/shard_map/ppermute | solution.py:278
  9.7 0.9 %copy-done.2 = f32[2,128,128]{2,1,0:T(8,128)S(1)} copy-done((f32[2,128,128]{2,1,0:T(8,128)S(1)}, f32[2,128,128]{2,1,0:T(8,128)}, u32[]{:S(2)}) %copy-start.2) | copy-done | bytes 131096
  10.6 0.9 %prepare.1 = (f32[4,128,128]{2,1,0:T(8,128)S(1)}, f32[6,128,128]{2,1,0:T(8,128)S(1)}, s32[8,128]{1,0:T(8,128)S(1)}) custom-call(s32[2,6]{1,0:T(2,128)S(1)} %bitcast.13, s32[1,1]{1,0:T(1,128)S(6)} %copy.8.count, f32[128,128]{1,0:T(8,128)S(1)} %copy-done.3, f32[2,128,128]{2,1,0:T(8,128)S(1)} %copy-done.2, f32[6,128,128]{2,1,0:T(8,128)S(1)} %bitcast.12), custom_call_target="tpu_custom_call" | custom-call | tf_op jit(solution)/shard_map/prepare/pallas_call | solution.py:78
  11.6 0.9 %collective-permute-start.5 = (f32[2,192,128]{2,1,0:T(8,128)S(1)}, f32[2,192,128]{2,1,0:T(8,128)S(1)}, u32[]{:S(2)}, u32[]{:S(2)}) collective-permute-start(f32[2,192,128]{2,1,0:T(8,128)S(1)} %pad_maximum_fusion.mid_ref), channel_id=1, source_target_pairs={{0,1},{1,0},{2,3},{3,2},{4,5},{5,4},{6,7},{7,6},{8,9},{9,8},{10,11... | collective-permute-start | bytes 589832 | tf_op jit(solution)/shard_map/ppermute | solution.py:278
  12.6 1.0 %collective-permute-done.5.near_ref = f32[2,192,128]{2,1,0:T(8,128)S(1)} collective-permute-done((f32[2,192,128]{2,1,0:T(8,128)S(1)}, f32[2,192,128]{2,1,0:T(8,128)S(1)}, u32[]{:S(2)}, u32[]{:S(2)}) %collective-permute-start.5) | collective-permute-done | bytes 196640 | tf_op jit(solution)/shard_map/ppermute | solution.py:278
  13.6 5.9 %tile_gradient.2 = (f32[2,192,128]{2,1,0:T(8,128)S(1)}, f32[2,192,128]{2,1,0:T(8,128)S(1)}, f32[2,192,128]{2,1,0:T(8,128)S(1)}) custom-call(s32[8,128]{1,0:T(8,128)S(1)} %get-tuple-element.14.plan, f32[2,192,128]{2,1,0:T(8,128)S(1)} %pad_maximum_fusion.1.far_ref, f32[2,192,128]{2,1,0:T(8,128)S(1)} %pad_maximum_fusion.mid_ref, ...), custom_call_target="tpu_custom_call" | custom-call | tf_op jit(solution)/shard_map/tile_gradient/pallas_call | solution.py:260
  19.5 0.4 collective-permute-start.6
  19.9 1.5 %collective-permute-start.7 = (f32[2,192,128]{2,1,0:T(8,128)S(1)}, f32[2,192,128]{2,1,0:T(8,128)S(1)}, u32[]{:S(2)}, u32[]{:S(2)}) collective-permute-start(f32[2,192,128]{2,1,0:T(8,128)S(1)} %get-tuple-element.19), channel_id=1, source_target_pairs={{0,8},{1,2},{2,1},{3,4},{4,3},{5,6},{6,5},{7,15},{8,0},{9,10},{10,... | collective-permute-start | bytes 589832 | tf_op jit(solution)/shard_map/ppermute | solution.py:278
  21.4 4.2 %collective-permute-done.7 = f32[2,192,128]{2,1,0:T(8,128)S(1)} collective-permute-done((f32[2,192,128]{2,1,0:T(8,128)S(1)}, f32[2,192,128]{2,1,0:T(8,128)S(1)}, u32[]{:S(2)}, u32[]{:S(2)}) %collective-permute-start.7) | collective-permute-done | bytes 196640 | tf_op jit(solution)/shard_map/ppermute | solution.py:278
  25.6 1.6 %collective-permute-start.8 = (f32[2,128,128]{2,1,0:T(8,128)S(1)}, f32[2,128,128]{2,1,0:T(8,128)S(1)}, u32[]{:S(2)}, u32[]{:S(2)}) collective-permute-start(f32[2,128,128]{2,1,0:T(8,128)S(1)} %get-tuple-element.33), channel_id=1, source_target_pairs={{0,8},{1,9},{2,10},{3,11},{4,12},{5,13},{6,14},{7,15},{8,0},{9,1},... | collective-permute-start | bytes 393224 | tf_op jit(solution)/shard_map/ppermute | solution.py:278
  27.2 1.5 %collective-permute-start.9 = (f32[2,128,128]{2,1,0:T(8,128)S(1)}, f32[2,128,128]{2,1,0:T(8,128)S(1)}, u32[]{:S(2)}, u32[]{:S(2)}) collective-permute-start(f32[2,128,128]{2,1,0:T(8,128)S(1)} %get-tuple-element.34), channel_id=1, source_target_pairs={{0,24},{1,25},{2,26},{3,27},{4,28},{5,29},{6,30},{7,31},{8,16},{9,... | collective-permute-start | bytes 393224 | tf_op jit(solution)/shard_map/ppermute | solution.py:278
  28.7 0.6 collective-permute-start.10
  29.3 2.3 %collective-permute-done.8 = f32[2,128,128]{2,1,0:T(8,128)S(1)} collective-permute-done((f32[2,128,128]{2,1,0:T(8,128)S(1)}, f32[2,128,128]{2,1,0:T(8,128)S(1)}, u32[]{:S(2)}, u32[]{:S(2)}) %collective-permute-start.8) | collective-permute-done | bytes 131104 | tf_op jit(solution)/shard_map/ppermute | solution.py:278
  31.6 3.3 %collective-permute-done.9 = f32[2,128,128]{2,1,0:T(8,128)S(1)} collective-permute-done((f32[2,128,128]{2,1,0:T(8,128)S(1)}, f32[2,128,128]{2,1,0:T(8,128)S(1)}, u32[]{:S(2)}, u32[]{:S(2)}) %collective-permute-start.9) | collective-permute-done | bytes 131104 | tf_op jit(solution)/shard_map/ppermute | solution.py:278
  34.9 0.2 collective-permute-done.10
  35.3 1.6 %collective-permute-start.11 = (f32[2,192,128]{2,1,0:T(8,128)S(1)}, f32[2,192,128]{2,1,0:T(8,128)S(1)}, u32[]{:S(2)}, u32[]{:S(2)}) collective-permute-start(f32[2,192,128]{2,1,0:T(8,128)S(1)} %fusion.mid_ref), channel_id=1, source_target_pairs={{0,8},{1,2},{2,1},{3,4},{4,3},{5,6},{6,5},{7,15},{8,0},{9,10},{10,... | collective-permute-start | bytes 589832 | tf_op jit(solution)/shard_map/ppermute | solution.py:278
  36.9 4.2 %collective-permute-done.11.far_ref = f32[2,192,128]{2,1,0:T(8,128)S(1)} collective-permute-done((f32[2,192,128]{2,1,0:T(8,128)S(1)}, f32[2,192,128]{2,1,0:T(8,128)S(1)}, u32[]{:S(2)}, u32[]{:S(2)}) %collective-permute-start.11) | collective-permute-done | bytes 196640 | tf_op jit(solution)/shard_map/ppermute | solution.py:278
  41.0 5.9 %tile_gradient.3 = (f32[2,192,128]{2,1,0:T(8,128)S(1)}, f32[2,192,128]{2,1,0:T(8,128)S(1)}, f32[2,192,128]{2,1,0:T(8,128)S(1)}) custom-call(s32[8,128]{1,0:T(8,128)S(1)} %get-tuple-element.14.plan, f32[2,192,128]{2,1,0:T(8,128)S(1)} %collective-permute-done.11.far_ref, f32[2,192,128]{2,1,0:T(8,128)S(1)} %fusion.mid_ref, ...), custom_call_target="tpu_custom_call" | custom-call | tf_op jit(solution)/shard_map/tile_gradient/pallas_call | solution.py:260
  46.9 0.2 collective-permute-start.13
  47.1 1.6 %collective-permute-start.14 = (f32[2,64,128]{2,1,0:T(8,128)S(1)}, f32[2,64,128]{2,1,0:T(8,128)S(1)}, u32[]{:S(2)}, u32[]{:S(2)}) collective-permute-start(f32[2,64,128]{2,1,0:T(8,128)S(1)} %get-tuple-element.28), channel_id=1, source_target_pairs={{0,8},{1,2},{2,1},{3,4},{4,3},{5,6},{6,5},{7,15},{8,0},{9,10},{10,... | collective-permute-start | bytes 196616 | tf_op jit(solution)/shard_map/ppermute | solution.py:278
  48.7 0.5 collective-permute-start.15
  49.2 1.4 %collective-permute-start.16 = (f32[2,64,128]{2,1,0:T(8,128)S(1)}, f32[2,64,128]{2,1,0:T(8,128)S(1)}, u32[]{:S(2)}, u32[]{:S(2)}) collective-permute-start(f32[2,64,128]{2,1,0:T(8,128)S(1)} %get-tuple-element.30), channel_id=1, source_target_pairs={{0,24},{1,26},{2,25},{3,28},{4,27},{5,30},{6,29},{7,31},{8,16},{9,... | collective-permute-start | bytes 196616 | tf_op jit(solution)/shard_map/ppermute | solution.py:278
  50.7 0.8 %collective-permute-start.17 = (f32[2,64,128]{2,1,0:T(8,128)S(1)}, f32[2,64,128]{2,1,0:T(8,128)S(1)}, u32[]{:S(2)}, u32[]{:S(2)}) collective-permute-start(f32[2,64,128]{2,1,0:T(8,128)S(1)} %get-tuple-element.31), channel_id=1, source_target_pairs={{0,8},{1,9},{2,10},{3,11},{4,12},{5,13},{6,14},{7,15},{8,0},{9,1},... | collective-permute-start | bytes 196616 | tf_op jit(solution)/shard_map/ppermute | solution.py:278
  51.5 2.2 %collective-permute-start.18 = (f32[2,64,128]{2,1,0:T(8,128)S(1)}, f32[2,64,128]{2,1,0:T(8,128)S(1)}, u32[]{:S(2)}, u32[]{:S(2)}) collective-permute-start(f32[2,64,128]{2,1,0:T(8,128)S(1)} %get-tuple-element.32), channel_id=1, source_target_pairs={{0,24},{1,25},{2,26},{3,27},{4,28},{5,29},{6,30},{7,31},{8,16},{9,... | collective-permute-start | bytes 196616 | tf_op jit(solution)/shard_map/ppermute | solution.py:278
  53.8 0.6 %collective-permute-done.16 = f32[2,64,128]{2,1,0:T(8,128)S(1)} collective-permute-done((f32[2,64,128]{2,1,0:T(8,128)S(1)}, f32[2,64,128]{2,1,0:T(8,128)S(1)}, u32[]{:S(2)}, u32[]{:S(2)}) %collective-permute-start.16) | collective-permute-done | bytes 65568 | tf_op jit(solution)/shard_map/ppermute | solution.py:278
  54.4 2.8 %collective-permute-done.17 = f32[2,64,128]{2,1,0:T(8,128)S(1)} collective-permute-done((f32[2,64,128]{2,1,0:T(8,128)S(1)}, f32[2,64,128]{2,1,0:T(8,128)S(1)}, u32[]{:S(2)}, u32[]{:S(2)}) %collective-permute-start.17) | collective-permute-done | bytes 65568 | tf_op jit(solution)/shard_map/ppermute | solution.py:278
  57.1 0.9 %collective-permute-done.18 = f32[2,64,128]{2,1,0:T(8,128)S(1)} collective-permute-done((f32[2,64,128]{2,1,0:T(8,128)S(1)}, f32[2,64,128]{2,1,0:T(8,128)S(1)}, u32[]{:S(2)}, u32[]{:S(2)}) %collective-permute-start.18) | collective-permute-done | bytes 65568 | tf_op jit(solution)/shard_map/ppermute | solution.py:278
  58.2 0.7 %pad_maximum_fusion.2 = f32[2,2,64,64]{3,2,1,0:T(8,128)} fusion(f32[1,2,64,64]{3,2,1,0:T(8,128)S(1)} %get-tuple-element.42, f32[1,2,64,64]{3,2,1,0:T(8,128)S(1)} %get-tuple-element.41), kind=kLoop, calls=%fused_computation.5 | loop fusion | flops 16384 | bytes 131072 | tf_op jit(solution)/shard_map/stack | solution.py:391
  (37 shorter events, 0.9 us)
Async XLA Ops:
  0.0 9.7 %copy-start.1 = (f32[1,1,6,128,128]{4,3,2,1,0:T(8,128)S(1)}, f32[1,1,6,128,128]{4,3,2,1,0:T(8,128)}, u32[]{:S(2)}) copy-start(f32[1,1,6,128,128]{4,3,2,1,0:T(8,128)} %param.12) | copy-start | bytes 1179652
  0.9 8.8 %copy-start.3 = (f32[128,128]{1,0:T(8,128)S(1)}, f32[128,128]{1,0:T(8,128)}, u32[]{:S(2)}) copy-start(f32[128,128]{1,0:T(8,128)} %phase_ref.1) | copy-start | bytes 196612
  0.9 8.8 %copy-start.4 = (s32[1,1,6,2]{2,3,1,0:T(2,128)S(1)}, s32[1,1,6,2]{2,3,1,0:T(2,128)}, u32[]{:S(2)}) copy-start(s32[1,1,6,2]{2,3,1,0:T(2,128)} %param.10) | copy-start | bytes 148
  1.1 12.5 %copy-start = (bf16[8,256,256]{2,1,0:T(8,128)(2,1)S(1)}, bf16[8,256,256]{2,1,0:T(8,128)(2,1)}, u32[]{:S(2)}) copy-start(bf16[8,256,256]{2,1,0:T(8,128)(2,1)} %constant.46.clone.table_ref) | copy-start | bytes 3145732
  1.1 10.4 %collective-permute-start.1 = (f32[2,64,128]{2,1,0:T(8,128)S(1)}, f32[2,64,128]{2,1,0:T(8,128)S(1)}, u32[]{:S(2)}, u32[]{:S(2)}) collective-permute-start(f32[2,64,128]{2,1,0:T(8,128)S(1)} %pad_maximum_fusion.3), channel_id=1, source_target_pairs={{0,24},{1,25},{2,26},{3,27},{4,28},{5,29},{6,30},{7,31},{8,16},{9,... | collective-permute-start | bytes 196616 | tf_op jit(solution)/shard_map/ppermute | solution.py:278
  5.1 6.5 %collective-permute-start = (f32[2,64,128]{2,1,0:T(8,128)S(1)}, f32[2,64,128]{2,1,0:T(8,128)S(1)}, u32[]{:S(2)}, u32[]{:S(2)}) collective-permute-start(f32[2,64,128]{2,1,0:T(8,128)S(1)} %pad_maximum_fusion.3), channel_id=1, source_target_pairs={{0,8},{1,9},{2,10},{3,11},{4,12},{5,13},{6,14},{7,15},{8,0},{9,1},... | collective-permute-start | bytes 196616 | tf_op jit(solution)/shard_map/ppermute | solution.py:278
  5.6 6.9 %collective-permute-start.3 = (f32[2,64,128]{2,1,0:T(8,128)S(1)}, f32[2,64,128]{2,1,0:T(8,128)S(1)}, u32[]{:S(2)}, u32[]{:S(2)}) collective-permute-start(f32[2,64,128]{2,1,0:T(8,128)S(1)} %pad_maximum_fusion.3), channel_id=1, source_target_pairs={{0,24},{1,26},{2,25},{3,28},{4,27},{5,30},{6,29},{7,31},{8,16},{9,... | collective-permute-start | bytes 196616 | tf_op jit(solution)/shard_map/ppermute | solution.py:278
  7.0 5.5 %collective-permute-start.2 = (f32[2,64,128]{2,1,0:T(8,128)S(1)}, f32[2,64,128]{2,1,0:T(8,128)S(1)}, u32[]{:S(2)}, u32[]{:S(2)}) collective-permute-start(f32[2,64,128]{2,1,0:T(8,128)S(1)} %pad_maximum_fusion.3), channel_id=1, source_target_pairs={{0,8},{1,10},{2,9},{3,12},{4,11},{5,14},{6,13},{7,15},{8,0},{9,2},... | collective-permute-start | bytes 196616 | tf_op jit(solution)/shard_map/ppermute | solution.py:278
  7.2 5.4 %collective-permute-start.4 = (f32[2,64,128]{2,1,0:T(8,128)S(1)}, f32[2,64,128]{2,1,0:T(8,128)S(1)}, u32[]{:S(2)}, u32[]{:S(2)}) collective-permute-start(f32[2,64,128]{2,1,0:T(8,128)S(1)} %pad_maximum_fusion.3), channel_id=1, source_target_pairs={{0,8},{1,2},{2,1},{3,4},{4,3},{5,6},{6,5},{7,15},{8,0},{9,10},{10,... | collective-permute-start | bytes 196616 | tf_op jit(solution)/shard_map/ppermute | solution.py:278
  9.7 0.9 %copy-start.2 = (f32[2,128,128]{2,1,0:T(8,128)S(1)}, f32[2,128,128]{2,1,0:T(8,128)}, u32[]{:S(2)}) copy-start(f32[2,128,128]{2,1,0:T(8,128)} %probe_ref.1) | copy-start | bytes 393220
  11.6 2.0 %collective-permute-start.5 = (f32[2,192,128]{2,1,0:T(8,128)S(1)}, f32[2,192,128]{2,1,0:T(8,128)S(1)}, u32[]{:S(2)}, u32[]{:S(2)}) collective-permute-start(f32[2,192,128]{2,1,0:T(8,128)S(1)} %pad_maximum_fusion.mid_ref), channel_id=1, source_target_pairs={{0,1},{1,0},{2,3},{3,2},{4,5},{5,4},{6,7},{7,6},{8,9},{9,8},{10,11... | collective-permute-start | bytes 589832 | tf_op jit(solution)/shard_map/ppermute | solution.py:278
  19.5 1.9 %collective-permute-start.6 = (f32[2,192,128]{2,1,0:T(8,128)S(1)}, f32[2,192,128]{2,1,0:T(8,128)S(1)}, u32[]{:S(2)}, u32[]{:S(2)}) collective-permute-start(f32[2,192,128]{2,1,0:T(8,128)S(1)} %get-tuple-element.18), channel_id=1, source_target_pairs={{0,1},{1,0},{2,3},{3,2},{4,5},{5,4},{6,7},{7,6},{8,9},{9,8},{10,11... | collective-permute-start | bytes 589832 | tf_op jit(solution)/shard_map/ppermute | solution.py:278
  19.9 5.7 %collective-permute-start.7 = (f32[2,192,128]{2,1,0:T(8,128)S(1)}, f32[2,192,128]{2,1,0:T(8,128)S(1)}, u32[]{:S(2)}, u32[]{:S(2)}) collective-permute-start(f32[2,192,128]{2,1,0:T(8,128)S(1)} %get-tuple-element.19), channel_id=1, source_target_pairs={{0,8},{1,2},{2,1},{3,4},{4,3},{5,6},{6,5},{7,15},{8,0},{9,10},{10,... | collective-permute-start | bytes 589832 | tf_op jit(solution)/shard_map/ppermute | solution.py:278
  25.6 5.9 %collective-permute-start.8 = (f32[2,128,128]{2,1,0:T(8,128)S(1)}, f32[2,128,128]{2,1,0:T(8,128)S(1)}, u32[]{:S(2)}, u32[]{:S(2)}) collective-permute-start(f32[2,128,128]{2,1,0:T(8,128)S(1)} %get-tuple-element.33), channel_id=1, source_target_pairs={{0,8},{1,9},{2,10},{3,11},{4,12},{5,13},{6,14},{7,15},{8,0},{9,1},... | collective-permute-start | bytes 393224 | tf_op jit(solution)/shard_map/ppermute | solution.py:278
  27.2 7.6 %collective-permute-start.9 = (f32[2,128,128]{2,1,0:T(8,128)S(1)}, f32[2,128,128]{2,1,0:T(8,128)S(1)}, u32[]{:S(2)}, u32[]{:S(2)}) collective-permute-start(f32[2,128,128]{2,1,0:T(8,128)S(1)} %get-tuple-element.34), channel_id=1, source_target_pairs={{0,24},{1,25},{2,26},{3,27},{4,28},{5,29},{6,30},{7,31},{8,16},{9,... | collective-permute-start | bytes 393224 | tf_op jit(solution)/shard_map/ppermute | solution.py:278
  28.7 6.4 %collective-permute-start.10 = (f32[2,64,128]{2,1,0:T(8,128)S(1)}, f32[2,64,128]{2,1,0:T(8,128)S(1)}, u32[]{:S(2)}, u32[]{:S(2)}) collective-permute-start(f32[2,64,128]{2,1,0:T(8,128)S(1)} %slice_select_fusion.4), channel_id=1, source_target_pairs={{0,16},{1,17},{2,18},{3,19},{4,20},{5,21},{6,22},{7,23},{8,24},{9,... | collective-permute-start | bytes 196616 | tf_op jit(solution)/shard_map/ppermute | solution.py:278
  35.2 1.7 %collective-permute-start.12 = (f32[2,192,128]{2,1,0:T(8,128)S(1)}, f32[2,192,128]{2,1,0:T(8,128)S(1)}, u32[]{:S(2)}, u32[]{:S(2)}) collective-permute-start(f32[2,192,128]{2,1,0:T(8,128)S(1)} %fusion.mid_ref), channel_id=1, source_target_pairs={{0,1},{1,0},{2,3},{3,2},{4,5},{5,4},{6,7},{7,6},{8,9},{9,8},{10,11... | collective-permute-start | bytes 589832 | tf_op jit(solution)/shard_map/ppermute | solution.py:278
  35.3 5.7 %collective-permute-start.11 = (f32[2,192,128]{2,1,0:T(8,128)S(1)}, f32[2,192,128]{2,1,0:T(8,128)S(1)}, u32[]{:S(2)}, u32[]{:S(2)}) collective-permute-start(f32[2,192,128]{2,1,0:T(8,128)S(1)} %fusion.mid_ref), channel_id=1, source_target_pairs={{0,8},{1,2},{2,1},{3,4},{4,3},{5,6},{6,5},{7,15},{8,0},{9,10},{10,... | collective-permute-start | bytes 589832 | tf_op jit(solution)/shard_map/ppermute | solution.py:278
  46.9 3.7 %collective-permute-start.13 = (f32[2,192,128]{2,1,0:T(8,128)S(1)}, f32[2,192,128]{2,1,0:T(8,128)S(1)}, u32[]{:S(2)}, u32[]{:S(2)}) collective-permute-start(f32[2,192,128]{2,1,0:T(8,128)S(1)} %get-tuple-element.21), channel_id=1, source_target_pairs={{0,1},{1,0},{2,3},{3,2},{4,5},{5,4},{6,7},{7,6},{8,9},{9,8},{10,11... | collective-permute-start | bytes 589832 | tf_op jit(solution)/shard_map/ppermute | solution.py:278
  47.1 6.7 %collective-permute-start.14 = (f32[2,64,128]{2,1,0:T(8,128)S(1)}, f32[2,64,128]{2,1,0:T(8,128)S(1)}, u32[]{:S(2)}, u32[]{:S(2)}) collective-permute-start(f32[2,64,128]{2,1,0:T(8,128)S(1)} %get-tuple-element.28), channel_id=1, source_target_pairs={{0,8},{1,2},{2,1},{3,4},{4,3},{5,6},{6,5},{7,15},{8,0},{9,10},{10,... | collective-permute-start | bytes 196616 | tf_op jit(solution)/shard_map/ppermute | solution.py:278
  48.7 5.1 %collective-permute-start.15 = (f32[2,64,128]{2,1,0:T(8,128)S(1)}, f32[2,64,128]{2,1,0:T(8,128)S(1)}, u32[]{:S(2)}, u32[]{:S(2)}) collective-permute-start(f32[2,64,128]{2,1,0:T(8,128)S(1)} %get-tuple-element.29), channel_id=1, source_target_pairs={{0,8},{1,10},{2,9},{3,12},{4,11},{5,14},{6,13},{7,15},{8,0},{9,2},... | collective-permute-start | bytes 196616 | tf_op jit(solution)/shard_map/ppermute | solution.py:278
  49.2 5.2 %collective-permute-start.16 = (f32[2,64,128]{2,1,0:T(8,128)S(1)}, f32[2,64,128]{2,1,0:T(8,128)S(1)}, u32[]{:S(2)}, u32[]{:S(2)}) collective-permute-start(f32[2,64,128]{2,1,0:T(8,128)S(1)} %get-tuple-element.30), channel_id=1, source_target_pairs={{0,24},{1,26},{2,25},{3,28},{4,27},{5,30},{6,29},{7,31},{8,16},{9,... | collective-permute-start | bytes 196616 | tf_op jit(solution)/shard_map/ppermute | solution.py:278
  50.7 6.5 %collective-permute-start.17 = (f32[2,64,128]{2,1,0:T(8,128)S(1)}, f32[2,64,128]{2,1,0:T(8,128)S(1)}, u32[]{:S(2)}, u32[]{:S(2)}) collective-permute-start(f32[2,64,128]{2,1,0:T(8,128)S(1)} %get-tuple-element.31), channel_id=1, source_target_pairs={{0,8},{1,9},{2,10},{3,11},{4,12},{5,13},{6,14},{7,15},{8,0},{9,1},... | collective-permute-start | bytes 196616 | tf_op jit(solution)/shard_map/ppermute | solution.py:278
  51.5 6.6 %collective-permute-start.18 = (f32[2,64,128]{2,1,0:T(8,128)S(1)}, f32[2,64,128]{2,1,0:T(8,128)S(1)}, u32[]{:S(2)}, u32[]{:S(2)}) collective-permute-start(f32[2,64,128]{2,1,0:T(8,128)S(1)} %get-tuple-element.32), channel_id=1, source_target_pairs={{0,24},{1,25},{2,26},{3,27},{4,28},{5,29},{6,30},{7,31},{8,16},{9,... | collective-permute-start | bytes 196616 | tf_op jit(solution)/shard_map/ppermute | solution.py:278

commit v5 on v4

--- a/solution.py
+++ b/solution.py
@@ -42,7 +42,7 @@
 
 def column_place():
     col, broad = lax.axis_index("tx"), lax.axis_size("tx")
-    is_first = lax.rem(col, 2) == 0
+    is_first = (col & 1) == 0
     return is_first, jnp.where(is_first, col, broad - 1 - col) > 0
 
 
@@ -65,7 +65,7 @@
         ordered_ref[k] = even_odd(data_ref.at[k])
     line = lax.broadcasted_iota(jnp.int32, plan_ref.shape, 0)
     slot = lax.broadcasted_iota(jnp.int32, plan_ref.shape, 1)
-    plan = jnp.where(line == 2, count[0, 0], 0)
+    plan = jnp.where(line == 2, jnp.broadcast_to(count[...], plan_ref.shape), 0)
     for k in range(data_ref.shape[0]):
         pair = jnp.where(line == 0, offsets[0, k], offsets[1, k])
         plan = jnp.where((slot == k) & (line < 2), pair, plan)
@@ -82,7 +82,7 @@
             jax.ShapeDtypeStruct(data.shape, jnp.float32),
             jax.ShapeDtypeStruct((8, 128), jnp.int32),
         ),
-        in_specs=[smem] * 2 + [vmem] * 3,
+        in_specs=[smem] + [vmem] * 4,
         out_specs=(vmem, vmem, vmem),
         compiler_params=pltpu.CompilerParams(vmem_limit_bytes=16 * 1024 * 1024),
         name="prepare",
@@ -207,18 +207,18 @@
         col = [plan[1, k] for k in slots]
 
         def window(q, s):
-            back = jnp.where(col[q] == 0, 0, lanes - col[q])
-            parts = []
-            for part in range(2):
-                rows_of = pl.ds(row[q], length)
-                both = jnp.where(wide >= col[q], ext[s, part, 0, rows_of, :], ext[s, part, 1, rows_of, :])
-                parts.append(pltpu.roll(both, back, 1))
-            return tuple(parts)
+            rows_of = pl.ds(row[q], length)
+            return tuple(
+                jnp.where(wide >= col[q], ext[s, part, 0, rows_of, :], ext[s, part, 1, rows_of, :])
+                for part in range(2)
+            )
 
         prop = (field_ref[2], field_ref[3])
-        probe = (field_ref[0], field_ref[1])
+        probes = [
+            tuple(pltpu.roll(field_ref[part], col[q], 1) for part in range(2)) for q in range(group)
+        ]
         windows = [[window(q, s) for q in range(group)] for s in range(layers)]
-        fields = [[probe] * group]
+        fields = [probes]
         for s in range(layers):
             exits = [times(fields[s][q], windows[s][q]) for q in range(group)]
             if s < layers - 1:
@@ -235,10 +235,9 @@
             for q in range(group):
                 own = conj_times(fields[s][q], grad[q])
                 for part in range(2):
-                    turned = pltpu.roll(own[part], col[q], 1)
                     rows_of = pl.ds(row[q], length)
-                    acc[s, part, 0, rows_of, :] += jnp.where(wide >= col[q], turned, 0.0)
-                    acc[s, part, 1, rows_of, :] += jnp.where(wide < col[q], turned, 0.0)
+                    acc[s, part, 0, rows_of, :] += jnp.where(wide >= col[q], own[part], 0.0)
+                    acc[s, part, 1, rows_of, :] += jnp.where(wide < col[q], own[part], 0.0)
             if s > 0:
                 spectrum = fourier([conj_times(windows[s][q], grad[q]) for q in range(group)])
                 grad = inverse([conj_times(prop, b) for b in spectrum])
@@ -332,7 +331,7 @@
     )
     _, has_far = column_place()
     has_above, has_below = row > 0, row < tall - 1
-    odd = row % 2 == 1
+    odd = (row & 1) == 1
 
     def masked(keep, x):
         return jnp.where(keep, x, 0.0)
@@ -367,7 +366,7 @@
             down, up = sorted_rows(pair, cross)
             above, inside, below = top + down[:, :core], mid + down[:, core:] + up[:, :core], bottom + up[:, core:]
             if tall > 2:
-                early = row % 4 < 2
+                early = (row & 2) == 0
                 got = exchange(jnp.where(early, bottom, top), within_column(two_pair))
                 above, below = above + masked(~early, got), below + masked(early, got)
             if tall > 4:

time: 59 us -> 58.9 us (level)
  transfers between devices with their start and end apart: 19 -> 19, of which waited for: 9 -> 10; matrix products, arithmetic and copies ran while one was open for 0% -> 0% of each run, Pallas kernels for 1% -> 1%
where the time goes in v5:
time: 58.9 us; the launch traced here: 58.7 us
  starting transfers between devices  22.7 us (39%)
  waiting for transfers between devices  19.5 us (33%)
  Pallas kernels  12.5 us (21%)
  local copies, waits for them, and re-layouts  1.93 us (3%)
  other arithmetic  1.21 us (2%)
  between operations  0.85 us (1%)
    ppermute x19, starting transfers between devices, exchange(): return lax.ppermute(shard, ('ty', 'tx'), pairs)  22.7 us
    ppermute x19, waiting for transfers between devices, exchange(): return lax.ppermute(shard, ('ty', 'tx'), pairs)  19.5 us
    pallas_call x2, Pallas kernels, tile_gradient(): pl.pallas_call(gradient_kernel, out_shape=(strip, strip, strip), in_specs...  11.7 us
  transfers between devices with their start and end apart: 19, of which 10 were waited for; matrix products, arithmetic and copies ran while one was open for 0% of the time, Pallas kernels for 1%

profile of v5, /device:TPU:0, one launch (start us, length us, event | category | flops | bytes accessed | tf_op | source)
XLA Modules:
  0.0 58.7 jit_solution(14404423280119238521)
XLA Ops:
  0.0 0.9 %slice_bitcast_fusion.3 = (f32[2,64,64]{2,1,0:T(8,128)S(1)}, f32[2,64,64]{2,1,0:T(8,128)S(1)}) fusion(f32[2,2,64,64]{3,2,1,0:T(8,128)} %param.7), kind=kLoop, calls=%fused_computation.31 | loop fusion | bytes 131072 | tf_op jit(solution)/shard_map/squeeze | solution.py:350
  1.1 3.0 %collective-permute-start = (f32[2,64,128]{2,1,0:T(8,128)S(1)}, f32[2,64,128]{2,1,0:T(8,128)S(1)}, u32[]{:S(2)}, u32[]{:S(2)}) collective-permute-start(f32[2,64,128]{2,1,0:T(8,128)S(1)} %pad_maximum_fusion.3), channel_id=1, source_target_pairs={{0,8},{1,9},{2,10},{3,11},{4,12},{5,13},{6,14},{7,15},{8,0},{9,1},... | collective-permute-start | bytes 196616 | tf_op jit(solution)/shard_map/ppermute | solution.py:277
  4.1 1.5 %collective-permute-start.1 = (f32[2,64,128]{2,1,0:T(8,128)S(1)}, f32[2,64,128]{2,1,0:T(8,128)S(1)}, u32[]{:S(2)}, u32[]{:S(2)}) collective-permute-start(f32[2,64,128]{2,1,0:T(8,128)S(1)} %pad_maximum_fusion.3), channel_id=1, source_target_pairs={{0,24},{1,25},{2,26},{3,27},{4,28},{5,29},{6,30},{7,31},{8,16},{9,... | collective-permute-start | bytes 196616 | tf_op jit(solution)/shard_map/ppermute | solution.py:277
  5.6 1.5 %collective-permute-start.2 = (f32[2,64,128]{2,1,0:T(8,128)S(1)}, f32[2,64,128]{2,1,0:T(8,128)S(1)}, u32[]{:S(2)}, u32[]{:S(2)}) collective-permute-start(f32[2,64,128]{2,1,0:T(8,128)S(1)} %pad_maximum_fusion.3), channel_id=1, source_target_pairs={{0,8},{1,10},{2,9},{3,12},{4,11},{5,14},{6,13},{7,15},{8,0},{9,2},... | collective-permute-start | bytes 196616 | tf_op jit(solution)/shard_map/ppermute | solution.py:277
  7.1 1.9 %collective-permute-start.4 = (f32[2,64,128]{2,1,0:T(8,128)S(1)}, f32[2,64,128]{2,1,0:T(8,128)S(1)}, u32[]{:S(2)}, u32[]{:S(2)}) collective-permute-start(f32[2,64,128]{2,1,0:T(8,128)S(1)} %pad_maximum_fusion.3), channel_id=1, source_target_pairs={{0,8},{1,2},{2,1},{3,4},{4,3},{5,6},{6,5},{7,15},{8,0},{9,10},{10,... | collective-permute-start | bytes 196616 | tf_op jit(solution)/shard_map/ppermute | solution.py:277
  9.7 0.9 %copy-done.2 = f32[2,128,128]{2,1,0:T(8,128)S(1)} copy-done((f32[2,128,128]{2,1,0:T(8,128)S(1)}, f32[2,128,128]{2,1,0:T(8,128)}, u32[]{:S(2)}) %copy-start.2) | copy-done | bytes 131096
  10.6 0.9 %prepare.1 = (f32[4,128,128]{2,1,0:T(8,128)S(1)}, f32[6,128,128]{2,1,0:T(8,128)S(1)}, s32[8,128]{1,0:T(8,128)S(1)}) custom-call(s32[2,6]{1,0:T(2,128)S(1)} %bitcast.13, s32[1,1]{1,0:T(1,128)S(6)} %copy.8.count, f32[128,128]{1,0:T(8,128)S(1)} %copy-done.3, f32[2,128,128]{2,1,0:T(8,128)S(1)} %copy-done.2, f32[6,128,128]{2,1,0:T(8,128)S(1)} %bitcast.12), custom_call_target="tpu_custom_call" | custom-call | tf_op jit(solution)/shard_map/prepare/pallas_call | solution.py:78
  11.6 0.9 %collective-permute-start.5 = (f32[2,192,128]{2,1,0:T(8,128)S(1)}, f32[2,192,128]{2,1,0:T(8,128)S(1)}, u32[]{:S(2)}, u32[]{:S(2)}) collective-permute-start(f32[2,192,128]{2,1,0:T(8,128)S(1)} %pad_maximum_fusion.mid_ref), channel_id=1, source_target_pairs={{0,1},{1,0},{2,3},{3,2},{4,5},{5,4},{6,7},{7,6},{8,9},{9,8},{10,11... | collective-permute-start | bytes 589832 | tf_op jit(solution)/shard_map/ppermute | solution.py:277
  12.6 1.0 %collective-permute-done.5.near_ref = f32[2,192,128]{2,1,0:T(8,128)S(1)} collective-permute-done((f32[2,192,128]{2,1,0:T(8,128)S(1)}, f32[2,192,128]{2,1,0:T(8,128)S(1)}, u32[]{:S(2)}, u32[]{:S(2)}) %collective-permute-start.5) | collective-permute-done | bytes 196640 | tf_op jit(solution)/shard_map/ppermute | solution.py:277
  13.6 5.8 %tile_gradient.2 = (f32[2,192,128]{2,1,0:T(8,128)S(1)}, f32[2,192,128]{2,1,0:T(8,128)S(1)}, f32[2,192,128]{2,1,0:T(8,128)S(1)}) custom-call(s32[8,128]{1,0:T(8,128)S(1)} %get-tuple-element.14.plan, f32[2,192,128]{2,1,0:T(8,128)S(1)} %pad_maximum_fusion.1.far_ref, f32[2,192,128]{2,1,0:T(8,128)S(1)} %pad_maximum_fusion.mid_ref, ...), custom_call_target="tpu_custom_call" | custom-call | tf_op jit(solution)/shard_map/tile_gradient/pallas_call | solution.py:259
  19.4 0.4 collective-permute-start.6
  19.9 1.5 %collective-permute-start.7 = (f32[2,192,128]{2,1,0:T(8,128)S(1)}, f32[2,192,128]{2,1,0:T(8,128)S(1)}, u32[]{:S(2)}, u32[]{:S(2)}) collective-permute-start(f32[2,192,128]{2,1,0:T(8,128)S(1)} %get-tuple-element.19), channel_id=1, source_target_pairs={{0,8},{1,2},{2,1},{3,4},{4,3},{5,6},{6,5},{7,15},{8,0},{9,10},{10,... | collective-permute-start | bytes 589832 | tf_op jit(solution)/shard_map/ppermute | solution.py:277
  21.4 4.2 %collective-permute-done.7 = f32[2,192,128]{2,1,0:T(8,128)S(1)} collective-permute-done((f32[2,192,128]{2,1,0:T(8,128)S(1)}, f32[2,192,128]{2,1,0:T(8,128)S(1)}, u32[]{:S(2)}, u32[]{:S(2)}) %collective-permute-start.7) | collective-permute-done | bytes 196640 | tf_op jit(solution)/shard_map/ppermute | solution.py:277
  25.6 1.6 %collective-permute-start.8 = (f32[2,128,128]{2,1,0:T(8,128)S(1)}, f32[2,128,128]{2,1,0:T(8,128)S(1)}, u32[]{:S(2)}, u32[]{:S(2)}) collective-permute-start(f32[2,128,128]{2,1,0:T(8,128)S(1)} %get-tuple-element.33), channel_id=1, source_target_pairs={{0,8},{1,9},{2,10},{3,11},{4,12},{5,13},{6,14},{7,15},{8,0},{9,1},... | collective-permute-start | bytes 393224 | tf_op jit(solution)/shard_map/ppermute | solution.py:277
  27.2 1.5 %collective-permute-start.9 = (f32[2,128,128]{2,1,0:T(8,128)S(1)}, f32[2,128,128]{2,1,0:T(8,128)S(1)}, u32[]{:S(2)}, u32[]{:S(2)}) collective-permute-start(f32[2,128,128]{2,1,0:T(8,128)S(1)} %get-tuple-element.34), channel_id=1, source_target_pairs={{0,24},{1,25},{2,26},{3,27},{4,28},{5,29},{6,30},{7,31},{8,16},{9,... | collective-permute-start | bytes 393224 | tf_op jit(solution)/shard_map/ppermute | solution.py:277
  28.7 0.6 collective-permute-start.10
  29.2 2.3 %collective-permute-done.8 = f32[2,128,128]{2,1,0:T(8,128)S(1)} collective-permute-done((f32[2,128,128]{2,1,0:T(8,128)S(1)}, f32[2,128,128]{2,1,0:T(8,128)S(1)}, u32[]{:S(2)}, u32[]{:S(2)}) %collective-permute-start.8) | collective-permute-done | bytes 131104 | tf_op jit(solution)/shard_map/ppermute | solution.py:277
  31.5 3.3 %collective-permute-done.9 = f32[2,128,128]{2,1,0:T(8,128)S(1)} collective-permute-done((f32[2,128,128]{2,1,0:T(8,128)S(1)}, f32[2,128,128]{2,1,0:T(8,128)S(1)}, u32[]{:S(2)}, u32[]{:S(2)}) %collective-permute-start.9) | collective-permute-done | bytes 131104 | tf_op jit(solution)/shard_map/ppermute | solution.py:277
  34.8 0.2 collective-permute-done.10
  35.2 1.6 %collective-permute-start.11 = (f32[2,192,128]{2,1,0:T(8,128)S(1)}, f32[2,192,128]{2,1,0:T(8,128)S(1)}, u32[]{:S(2)}, u32[]{:S(2)}) collective-permute-start(f32[2,192,128]{2,1,0:T(8,128)S(1)} %fusion.mid_ref), channel_id=1, source_target_pairs={{0,8},{1,2},{2,1},{3,4},{4,3},{5,6},{6,5},{7,15},{8,0},{9,10},{10,... | collective-permute-start | bytes 589832 | tf_op jit(solution)/shard_map/ppermute | solution.py:277
  36.8 4.1 %collective-permute-done.11.far_ref = f32[2,192,128]{2,1,0:T(8,128)S(1)} collective-permute-done((f32[2,192,128]{2,1,0:T(8,128)S(1)}, f32[2,192,128]{2,1,0:T(8,128)S(1)}, u32[]{:S(2)}, u32[]{:S(2)}) %collective-permute-start.11) | collective-permute-done | bytes 196640 | tf_op jit(solution)/shard_map/ppermute | solution.py:277
  40.9 5.8 %tile_gradient.3 = (f32[2,192,128]{2,1,0:T(8,128)S(1)}, f32[2,192,128]{2,1,0:T(8,128)S(1)}, f32[2,192,128]{2,1,0:T(8,128)S(1)}) custom-call(s32[8,128]{1,0:T(8,128)S(1)} %get-tuple-element.14.plan, f32[2,192,128]{2,1,0:T(8,128)S(1)} %collective-permute-done.11.far_ref, f32[2,192,128]{2,1,0:T(8,128)S(1)} %fusion.mid_ref, ...), custom_call_target="tpu_custom_call" | custom-call | tf_op jit(solution)/shard_map/tile_gradient/pallas_call | solution.py:259
  46.9 1.6 %collective-permute-start.14 = (f32[2,64,128]{2,1,0:T(8,128)S(1)}, f32[2,64,128]{2,1,0:T(8,128)S(1)}, u32[]{:S(2)}, u32[]{:S(2)}) collective-permute-start(f32[2,64,128]{2,1,0:T(8,128)S(1)} %get-tuple-element.28), channel_id=1, source_target_pairs={{0,8},{1,2},{2,1},{3,4},{4,3},{5,6},{6,5},{7,15},{8,0},{9,10},{10,... | collective-permute-start | bytes 196616 | tf_op jit(solution)/shard_map/ppermute | solution.py:277
  48.5 0.5 collective-permute-start.15
  49.0 1.5 %collective-permute-start.16 = (f32[2,64,128]{2,1,0:T(8,128)S(1)}, f32[2,64,128]{2,1,0:T(8,128)S(1)}, u32[]{:S(2)}, u32[]{:S(2)}) collective-permute-start(f32[2,64,128]{2,1,0:T(8,128)S(1)} %get-tuple-element.30), channel_id=1, source_target_pairs={{0,24},{1,26},{2,25},{3,28},{4,27},{5,30},{6,29},{7,31},{8,16},{9,... | collective-permute-start | bytes 196616 | tf_op jit(solution)/shard_map/ppermute | solution.py:277
  50.5 0.8 %collective-permute-start.17 = (f32[2,64,128]{2,1,0:T(8,128)S(1)}, f32[2,64,128]{2,1,0:T(8,128)S(1)}, u32[]{:S(2)}, u32[]{:S(2)}) collective-permute-start(f32[2,64,128]{2,1,0:T(8,128)S(1)} %get-tuple-element.31), channel_id=1, source_target_pairs={{0,8},{1,9},{2,10},{3,11},{4,12},{5,13},{6,14},{7,15},{8,0},{9,1},... | collective-permute-start | bytes 196616 | tf_op jit(solution)/shard_map/ppermute | solution.py:277
  51.3 2.3 %collective-permute-start.18 = (f32[2,64,128]{2,1,0:T(8,128)S(1)}, f32[2,64,128]{2,1,0:T(8,128)S(1)}, u32[]{:S(2)}, u32[]{:S(2)}) collective-permute-start(f32[2,64,128]{2,1,0:T(8,128)S(1)} %get-tuple-element.32), channel_id=1, source_target_pairs={{0,24},{1,25},{2,26},{3,27},{4,28},{5,29},{6,30},{7,31},{8,16},{9,... | collective-permute-start | bytes 196616 | tf_op jit(solution)/shard_map/ppermute | solution.py:277
  53.6 0.1 collective-permute-done.15
  53.7 0.4 collective-permute-done.16
  54.1 2.8 %collective-permute-done.17 = f32[2,64,128]{2,1,0:T(8,128)S(1)} collective-permute-done((f32[2,64,128]{2,1,0:T(8,128)S(1)}, f32[2,64,128]{2,1,0:T(8,128)S(1)}, u32[]{:S(2)}, u32[]{:S(2)}) %collective-permute-start.17) | collective-permute-done | bytes 65568 | tf_op jit(solution)/shard_map/ppermute | solution.py:277
  57.0 0.9 %collective-permute-done.18 = f32[2,64,128]{2,1,0:T(8,128)S(1)} collective-permute-done((f32[2,64,128]{2,1,0:T(8,128)S(1)}, f32[2,64,128]{2,1,0:T(8,128)S(1)}, u32[]{:S(2)}, u32[]{:S(2)}) %collective-permute-start.18) | collective-permute-done | bytes 65568 | tf_op jit(solution)/shard_map/ppermute | solution.py:277
  58.1 0.7 %pad_maximum_fusion.2 = f32[2,2,64,64]{3,2,1,0:T(8,128)} fusion(f32[1,2,64,64]{3,2,1,0:T(8,128)S(1)} %get-tuple-element.42, f32[1,2,64,64]{3,2,1,0:T(8,128)S(1)} %get-tuple-element.41), kind=kLoop, calls=%fused_computation.5 | loop fusion | flops 16384 | bytes 131072 | tf_op jit(solution)/shard_map/stack | solution.py:390
  (37 shorter events, 0.8 us)
Async XLA Ops:
  0.0 9.7 %copy-start.1 = (f32[1,1,6,128,128]{4,3,2,1,0:T(8,128)S(1)}, f32[1,1,6,128,128]{4,3,2,1,0:T(8,128)}, u32[]{:S(2)}) copy-start(f32[1,1,6,128,128]{4,3,2,1,0:T(8,128)} %param.12) | copy-start | bytes 1179652
  0.9 8.8 %copy-start.3 = (f32[128,128]{1,0:T(8,128)S(1)}, f32[128,128]{1,0:T(8,128)}, u32[]{:S(2)}) copy-start(f32[128,128]{1,0:T(8,128)} %phase_ref.1) | copy-start | bytes 196612
  0.9 8.8 %copy-start.4 = (s32[1,1,6,2]{2,3,1,0:T(2,128)S(1)}, s32[1,1,6,2]{2,3,1,0:T(2,128)}, u32[]{:S(2)}) copy-start(s32[1,1,6,2]{2,3,1,0:T(2,128)} %param.10) | copy-start | bytes 148
  1.1 12.5 %copy-start = (bf16[8,256,256]{2,1,0:T(8,128)(2,1)S(1)}, bf16[8,256,256]{2,1,0:T(8,128)(2,1)}, u32[]{:S(2)}) copy-start(bf16[8,256,256]{2,1,0:T(8,128)(2,1)} %constant.26.clone.table_ref) | copy-start | bytes 3145732
  1.1 10.4 %collective-permute-start = (f32[2,64,128]{2,1,0:T(8,128)S(1)}, f32[2,64,128]{2,1,0:T(8,128)S(1)}, u32[]{:S(2)}, u32[]{:S(2)}) collective-permute-start(f32[2,64,128]{2,1,0:T(8,128)S(1)} %pad_maximum_fusion.3), channel_id=1, source_target_pairs={{0,8},{1,9},{2,10},{3,11},{4,12},{5,13},{6,14},{7,15},{8,0},{9,1},... | collective-permute-start | bytes 196616 | tf_op jit(solution)/shard_map/ppermute | solution.py:277
  4.1 7.4 %collective-permute-start.1 = (f32[2,64,128]{2,1,0:T(8,128)S(1)}, f32[2,64,128]{2,1,0:T(8,128)S(1)}, u32[]{:S(2)}, u32[]{:S(2)}) collective-permute-start(f32[2,64,128]{2,1,0:T(8,128)S(1)} %pad_maximum_fusion.3), channel_id=1, source_target_pairs={{0,24},{1,25},{2,26},{3,27},{4,28},{5,29},{6,30},{7,31},{8,16},{9,... | collective-permute-start | bytes 196616 | tf_op jit(solution)/shard_map/ppermute | solution.py:277
  5.6 6.9 %collective-permute-start.2 = (f32[2,64,128]{2,1,0:T(8,128)S(1)}, f32[2,64,128]{2,1,0:T(8,128)S(1)}, u32[]{:S(2)}, u32[]{:S(2)}) collective-permute-start(f32[2,64,128]{2,1,0:T(8,128)S(1)} %pad_maximum_fusion.3), channel_id=1, source_target_pairs={{0,8},{1,10},{2,9},{3,12},{4,11},{5,14},{6,13},{7,15},{8,0},{9,2},... | collective-permute-start | bytes 196616 | tf_op jit(solution)/shard_map/ppermute | solution.py:277
  7.1 5.5 %collective-permute-start.3 = (f32[2,64,128]{2,1,0:T(8,128)S(1)}, f32[2,64,128]{2,1,0:T(8,128)S(1)}, u32[]{:S(2)}, u32[]{:S(2)}) collective-permute-start(f32[2,64,128]{2,1,0:T(8,128)S(1)} %pad_maximum_fusion.3), channel_id=1, source_target_pairs={{0,24},{1,26},{2,25},{3,28},{4,27},{5,30},{6,29},{7,31},{8,16},{9,... | collective-permute-start | bytes 196616 | tf_op jit(solution)/shard_map/ppermute | solution.py:277
  7.1 5.5 %collective-permute-start.4 = (f32[2,64,128]{2,1,0:T(8,128)S(1)}, f32[2,64,128]{2,1,0:T(8,128)S(1)}, u32[]{:S(2)}, u32[]{:S(2)}) collective-permute-start(f32[2,64,128]{2,1,0:T(8,128)S(1)} %pad_maximum_fusion.3), channel_id=1, source_target_pairs={{0,8},{1,2},{2,1},{3,4},{4,3},{5,6},{6,5},{7,15},{8,0},{9,10},{10,... | collective-permute-start | bytes 196616 | tf_op jit(solution)/shard_map/ppermute | solution.py:277
  9.7 0.9 %copy-start.2 = (f32[2,128,128]{2,1,0:T(8,128)S(1)}, f32[2,128,128]{2,1,0:T(8,128)}, u32[]{:S(2)}) copy-start(f32[2,128,128]{2,1,0:T(8,128)} %probe_ref.1) | copy-start | bytes 393220
  11.6 2.0 %collective-permute-start.5 = (f32[2,192,128]{2,1,0:T(8,128)S(1)}, f32[2,192,128]{2,1,0:T(8,128)S(1)}, u32[]{:S(2)}, u32[]{:S(2)}) collective-permute-start(f32[2,192,128]{2,1,0:T(8,128)S(1)} %pad_maximum_fusion.mid_ref), channel_id=1, source_target_pairs={{0,1},{1,0},{2,3},{3,2},{4,5},{5,4},{6,7},{7,6},{8,9},{9,8},{10,11... | collective-permute-start | bytes 589832 | tf_op jit(solution)/shard_map/ppermute | solution.py:277
  19.4 1.9 %collective-permute-start.6 = (f32[2,192,128]{2,1,0:T(8,128)S(1)}, f32[2,192,128]{2,1,0:T(8,128)S(1)}, u32[]{:S(2)}, u32[]{:S(2)}) collective-permute-start(f32[2,192,128]{2,1,0:T(8,128)S(1)} %get-tuple-element.18), channel_id=1, source_target_pairs={{0,1},{1,0},{2,3},{3,2},{4,5},{5,4},{6,7},{7,6},{8,9},{9,8},{10,11... | collective-permute-start | bytes 589832 | tf_op jit(solution)/shard_map/ppermute | solution.py:277
  19.9 5.7 %collective-permute-start.7 = (f32[2,192,128]{2,1,0:T(8,128)S(1)}, f32[2,192,128]{2,1,0:T(8,128)S(1)}, u32[]{:S(2)}, u32[]{:S(2)}) collective-permute-start(f32[2,192,128]{2,1,0:T(8,128)S(1)} %get-tuple-element.19), channel_id=1, source_target_pairs={{0,8},{1,2},{2,1},{3,4},{4,3},{5,6},{6,5},{7,15},{8,0},{9,10},{10,... | collective-permute-start | bytes 589832 | tf_op jit(solution)/shard_map/ppermute | solution.py:277
  25.6 5.9 %collective-permute-start.8 = (f32[2,128,128]{2,1,0:T(8,128)S(1)}, f32[2,128,128]{2,1,0:T(8,128)S(1)}, u32[]{:S(2)}, u32[]{:S(2)}) collective-permute-start(f32[2,128,128]{2,1,0:T(8,128)S(1)} %get-tuple-element.33), channel_id=1, source_target_pairs={{0,8},{1,9},{2,10},{3,11},{4,12},{5,13},{6,14},{7,15},{8,0},{9,1},... | collective-permute-start | bytes 393224 | tf_op jit(solution)/shard_map/ppermute | solution.py:277
  27.2 7.7 %collective-permute-start.9 = (f32[2,128,128]{2,1,0:T(8,128)S(1)}, f32[2,128,128]{2,1,0:T(8,128)S(1)}, u32[]{:S(2)}, u32[]{:S(2)}) collective-permute-start(f32[2,128,128]{2,1,0:T(8,128)S(1)} %get-tuple-element.34), channel_id=1, source_target_pairs={{0,24},{1,25},{2,26},{3,27},{4,28},{5,29},{6,30},{7,31},{8,16},{9,... | collective-permute-start | bytes 393224 | tf_op jit(solution)/shard_map/ppermute | solution.py:277
  28.7 6.4 %collective-permute-start.10 = (f32[2,64,128]{2,1,0:T(8,128)S(1)}, f32[2,64,128]{2,1,0:T(8,128)S(1)}, u32[]{:S(2)}, u32[]{:S(2)}) collective-permute-start(f32[2,64,128]{2,1,0:T(8,128)S(1)} %slice_select_fusion.4), channel_id=1, source_target_pairs={{0,16},{1,17},{2,18},{3,19},{4,20},{5,21},{6,22},{7,23},{8,24},{9,... | collective-permute-start | bytes 196616 | tf_op jit(solution)/shard_map/ppermute | solution.py:277
  35.2 5.7 %collective-permute-start.11 = (f32[2,192,128]{2,1,0:T(8,128)S(1)}, f32[2,192,128]{2,1,0:T(8,128)S(1)}, u32[]{:S(2)}, u32[]{:S(2)}) collective-permute-start(f32[2,192,128]{2,1,0:T(8,128)S(1)} %fusion.mid_ref), channel_id=1, source_target_pairs={{0,8},{1,2},{2,1},{3,4},{4,3},{5,6},{6,5},{7,15},{8,0},{9,10},{10,... | collective-permute-start | bytes 589832 | tf_op jit(solution)/shard_map/ppermute | solution.py:277
  36.8 4.1 %collective-permute-start.12 = (f32[2,192,128]{2,1,0:T(8,128)S(1)}, f32[2,192,128]{2,1,0:T(8,128)S(1)}, u32[]{:S(2)}, u32[]{:S(2)}) collective-permute-start(f32[2,192,128]{2,1,0:T(8,128)S(1)} %fusion.mid_ref), channel_id=1, source_target_pairs={{0,1},{1,0},{2,3},{3,2},{4,5},{5,4},{6,7},{7,6},{8,9},{9,8},{10,11... | collective-permute-start | bytes 589832 | tf_op jit(solution)/shard_map/ppermute | solution.py:277
  46.8 3.7 %collective-permute-start.13 = (f32[2,192,128]{2,1,0:T(8,128)S(1)}, f32[2,192,128]{2,1,0:T(8,128)S(1)}, u32[]{:S(2)}, u32[]{:S(2)}) collective-permute-start(f32[2,192,128]{2,1,0:T(8,128)S(1)} %get-tuple-element.21), channel_id=1, source_target_pairs={{0,1},{1,0},{2,3},{3,2},{4,5},{5,4},{6,7},{7,6},{8,9},{9,8},{10,11... | collective-permute-start | bytes 589832 | tf_op jit(solution)/shard_map/ppermute | solution.py:277
  46.9 6.7 %collective-permute-start.14 = (f32[2,64,128]{2,1,0:T(8,128)S(1)}, f32[2,64,128]{2,1,0:T(8,128)S(1)}, u32[]{:S(2)}, u32[]{:S(2)}) collective-permute-start(f32[2,64,128]{2,1,0:T(8,128)S(1)} %get-tuple-element.28), channel_id=1, source_target_pairs={{0,8},{1,2},{2,1},{3,4},{4,3},{5,6},{6,5},{7,15},{8,0},{9,10},{10,... | collective-permute-start | bytes 196616 | tf_op jit(solution)/shard_map/ppermute | solution.py:277
  48.5 5.2 %collective-permute-start.15 = (f32[2,64,128]{2,1,0:T(8,128)S(1)}, f32[2,64,128]{2,1,0:T(8,128)S(1)}, u32[]{:S(2)}, u32[]{:S(2)}) collective-permute-start(f32[2,64,128]{2,1,0:T(8,128)S(1)} %get-tuple-element.29), channel_id=1, source_target_pairs={{0,8},{1,10},{2,9},{3,12},{4,11},{5,14},{6,13},{7,15},{8,0},{9,2},... | collective-permute-start | bytes 196616 | tf_op jit(solution)/shard_map/ppermute | solution.py:277
  49.0 5.2 %collective-permute-start.16 = (f32[2,64,128]{2,1,0:T(8,128)S(1)}, f32[2,64,128]{2,1,0:T(8,128)S(1)}, u32[]{:S(2)}, u32[]{:S(2)}) collective-permute-start(f32[2,64,128]{2,1,0:T(8,128)S(1)} %get-tuple-element.30), channel_id=1, source_target_pairs={{0,24},{1,26},{2,25},{3,28},{4,27},{5,30},{6,29},{7,31},{8,16},{9,... | collective-permute-start | bytes 196616 | tf_op jit(solution)/shard_map/ppermute | solution.py:277
  50.5 6.5 %collective-permute-start.17 = (f32[2,64,128]{2,1,0:T(8,128)S(1)}, f32[2,64,128]{2,1,0:T(8,128)S(1)}, u32[]{:S(2)}, u32[]{:S(2)}) collective-permute-start(f32[2,64,128]{2,1,0:T(8,128)S(1)} %get-tuple-element.31), channel_id=1, source_target_pairs={{0,8},{1,9},{2,10},{3,11},{4,12},{5,13},{6,14},{7,15},{8,0},{9,1},... | collective-permute-start | bytes 196616 | tf_op jit(solution)/shard_map/ppermute | solution.py:277
  51.3 6.6 %collective-permute-start.18 = (f32[2,64,128]{2,1,0:T(8,128)S(1)}, f32[2,64,128]{2,1,0:T(8,128)S(1)}, u32[]{:S(2)}, u32[]{:S(2)}) collective-permute-start(f32[2,64,128]{2,1,0:T(8,128)S(1)} %get-tuple-element.32), channel_id=1, source_target_pairs={{0,24},{1,25},{2,26},{3,27},{4,28},{5,29},{6,30},{7,31},{8,16},{9,... | collective-permute-start | bytes 196616 | tf_op jit(solution)/shard_map/ppermute | solution.py:277

commit v6 on v5

--- a/solution.py
+++ b/solution.py
@@ -287,10 +287,14 @@
         to_col = col + 1 if col % 2 else col - 1
         inside = 0 <= to_col < broad
         if inside:
-            return rows(row), to_col
-        return (row ^ 1 if rows is same_row else rows(row)), col
+            return (row if is_end(rows, row) else rows(row)), to_col
+        return row ^ (2 if lax.axis_size("ty") > 2 else 1), col
 
     return partner
+
+
+def is_end(rows, row):
+    return rows is row_cross and row in (0, lax.axis_size("ty") - 1)
 
 
 def same_row(row):
@@ -314,7 +318,7 @@
 
 
 def within_column(rows):
-    return lambda row, col: (rows(row), col)
+    return lambda row, col: (row, col ^ 1) if is_end(rows, row) else (rows(row), col)
 
 
 def on_device(

time: 58.9 us -> 55.3 us (0.939)
  starting transfers between devices: 22.7 us -> 20.6 us
  waiting for transfers between devices: 19.5 us -> 18 us
    ppermute x19, starting transfers between devices: 22.7 us -> 20.6 us  [exchange(): return lax.ppermute(shard, ('ty', 'tx'), pairs)]
    ppermute x19, waiting for transfers between devices: 19.5 us -> 18 us  [exchange(): return lax.ppermute(shard, ('ty', 'tx'), pairs)]
  transfers between devices with their start and end apart: 19 -> 19, of which waited for: 10 -> 9; matrix products, arithmetic and copies ran while one was open for 0% -> 0% of each run, Pallas kernels for 1% -> 2%
where the time goes in v6:
time: 55.3 us; the launch traced here: 55.2 us
  starting transfers between devices  20.6 us (37%)
  waiting for transfers between devices  18 us (33%)
  Pallas kernels  12.5 us (23%)
  local copies, waits for them, and re-layouts  1.93 us (3%)
  other arithmetic  1.21 us (2%)
  between operations  0.88 us (2%)
    ppermute x19, starting transfers between devices, exchange(): return lax.ppermute(shard, ('ty', 'tx'), pairs)  20.6 us
    ppermute x19, waiting for transfers between devices, exchange(): return lax.ppermute(shard, ('ty', 'tx'), pairs)  18 us
    pallas_call x2, Pallas kernels, tile_gradient(): pl.pallas_call(gradient_kernel, out_shape=(strip, strip, strip), in_specs...  11.7 us
  transfers between devices with their start and end apart: 19, of which 9 were waited for; matrix products, arithmetic and copies ran while one was open for 0% of the time, Pallas kernels for 2%

profile of v6, /device:TPU:0, one launch (start us, length us, event | category | flops | bytes accessed | tf_op | source)
XLA Modules:
  0.0 55.2 jit_solution(3421059350318653654)
XLA Ops:
  0.0 0.9 %slice_bitcast_fusion.3 = (f32[2,64,64]{2,1,0:T(8,128)S(1)}, f32[2,64,64]{2,1,0:T(8,128)S(1)}) fusion(f32[2,2,64,64]{3,2,1,0:T(8,128)} %param.7), kind=kLoop, calls=%fused_computation.31 | loop fusion | bytes 131072 | tf_op jit(solution)/shard_map/squeeze | solution.py:354
  1.0 0.1 pad_maximum_fusion.3
  1.1 3.0 %collective-permute-start = (f32[2,64,128]{2,1,0:T(8,128)S(1)}, f32[2,64,128]{2,1,0:T(8,128)S(1)}, u32[]{:S(2)}, u32[]{:S(2)}) collective-permute-start(f32[2,64,128]{2,1,0:T(8,128)S(1)} %pad_maximum_fusion.3), channel_id=1, source_target_pairs={{0,8},{1,9},{2,10},{3,11},{4,12},{5,13},{6,14},{7,15},{8,0},{9,1},... | collective-permute-start | bytes 196616 | tf_op jit(solution)/shard_map/ppermute | solution.py:277
  4.1 1.5 %collective-permute-start.2 = (f32[2,64,128]{2,1,0:T(8,128)S(1)}, f32[2,64,128]{2,1,0:T(8,128)S(1)}, u32[]{:S(2)}, u32[]{:S(2)}) collective-permute-start(f32[2,64,128]{2,1,0:T(8,128)S(1)} %pad_maximum_fusion.3), channel_id=1, source_target_pairs={{0,16},{1,10},{2,9},{3,12},{4,11},{5,14},{6,13},{7,23},{8,24},{9,2... | collective-permute-start | bytes 196616 | tf_op jit(solution)/shard_map/ppermute | solution.py:277
  5.6 0.5 collective-permute-start.3
  6.1 1.5 %collective-permute-start.4 = (f32[2,64,128]{2,1,0:T(8,128)S(1)}, f32[2,64,128]{2,1,0:T(8,128)S(1)}, u32[]{:S(2)}, u32[]{:S(2)}) collective-permute-start(f32[2,64,128]{2,1,0:T(8,128)S(1)} %pad_maximum_fusion.3), channel_id=1, source_target_pairs={{0,16},{1,2},{2,1},{3,4},{4,3},{5,6},{6,5},{7,23},{8,24},{9,10},{1... | collective-permute-start | bytes 196616 | tf_op jit(solution)/shard_map/ppermute | solution.py:277
  8.4 0.9 %copy-done.2 = f32[2,128,128]{2,1,0:T(8,128)S(1)} copy-done((f32[2,128,128]{2,1,0:T(8,128)S(1)}, f32[2,128,128]{2,1,0:T(8,128)}, u32[]{:S(2)}) %copy-start.2) | copy-done | bytes 131096
  9.3 0.9 %prepare.1 = (f32[4,128,128]{2,1,0:T(8,128)S(1)}, f32[6,128,128]{2,1,0:T(8,128)S(1)}, s32[8,128]{1,0:T(8,128)S(1)}) custom-call(s32[2,6]{1,0:T(2,128)S(1)} %bitcast.13, s32[1,1]{1,0:T(1,128)S(6)} %copy.8.count, f32[128,128]{1,0:T(8,128)S(1)} %copy-done.3, f32[2,128,128]{2,1,0:T(8,128)S(1)} %copy-done.2, f32[6,128,128]{2,1,0:T(8,128)S(1)} %bitcast.12), custom_call_target="tpu_custom_call" | custom-call | tf_op jit(solution)/shard_map/prepare/pallas_call | solution.py:78
  10.2 0.1 pad_maximum_fusion.mid_ref
  10.3 2.4 %collective-permute-start.5 = (f32[2,192,128]{2,1,0:T(8,128)S(1)}, f32[2,192,128]{2,1,0:T(8,128)S(1)}, u32[]{:S(2)}, u32[]{:S(2)}) collective-permute-start(f32[2,192,128]{2,1,0:T(8,128)S(1)} %pad_maximum_fusion.mid_ref), channel_id=1, source_target_pairs={{0,1},{1,0},{2,3},{3,2},{4,5},{5,4},{6,7},{7,6},{8,9},{9,8},{10,11... | collective-permute-start | bytes 589832 | tf_op jit(solution)/shard_map/ppermute | solution.py:277
  12.7 1.0 %collective-permute-done.5.near_ref = f32[2,192,128]{2,1,0:T(8,128)S(1)} collective-permute-done((f32[2,192,128]{2,1,0:T(8,128)S(1)}, f32[2,192,128]{2,1,0:T(8,128)S(1)}, u32[]{:S(2)}, u32[]{:S(2)}) %collective-permute-start.5) | collective-permute-done | bytes 196640 | tf_op jit(solution)/shard_map/ppermute | solution.py:277
  13.7 5.8 %tile_gradient.2 = (f32[2,192,128]{2,1,0:T(8,128)S(1)}, f32[2,192,128]{2,1,0:T(8,128)S(1)}, f32[2,192,128]{2,1,0:T(8,128)S(1)}) custom-call(s32[8,128]{1,0:T(8,128)S(1)} %get-tuple-element.14.plan, f32[2,192,128]{2,1,0:T(8,128)S(1)} %pad_maximum_fusion.1.far_ref, f32[2,192,128]{2,1,0:T(8,128)S(1)} %pad_maximum_fusion.mid_ref, ...), custom_call_target="tpu_custom_call" | custom-call | tf_op jit(solution)/shard_map/tile_gradient/pallas_call | solution.py:259
  19.5 0.4 collective-permute-start.6
  19.9 1.1 %collective-permute-done.6 = f32[2,192,128]{2,1,0:T(8,128)S(1)} collective-permute-done((f32[2,192,128]{2,1,0:T(8,128)S(1)}, f32[2,192,128]{2,1,0:T(8,128)S(1)}, u32[]{:S(2)}, u32[]{:S(2)}) %collective-permute-start.6) | collective-permute-done | bytes 196640 | tf_op jit(solution)/shard_map/ppermute | solution.py:277
  21.0 4.6 %collective-permute-done.7 = f32[2,192,128]{2,1,0:T(8,128)S(1)} collective-permute-done((f32[2,192,128]{2,1,0:T(8,128)S(1)}, f32[2,192,128]{2,1,0:T(8,128)S(1)}, u32[]{:S(2)}, u32[]{:S(2)}) %collective-permute-start.7) | collective-permute-done | bytes 196640 | tf_op jit(solution)/shard_map/ppermute | solution.py:277
  25.8 0.1 collective-permute-start.9
  25.9 3.5 %collective-permute-start.10 = (f32[2,64,128]{2,1,0:T(8,128)S(1)}, f32[2,64,128]{2,1,0:T(8,128)S(1)}, u32[]{:S(2)}, u32[]{:S(2)}) collective-permute-start(f32[2,64,128]{2,1,0:T(8,128)S(1)} %slice_select_fusion.4), channel_id=1, source_target_pairs={{0,16},{1,17},{2,18},{3,19},{4,20},{5,21},{6,22},{7,23},{8,24},{9,... | collective-permute-start | bytes 196616 | tf_op jit(solution)/shard_map/ppermute | solution.py:277
  29.3 2.8 %collective-permute-done.8 = f32[2,128,128]{2,1,0:T(8,128)S(1)} collective-permute-done((f32[2,128,128]{2,1,0:T(8,128)S(1)}, f32[2,128,128]{2,1,0:T(8,128)S(1)}, u32[]{:S(2)}, u32[]{:S(2)}) %collective-permute-start.8) | collective-permute-done | bytes 131104 | tf_op jit(solution)/shard_map/ppermute | solution.py:277
  32.1 1.0 %collective-permute-done.10 = f32[2,64,128]{2,1,0:T(8,128)S(1)} collective-permute-done((f32[2,64,128]{2,1,0:T(8,128)S(1)}, f32[2,64,128]{2,1,0:T(8,128)S(1)}, u32[]{:S(2)}, u32[]{:S(2)}) %collective-permute-start.10) | collective-permute-done | bytes 65568 | tf_op jit(solution)/shard_map/ppermute | solution.py:277
  33.2 0.1 fusion.mid_ref
  33.3 2.5 %collective-permute-start.11 = (f32[2,192,128]{2,1,0:T(8,128)S(1)}, f32[2,192,128]{2,1,0:T(8,128)S(1)}, u32[]{:S(2)}, u32[]{:S(2)}) collective-permute-start(f32[2,192,128]{2,1,0:T(8,128)S(1)} %fusion.mid_ref), channel_id=1, source_target_pairs={{0,16},{1,2},{2,1},{3,4},{4,3},{5,6},{6,5},{7,23},{8,24},{9,10},{1... | collective-permute-start | bytes 589832 | tf_op jit(solution)/shard_map/ppermute | solution.py:277
  35.8 3.6 %collective-permute-done.11.far_ref = f32[2,192,128]{2,1,0:T(8,128)S(1)} collective-permute-done((f32[2,192,128]{2,1,0:T(8,128)S(1)}, f32[2,192,128]{2,1,0:T(8,128)S(1)}, u32[]{:S(2)}, u32[]{:S(2)}) %collective-permute-start.11) | collective-permute-done | bytes 196640 | tf_op jit(solution)/shard_map/ppermute | solution.py:277
  39.5 5.8 %tile_gradient.3 = (f32[2,192,128]{2,1,0:T(8,128)S(1)}, f32[2,192,128]{2,1,0:T(8,128)S(1)}, f32[2,192,128]{2,1,0:T(8,128)S(1)}) custom-call(s32[8,128]{1,0:T(8,128)S(1)} %get-tuple-element.14.plan, f32[2,192,128]{2,1,0:T(8,128)S(1)} %collective-permute-done.11.far_ref, f32[2,192,128]{2,1,0:T(8,128)S(1)} %fusion.mid_ref, ...), custom_call_target="tpu_custom_call" | custom-call | tf_op jit(solution)/shard_map/tile_gradient/pallas_call | solution.py:259
  45.4 2.1 %collective-permute-start.14 = (f32[2,64,128]{2,1,0:T(8,128)S(1)}, f32[2,64,128]{2,1,0:T(8,128)S(1)}, u32[]{:S(2)}, u32[]{:S(2)}) collective-permute-start(f32[2,64,128]{2,1,0:T(8,128)S(1)} %get-tuple-element.28), channel_id=1, source_target_pairs={{0,16},{1,2},{2,1},{3,4},{4,3},{5,6},{6,5},{7,23},{8,24},{9,10},{1... | collective-permute-start | bytes 196616 | tf_op jit(solution)/shard_map/ppermute | solution.py:277
  47.5 0.1 collective-permute-start.15
  47.6 1.9 %collective-permute-start.16 = (f32[2,64,128]{2,1,0:T(8,128)S(1)}, f32[2,64,128]{2,1,0:T(8,128)S(1)}, u32[]{:S(2)}, u32[]{:S(2)}) collective-permute-start(f32[2,64,128]{2,1,0:T(8,128)S(1)} %get-tuple-element.30), channel_id=1, source_target_pairs={{0,16},{1,2},{2,1},{3,4},{4,3},{5,6},{6,5},{7,23},{8,24},{9,18},{1... | collective-permute-start | bytes 196616 | tf_op jit(solution)/shard_map/ppermute | solution.py:277
  49.7 0.8 %collective-permute-start.18 = (f32[2,64,128]{2,1,0:T(8,128)S(1)}, f32[2,64,128]{2,1,0:T(8,128)S(1)}, u32[]{:S(2)}, u32[]{:S(2)}) collective-permute-start(f32[2,64,128]{2,1,0:T(8,128)S(1)} %get-tuple-element.32), channel_id=1, source_target_pairs={{0,1},{1,0},{2,3},{3,2},{4,5},{5,4},{6,7},{7,6},{8,16},{9,17},{10,... | collective-permute-start | bytes 196616 | tf_op jit(solution)/shard_map/ppermute | solution.py:277
  50.5 1.3 %collective-permute-done.15 = f32[2,64,128]{2,1,0:T(8,128)S(1)} collective-permute-done((f32[2,64,128]{2,1,0:T(8,128)S(1)}, f32[2,64,128]{2,1,0:T(8,128)S(1)}, u32[]{:S(2)}, u32[]{:S(2)}) %collective-permute-start.15) | collective-permute-done | bytes 65568 | tf_op jit(solution)/shard_map/ppermute | solution.py:277
  51.8 0.7 %collective-permute-done.16 = f32[2,64,128]{2,1,0:T(8,128)S(1)} collective-permute-done((f32[2,64,128]{2,1,0:T(8,128)S(1)}, f32[2,64,128]{2,1,0:T(8,128)S(1)}, u32[]{:S(2)}, u32[]{:S(2)}) %collective-permute-start.16) | collective-permute-done | bytes 65568 | tf_op jit(solution)/shard_map/ppermute | solution.py:277
  52.5 1.9 %collective-permute-done.17 = f32[2,64,128]{2,1,0:T(8,128)S(1)} collective-permute-done((f32[2,64,128]{2,1,0:T(8,128)S(1)}, f32[2,64,128]{2,1,0:T(8,128)S(1)}, u32[]{:S(2)}, u32[]{:S(2)}) %collective-permute-start.17) | collective-permute-done | bytes 65568 | tf_op jit(solution)/shard_map/ppermute | solution.py:277
  54.4 0.1 slice_bitcast_fusion.1
  54.5 0.7 %pad_maximum_fusion.2 = f32[2,2,64,64]{3,2,1,0:T(8,128)} fusion(f32[1,2,64,64]{3,2,1,0:T(8,128)S(1)} %get-tuple-element.42, f32[1,2,64,64]{3,2,1,0:T(8,128)S(1)} %get-tuple-element.41), kind=kLoop, calls=%fused_computation.5 | loop fusion | flops 16384 | bytes 131072 | tf_op jit(solution)/shard_map/stack | solution.py:394
  (37 shorter events, 0.5 us)
Async XLA Ops:
  0.0 8.3 %copy-start.1 = (f32[1,1,6,128,128]{4,3,2,1,0:T(8,128)S(1)}, f32[1,1,6,128,128]{4,3,2,1,0:T(8,128)}, u32[]{:S(2)}) copy-start(f32[1,1,6,128,128]{4,3,2,1,0:T(8,128)} %param.12) | copy-start | bytes 1179652
  0.9 7.4 %copy-start.3 = (f32[128,128]{1,0:T(8,128)S(1)}, f32[128,128]{1,0:T(8,128)}, u32[]{:S(2)}) copy-start(f32[128,128]{1,0:T(8,128)} %phase_ref.1) | copy-start | bytes 196612
  0.9 7.4 %copy-start.4 = (s32[1,1,6,2]{2,3,1,0:T(2,128)S(1)}, s32[1,1,6,2]{2,3,1,0:T(2,128)}, u32[]{:S(2)}) copy-start(s32[1,1,6,2]{2,3,1,0:T(2,128)} %param.10) | copy-start | bytes 148
  1.1 12.6 %copy-start = (bf16[8,256,256]{2,1,0:T(8,128)(2,1)S(1)}, bf16[8,256,256]{2,1,0:T(8,128)(2,1)}, u32[]{:S(2)}) copy-start(bf16[8,256,256]{2,1,0:T(8,128)(2,1)} %constant.26.clone.table_ref) | copy-start | bytes 3145732
  1.1 9.1 %collective-permute-start = (f32[2,64,128]{2,1,0:T(8,128)S(1)}, f32[2,64,128]{2,1,0:T(8,128)S(1)}, u32[]{:S(2)}, u32[]{:S(2)}) collective-permute-start(f32[2,64,128]{2,1,0:T(8,128)S(1)} %pad_maximum_fusion.3), channel_id=1, source_target_pairs={{0,8},{1,9},{2,10},{3,11},{4,12},{5,13},{6,14},{7,15},{8,0},{9,1},... | collective-permute-start | bytes 196616 | tf_op jit(solution)/shard_map/ppermute | solution.py:277
  4.1 6.0 %collective-permute-start.1 = (f32[2,64,128]{2,1,0:T(8,128)S(1)}, f32[2,64,128]{2,1,0:T(8,128)S(1)}, u32[]{:S(2)}, u32[]{:S(2)}) collective-permute-start(f32[2,64,128]{2,1,0:T(8,128)S(1)} %pad_maximum_fusion.3), channel_id=1, source_target_pairs={{0,1},{1,0},{2,3},{3,2},{4,5},{5,4},{6,7},{7,6},{8,16},{9,17},{10,... | collective-permute-start | bytes 196616 | tf_op jit(solution)/shard_map/ppermute | solution.py:277
  4.1 8.5 %collective-permute-start.2 = (f32[2,64,128]{2,1,0:T(8,128)S(1)}, f32[2,64,128]{2,1,0:T(8,128)S(1)}, u32[]{:S(2)}, u32[]{:S(2)}) collective-permute-start(f32[2,64,128]{2,1,0:T(8,128)S(1)} %pad_maximum_fusion.3), channel_id=1, source_target_pairs={{0,16},{1,10},{2,9},{3,12},{4,11},{5,14},{6,13},{7,23},{8,24},{9,2... | collective-permute-start | bytes 196616 | tf_op jit(solution)/shard_map/ppermute | solution.py:277
  5.6 7.0 %collective-permute-start.3 = (f32[2,64,128]{2,1,0:T(8,128)S(1)}, f32[2,64,128]{2,1,0:T(8,128)S(1)}, u32[]{:S(2)}, u32[]{:S(2)}) collective-permute-start(f32[2,64,128]{2,1,0:T(8,128)S(1)} %pad_maximum_fusion.3), channel_id=1, source_target_pairs={{0,16},{1,2},{2,1},{3,4},{4,3},{5,6},{6,5},{7,23},{8,24},{9,18},{1... | collective-permute-start | bytes 196616 | tf_op jit(solution)/shard_map/ppermute | solution.py:277
  6.1 6.5 %collective-permute-start.4 = (f32[2,64,128]{2,1,0:T(8,128)S(1)}, f32[2,64,128]{2,1,0:T(8,128)S(1)}, u32[]{:S(2)}, u32[]{:S(2)}) collective-permute-start(f32[2,64,128]{2,1,0:T(8,128)S(1)} %pad_maximum_fusion.3), channel_id=1, source_target_pairs={{0,16},{1,2},{2,1},{3,4},{4,3},{5,6},{6,5},{7,23},{8,24},{9,10},{1... | collective-permute-start | bytes 196616 | tf_op jit(solution)/shard_map/ppermute | solution.py:277
  8.3 0.9 %copy-start.2 = (f32[2,128,128]{2,1,0:T(8,128)S(1)}, f32[2,128,128]{2,1,0:T(8,128)}, u32[]{:S(2)}) copy-start(f32[2,128,128]{2,1,0:T(8,128)} %probe_ref.1) | copy-start | bytes 393220
  10.3 3.4 %collective-permute-start.5 = (f32[2,192,128]{2,1,0:T(8,128)S(1)}, f32[2,192,128]{2,1,0:T(8,128)S(1)}, u32[]{:S(2)}, u32[]{:S(2)}) collective-permute-start(f32[2,192,128]{2,1,0:T(8,128)S(1)} %pad_maximum_fusion.mid_ref), channel_id=1, source_target_pairs={{0,1},{1,0},{2,3},{3,2},{4,5},{5,4},{6,7},{7,6},{8,9},{9,8},{10,11... | collective-permute-start | bytes 589832 | tf_op jit(solution)/shard_map/ppermute | solution.py:277
  19.5 1.5 %collective-permute-start.6 = (f32[2,192,128]{2,1,0:T(8,128)S(1)}, f32[2,192,128]{2,1,0:T(8,128)S(1)}, u32[]{:S(2)}, u32[]{:S(2)}) collective-permute-start(f32[2,192,128]{2,1,0:T(8,128)S(1)} %get-tuple-element.18), channel_id=1, source_target_pairs={{0,1},{1,0},{2,3},{3,2},{4,5},{5,4},{6,7},{7,6},{8,9},{9,8},{10,11... | collective-permute-start | bytes 589832 | tf_op jit(solution)/shard_map/ppermute | solution.py:277
  19.9 5.7 %collective-permute-start.7 = (f32[2,192,128]{2,1,0:T(8,128)S(1)}, f32[2,192,128]{2,1,0:T(8,128)S(1)}, u32[]{:S(2)}, u32[]{:S(2)}) collective-permute-start(f32[2,192,128]{2,1,0:T(8,128)S(1)} %get-tuple-element.19), channel_id=1, source_target_pairs={{0,16},{1,2},{2,1},{3,4},{4,3},{5,6},{6,5},{7,23},{8,24},{9,10},{1... | collective-permute-start | bytes 589832 | tf_op jit(solution)/shard_map/ppermute | solution.py:277
  25.7 6.4 %collective-permute-start.8 = (f32[2,128,128]{2,1,0:T(8,128)S(1)}, f32[2,128,128]{2,1,0:T(8,128)S(1)}, u32[]{:S(2)}, u32[]{:S(2)}) collective-permute-start(f32[2,128,128]{2,1,0:T(8,128)S(1)} %get-tuple-element.33), channel_id=1, source_target_pairs={{0,8},{1,9},{2,10},{3,11},{4,12},{5,13},{6,14},{7,15},{8,0},{9,1},... | collective-permute-start | bytes 393224 | tf_op jit(solution)/shard_map/ppermute | solution.py:277
  25.8 6.4 %collective-permute-start.9 = (f32[2,128,128]{2,1,0:T(8,128)S(1)}, f32[2,128,128]{2,1,0:T(8,128)S(1)}, u32[]{:S(2)}, u32[]{:S(2)}) collective-permute-start(f32[2,128,128]{2,1,0:T(8,128)S(1)} %get-tuple-element.34), channel_id=1, source_target_pairs={{0,1},{1,0},{2,3},{3,2},{4,5},{5,4},{6,7},{7,6},{8,16},{9,17},{10,... | collective-permute-start | bytes 393224 | tf_op jit(solution)/shard_map/ppermute | solution.py:277
  25.9 7.3 %collective-permute-start.10 = (f32[2,64,128]{2,1,0:T(8,128)S(1)}, f32[2,64,128]{2,1,0:T(8,128)S(1)}, u32[]{:S(2)}, u32[]{:S(2)}) collective-permute-start(f32[2,64,128]{2,1,0:T(8,128)S(1)} %slice_select_fusion.4), channel_id=1, source_target_pairs={{0,16},{1,17},{2,18},{3,19},{4,20},{5,21},{6,22},{7,23},{8,24},{9,... | collective-permute-start | bytes 196616 | tf_op jit(solution)/shard_map/ppermute | solution.py:277
  33.3 6.2 %collective-permute-start.11 = (f32[2,192,128]{2,1,0:T(8,128)S(1)}, f32[2,192,128]{2,1,0:T(8,128)S(1)}, u32[]{:S(2)}, u32[]{:S(2)}) collective-permute-start(f32[2,192,128]{2,1,0:T(8,128)S(1)} %fusion.mid_ref), channel_id=1, source_target_pairs={{0,16},{1,2},{2,1},{3,4},{4,3},{5,6},{6,5},{7,23},{8,24},{9,10},{1... | collective-permute-start | bytes 589832 | tf_op jit(solution)/shard_map/ppermute | solution.py:277
  35.8 3.7 %collective-permute-start.12 = (f32[2,192,128]{2,1,0:T(8,128)S(1)}, f32[2,192,128]{2,1,0:T(8,128)S(1)}, u32[]{:S(2)}, u32[]{:S(2)}) collective-permute-start(f32[2,192,128]{2,1,0:T(8,128)S(1)} %fusion.mid_ref), channel_id=1, source_target_pairs={{0,1},{1,0},{2,3},{3,2},{4,5},{5,4},{6,7},{7,6},{8,9},{9,8},{10,11... | collective-permute-start | bytes 589832 | tf_op jit(solution)/shard_map/ppermute | solution.py:277
  45.3 4.2 %collective-permute-start.13 = (f32[2,192,128]{2,1,0:T(8,128)S(1)}, f32[2,192,128]{2,1,0:T(8,128)S(1)}, u32[]{:S(2)}, u32[]{:S(2)}) collective-permute-start(f32[2,192,128]{2,1,0:T(8,128)S(1)} %get-tuple-element.21), channel_id=1, source_target_pairs={{0,1},{1,0},{2,3},{3,2},{4,5},{5,4},{6,7},{7,6},{8,9},{9,8},{10,11... | collective-permute-start | bytes 589832 | tf_op jit(solution)/shard_map/ppermute | solution.py:277
  45.4 5.1 %collective-permute-start.14 = (f32[2,64,128]{2,1,0:T(8,128)S(1)}, f32[2,64,128]{2,1,0:T(8,128)S(1)}, u32[]{:S(2)}, u32[]{:S(2)}) collective-permute-start(f32[2,64,128]{2,1,0:T(8,128)S(1)} %get-tuple-element.28), channel_id=1, source_target_pairs={{0,16},{1,2},{2,1},{3,4},{4,3},{5,6},{6,5},{7,23},{8,24},{9,10},{1... | collective-permute-start | bytes 196616 | tf_op jit(solution)/shard_map/ppermute | solution.py:277
  47.5 4.3 %collective-permute-start.15 = (f32[2,64,128]{2,1,0:T(8,128)S(1)}, f32[2,64,128]{2,1,0:T(8,128)S(1)}, u32[]{:S(2)}, u32[]{:S(2)}) collective-permute-start(f32[2,64,128]{2,1,0:T(8,128)S(1)} %get-tuple-element.29), channel_id=1, source_target_pairs={{0,16},{1,10},{2,9},{3,12},{4,11},{5,14},{6,13},{7,23},{8,24},{9,2... | collective-permute-start | bytes 196616 | tf_op jit(solution)/shard_map/ppermute | solution.py:277
  47.6 4.9 %collective-permute-start.16 = (f32[2,64,128]{2,1,0:T(8,128)S(1)}, f32[2,64,128]{2,1,0:T(8,128)S(1)}, u32[]{:S(2)}, u32[]{:S(2)}) collective-permute-start(f32[2,64,128]{2,1,0:T(8,128)S(1)} %get-tuple-element.30), channel_id=1, source_target_pairs={{0,16},{1,2},{2,1},{3,4},{4,3},{5,6},{6,5},{7,23},{8,24},{9,18},{1... | collective-permute-start | bytes 196616 | tf_op jit(solution)/shard_map/ppermute | solution.py:277
  49.6 4.8 %collective-permute-start.17 = (f32[2,64,128]{2,1,0:T(8,128)S(1)}, f32[2,64,128]{2,1,0:T(8,128)S(1)}, u32[]{:S(2)}, u32[]{:S(2)}) collective-permute-start(f32[2,64,128]{2,1,0:T(8,128)S(1)} %get-tuple-element.31), channel_id=1, source_target_pairs={{0,8},{1,9},{2,10},{3,11},{4,12},{5,13},{6,14},{7,15},{8,0},{9,1},... | collective-permute-start | bytes 196616 | tf_op jit(solution)/shard_map/ppermute | solution.py:277
  49.7 4.7 %collective-permute-start.18 = (f32[2,64,128]{2,1,0:T(8,128)S(1)}, f32[2,64,128]{2,1,0:T(8,128)S(1)}, u32[]{:S(2)}, u32[]{:S(2)}) collective-permute-start(f32[2,64,128]{2,1,0:T(8,128)S(1)} %get-tuple-element.32), channel_id=1, source_target_pairs={{0,1},{1,0},{2,3},{3,2},{4,5},{5,4},{6,7},{7,6},{8,16},{9,17},{10,... | collective-permute-start | bytes 196616 | tf_op jit(solution)/shard_map/ppermute | solution.py:277
